TPU v7x, 32 devices: a whole 2x2x4 slice. The times are simulated.
32 devices in a mesh: groups: 2 (over x), crate: 16 (over z, y, core).
Axes of the slice: x: 2, y: 2, z: 4, core: 2. Of those that a mesh axis runs over, the one named last changes fastest.
Arguments:
- voltages: bfloat16 [4096, 17920], P(('groups', 'crate')), parts along dimension 0, may hold values from -6 to 6
- gains: float32 [256, 2, 2048], P('crate'), may hold values from -4 to 4
- positions: float32 [3, 2048], replicated, may hold values from -64 to 64
- directions: float32 [3, 512], replicated, may hold values from -0.5 to 0.5
- input_order: int32 [2048], replicated, may hold values from 0 to 2047, each once
- delays: int32 [1024, 256], replicated, may hold values from 0 to 31
- search_beams: int32 [16], replicated, may hold values from 0 to 511, as said below
Outputs:
- beam_power: float32 [512, 512, 32], P(('groups', 'crate')), parts along dimension 0
- dm_plane: float32 [2048, 16, 32], P(('groups', 'crate')), parts along dimension 0
There are 2 independent parts, one for each index of `groups`. A program takes and returns all parts, laid end to end along the dimension named above; an argument that names none is the same for every part. Nothing has to cross between parts.
Inputs may be any that keep to these rules, and one draw needn't show every extreme that they name: `input_order`: each antenna is carried by exactly one input row. `search_beams`: 16 distinct beams, among them beam 0 and beam 512 - 1.
All inputs are finite; a program needn't handle non-finite values.
Results may differ from a plain program's by a relative error of at most 0.0082.
Values may be sent and summed in bfloat16 or wider, within the bound.
No kernel may reach another device: no remote copies, remote signals or barrier semaphores. Data moves between devices by JAX's collectives and lax.ppermute only.
A program may use at most 64 MiB of HBM per device.

v0:
```python
import math

import jax
import jax.numpy as jnp
from jax import lax
from jax.sharding import PartitionSpec as P

INPUTS = 2048
CH = 256
BEAMS = 512
TRIALS = 1024
TAPS = 4
TIME = 32
SEARCH = 16
FFTLEN = 512


TWO_PI = 2.0 * math.pi


def pfb_window():
    window_len = TAPS * FFTLEN
    sample_index = jnp.arange(window_len, dtype=jnp.int32).astype(jnp.float32)
    offsets = (sample_index - 0.5 * window_len + 0.5) / FFTLEN
    tapering = 0.54 - 0.46 * jnp.cos(TWO_PI * sample_index / (window_len - 1))
    return (jnp.sinc(offsets) * tapering).reshape(TAPS, FFTLEN)


def fold_frames(voltages, window):
    frames = voltages.reshape(voltages.shape[0], TIME + TAPS - 1, FFTLEN)
    summed = window[0] * frames[:, 0:TIME].astype(jnp.float32)
    for tap_index in range(1, TAPS):
        summed = summed + window[tap_index] * frames[:, tap_index : tap_index + TIME].astype(
            jnp.float32
        )
    return summed.astype(jnp.bfloat16)


def dft_table():
    channel_ids = jnp.arange(CH, dtype=jnp.int32)[:, None]
    sample_ids = jnp.arange(FFTLEN, dtype=jnp.int32)[None, :]
    angles = TWO_PI * (channel_ids * sample_ids % FFTLEN).astype(jnp.float32) / FFTLEN
    factor = 1.0 / math.sqrt(FFTLEN)
    stacked = jnp.stack([jnp.cos(angles) * factor, -jnp.sin(angles) * factor], axis=1)
    return stacked.reshape(2 * CH, FFTLEN).astype(jnp.bfloat16)


def time_table():
    step_ids = jnp.arange(TIME, dtype=jnp.int32)[:, None]
    bin_ids = jnp.arange(1, TIME // 2 + 1, dtype=jnp.int32)[None, :]
    angles = TWO_PI * (step_ids * bin_ids % TIME).astype(jnp.float32) / TIME
    factor = 1.0 / math.sqrt(TIME)
    return jnp.concatenate([jnp.cos(angles) * factor, -jnp.sin(angles) * factor], axis=1)


def array_geometry(positions, directions, input_order):
    placed = jnp.take(positions, input_order, axis=1)
    geometry = directions[0][:, None] * placed[0][None, :]
    geometry = geometry + directions[1][:, None] * placed[1][None, :]
    return geometry + directions[2][:, None] * placed[2][None, :]


def steering(geometry, gain_row, frequency):
    phases = TWO_PI * frequency * geometry
    cosine = jnp.cos(phases)
    sine_part = jnp.sin(phases)
    weight_norm = 1.0 / math.sqrt(INPUTS)
    w_real = ((gain_row[0] * cosine + gain_row[1] * sine_part) * weight_norm).astype(jnp.bfloat16)
    w_imag = ((gain_row[1] * cosine - gain_row[0] * sine_part) * weight_norm).astype(jnp.bfloat16)
    upper_rows = jnp.concatenate([w_real, -w_imag], axis=1)
    lower_rows = jnp.concatenate([w_imag, w_real], axis=1)
    return jnp.concatenate([upper_rows, lower_rows], axis=0)


def dedisperse(spectrum, delay_part):
    half_bins = TIME // 2
    bin_ids = jnp.arange(1, half_bins + 1, dtype=jnp.int32)
    turn_counts = delay_part[:, :, None] * bin_ids[None, None, :] % TIME
    angles = TWO_PI * turn_counts.astype(jnp.float32) / TIME
    cosine = jnp.cos(angles)
    sine_part = jnp.sin(angles)
    spec_real = spectrum[:, :, :half_bins]
    spec_imag = spectrum[:, :, half_bins:]
    highest = lax.Precision.HIGHEST
    out_real = jnp.einsum(
        "cbk,dck->dbk", spec_real, cosine, precision=highest, preferred_element_type=jnp.float32
    ) - jnp.einsum(
        "cbk,dck->dbk", spec_imag, sine_part, precision=highest, preferred_element_type=jnp.float32
    )
    out_imag = jnp.einsum(
        "cbk,dck->dbk", spec_real, sine_part, precision=highest, preferred_element_type=jnp.float32
    ) + jnp.einsum(
        "cbk,dck->dbk", spec_imag, cosine, precision=highest, preferred_element_type=jnp.float32
    )
    factor = 1.0 / math.sqrt(CH)
    return jnp.concatenate([out_real, out_imag], axis=2) * factor


def on_device(voltages, gains, positions, directions, input_order, delays, search_beams):
    window = pfb_window()
    folded = fold_frames(voltages, window)
    spectra = jnp.einsum("ks,its->kit", dft_table(), folded, preferred_element_type=jnp.float32)
    spectra = spectra.astype(jnp.bfloat16).reshape(CH, 2, voltages.shape[0], TIME)
    geometry = array_geometry(positions, directions, input_order)
    turned = lax.all_to_all(spectra, "crate", split_axis=0, concat_axis=2, tiled=True)
    local_count = turned.shape[0]
    first_channel = lax.axis_index("crate") * local_count

    def one_channel(packed):
        offsets, channel_data, gain_row = packed
        frequency = 1.0 + (first_channel + offsets).astype(jnp.float32) / CH
        weights = steering(geometry, gain_row, frequency)
        beam_sums = jnp.dot(
            weights,
            channel_data.reshape(2 * INPUTS, channel_data.shape[-1]),
            preferred_element_type=jnp.float32,
        )
        return beam_sums[:BEAMS] * beam_sums[:BEAMS] + beam_sums[BEAMS:] * beam_sums[BEAMS:]

    beam_power = lax.map(one_channel, (jnp.arange(local_count, dtype=jnp.int32), turned, gains))
    local_channels = beam_power.shape[0]
    chosen = jnp.take(beam_power, search_beams, axis=1)
    power_spectra = jnp.dot(
        chosen.reshape(local_channels * SEARCH, TIME),
        time_table(),
        precision=lax.Precision.HIGHEST,
        preferred_element_type=jnp.float32,
    )
    power_spectra = power_spectra.reshape(local_channels, SEARCH, TIME)
    trial_rows = TRIALS // lax.axis_size("crate")
    first_trial = lax.axis_index("crate") * trial_rows
    own_delays = lax.dynamic_slice_in_dim(delays, first_trial, trial_rows, 0)
    dm_plane = dedisperse(lax.all_gather(power_spectra, "crate", axis=0, tiled=True), own_delays)
    return (beam_power, dm_plane)


def solution(mesh):
    in_specs = (P(("groups", "crate"), None), P("crate", None, None), P(), P(), P(), P(), P())
    out_specs = (P(("groups", "crate"), None, None), P(("groups", "crate"), None, None))
    return jax.shard_map(
        on_device, mesh=mesh, in_specs=in_specs, out_specs=out_specs, check_vma=False
    )
```

profile of v0, /device:TPU:0, one launch (start us, length us, event | category | flops | bytes accessed | tf_op | source)
XLA Modules:
  0.0 846.9 jit_solution(9826374699885314655)
XLA Ops:
  41.1 69.6 %all-to-all-done = bf16[256,2,128,32]{2,1,3,0:T(2,128)(2,1)} async-done(((bf16[256,2,128,32]{2,1,3,0:T(2,128)(2,1)}), bf16[256,2,128,32]{2,1,3,0:T(2,128)(2,1)}, u32[]{:S(2)}, u32[]{:S(2)}) %all-to-all-start) | async-done | bytes 4194336 | tf_op jit(solution)/shard_map/all_to_all | solution.py:105
  110.7 18.8 %copy.57 = bf16[16,2,16,128,32]{4,3,2,1,0:T(8,128)(2,1)} copy(bf16[16,2,16,128,32]{3,1,4,0,2:T(2,128)(2,1)} %bitcast.3) | data formatting | bytes 8388608 | tf_op jit(solution)/shard_map/all_to_all | solution.py:105
  129.5 635.4 %while.11 = (s32[]{:T(128)}, f32[16,512,32]{1,2,0:T(8,128)S(1)}, f32[16,2,2048]{2,1,0:T(2,128)}, s32[16]{0:T(128)S(1)}, s32[]{:T(128)}, /*index=5*/bf16[16,2,204...) while((s32[]{:T(128)}, f32[16,512,32]{1,2,0:T(8,128)S(1)}, ...), condition=%wide.region_1.2_spmd.clone, body=%wide.region_0.1_spmd.clone.sunk | while | flops 333496320 | bytes 13824269 | solution.py:120
  131.7 17.2 %fusion.114 = (bf16[512,2048]{1,0:T(8,128)(2,1)S(1)}, bf16[512,2048]{1,0:T(8,128)(2,1)S(1)}) fusion(f32[2048]{0:T(1024)S(1)} %get-tuple-element.253, f32[512]{0:T(512)S(1)} %get-tuple-element.254, f32[2048]{0:T(1024)S(1)} %get-tuple-element.251, f32[512]{0:T(512)S(1)} %get-tuple-element.252, f32[2048]{0:T(1024)S(1)} %get-tuple-element.249, ...), kind=kLoop, calls=%fused_computation.23.clone.2 | loop fusion | flops 16777216 | bytes 4241412 | tf_op jit(solution)/shard_map/while/body/eval_jaxpr/convert_element_type | solution.py:69
  171.4 17.2 %fusion.114 = (bf16[512,2048]{1,0:T(8,128)(2,1)S(1)}, bf16[512,2048]{1,0:T(8,128)(2,1)S(1)}) fusion(f32[2048]{0:T(1024)S(1)} %get-tuple-element.253, f32[512]{0:T(512)S(1)} %get-tuple-element.254, f32[2048]{0:T(1024)S(1)} %get-tuple-element.251, f32[512]{0:T(512)S(1)} %get-tuple-element.252, f32[2048]{0:T(1024)S(1)} %get-tuple-element.249, ...), kind=kLoop, calls=%fused_computation.23.clone.2 | loop fusion | flops 16777216 | bytes 4241412 | tf_op jit(solution)/shard_map/while/body/eval_jaxpr/convert_element_type | solution.py:69
  188.6 16.6 %fusion.115 = bf16[512,2048]{1,0:T(8,128)(2,1)S(1)} fusion(f32[2048]{0:T(1024)S(1)} %bitcast.51, f32[2048]{0:T(1024)S(1)} %get-tuple-element.253, f32[512]{0:T(512)S(1)} %get-tuple-element.254, f32[2048]{0:T(1024)S(1)} %get-tuple-element.251, f32[512]{0:T(512)S(1)} %get-tuple-element.252, f32[2048]{0:T(1024)S(1)} %get-tuple-element.249, ...), kind=kLoop, calls=%fused_computation.33.clone.1 | loop fusion | flops 14680064 | bytes 2144260 | tf_op jit(solution)/shard_map/while/body/eval_jaxpr/neg | solution.py:70
  211.1 17.2 %fusion.114 = (bf16[512,2048]{1,0:T(8,128)(2,1)S(1)}, bf16[512,2048]{1,0:T(8,128)(2,1)S(1)}) fusion(f32[2048]{0:T(1024)S(1)} %get-tuple-element.253, f32[512]{0:T(512)S(1)} %get-tuple-element.254, f32[2048]{0:T(1024)S(1)} %get-tuple-element.251, f32[512]{0:T(512)S(1)} %get-tuple-element.252, f32[2048]{0:T(1024)S(1)} %get-tuple-element.249, ...), kind=kLoop, calls=%fused_computation.23.clone.2 | loop fusion | flops 16777216 | bytes 4241412 | tf_op jit(solution)/shard_map/while/body/eval_jaxpr/convert_element_type | solution.py:69
  228.3 16.6 %fusion.115 = bf16[512,2048]{1,0:T(8,128)(2,1)S(1)} fusion(f32[2048]{0:T(1024)S(1)} %bitcast.51, f32[2048]{0:T(1024)S(1)} %get-tuple-element.253, f32[512]{0:T(512)S(1)} %get-tuple-element.254, f32[2048]{0:T(1024)S(1)} %get-tuple-element.251, f32[512]{0:T(512)S(1)} %get-tuple-element.252, f32[2048]{0:T(1024)S(1)} %get-tuple-element.249, ...), kind=kLoop, calls=%fused_computation.33.clone.1 | loop fusion | flops 14680064 | bytes 2144260 | tf_op jit(solution)/shard_map/while/body/eval_jaxpr/neg | solution.py:70
  250.8 17.2 %fusion.114 = (bf16[512,2048]{1,0:T(8,128)(2,1)S(1)}, bf16[512,2048]{1,0:T(8,128)(2,1)S(1)}) fusion(f32[2048]{0:T(1024)S(1)} %get-tuple-element.253, f32[512]{0:T(512)S(1)} %get-tuple-element.254, f32[2048]{0:T(1024)S(1)} %get-tuple-element.251, f32[512]{0:T(512)S(1)} %get-tuple-element.252, f32[2048]{0:T(1024)S(1)} %get-tuple-element.249, ...), kind=kLoop, calls=%fused_computation.23.clone.2 | loop fusion | flops 16777216 | bytes 4241412 | tf_op jit(solution)/shard_map/while/body/eval_jaxpr/convert_element_type | solution.py:69
  268.0 16.6 %fusion.115 = bf16[512,2048]{1,0:T(8,128)(2,1)S(1)} fusion(f32[2048]{0:T(1024)S(1)} %bitcast.51, f32[2048]{0:T(1024)S(1)} %get-tuple-element.253, f32[512]{0:T(512)S(1)} %get-tuple-element.254, f32[2048]{0:T(1024)S(1)} %get-tuple-element.251, f32[512]{0:T(512)S(1)} %get-tuple-element.252, f32[2048]{0:T(1024)S(1)} %get-tuple-element.249, ...), kind=kLoop, calls=%fused_computation.33.clone.1 | loop fusion | flops 14680064 | bytes 2144260 | tf_op jit(solution)/shard_map/while/body/eval_jaxpr/neg | solution.py:70
  290.5 17.2 %fusion.114 = (bf16[512,2048]{1,0:T(8,128)(2,1)S(1)}, bf16[512,2048]{1,0:T(8,128)(2,1)S(1)}) fusion(f32[2048]{0:T(1024)S(1)} %get-tuple-element.253, f32[512]{0:T(512)S(1)} %get-tuple-element.254, f32[2048]{0:T(1024)S(1)} %get-tuple-element.251, f32[512]{0:T(512)S(1)} %get-tuple-element.252, f32[2048]{0:T(1024)S(1)} %get-tuple-element.249, ...), kind=kLoop, calls=%fused_computation.23.clone.2 | loop fusion | flops 16777216 | bytes 4241412 | tf_op jit(solution)/shard_map/while/body/eval_jaxpr/convert_element_type | solution.py:69
  307.7 16.6 %fusion.115 = bf16[512,2048]{1,0:T(8,128)(2,1)S(1)} fusion(f32[2048]{0:T(1024)S(1)} %bitcast.51, f32[2048]{0:T(1024)S(1)} %get-tuple-element.253, f32[512]{0:T(512)S(1)} %get-tuple-element.254, f32[2048]{0:T(1024)S(1)} %get-tuple-element.251, f32[512]{0:T(512)S(1)} %get-tuple-element.252, f32[2048]{0:T(1024)S(1)} %get-tuple-element.249, ...), kind=kLoop, calls=%fused_computation.33.clone.1 | loop fusion | flops 14680064 | bytes 2144260 | tf_op jit(solution)/shard_map/while/body/eval_jaxpr/neg | solution.py:70
  330.2 17.2 %fusion.114 = (bf16[512,2048]{1,0:T(8,128)(2,1)S(1)}, bf16[512,2048]{1,0:T(8,128)(2,1)S(1)}) fusion(f32[2048]{0:T(1024)S(1)} %get-tuple-element.253, f32[512]{0:T(512)S(1)} %get-tuple-element.254, f32[2048]{0:T(1024)S(1)} %get-tuple-element.251, f32[512]{0:T(512)S(1)} %get-tuple-element.252, f32[2048]{0:T(1024)S(1)} %get-tuple-element.249, ...), kind=kLoop, calls=%fused_computation.23.clone.2 | loop fusion | flops 16777216 | bytes 4241412 | tf_op jit(solution)/shard_map/while/body/eval_jaxpr/convert_element_type | solution.py:69
  369.9 17.2 %fusion.114 = (bf16[512,2048]{1,0:T(8,128)(2,1)S(1)}, bf16[512,2048]{1,0:T(8,128)(2,1)S(1)}) fusion(f32[2048]{0:T(1024)S(1)} %get-tuple-element.253, f32[512]{0:T(512)S(1)} %get-tuple-element.254, f32[2048]{0:T(1024)S(1)} %get-tuple-element.251, f32[512]{0:T(512)S(1)} %get-tuple-element.252, f32[2048]{0:T(1024)S(1)} %get-tuple-element.249, ...), kind=kLoop, calls=%fused_computation.23.clone.2 | loop fusion | flops 16777216 | bytes 4241412 | tf_op jit(solution)/shard_map/while/body/eval_jaxpr/convert_element_type | solution.py:69
  387.1 16.6 %fusion.115 = bf16[512,2048]{1,0:T(8,128)(2,1)S(1)} fusion(f32[2048]{0:T(1024)S(1)} %bitcast.51, f32[2048]{0:T(1024)S(1)} %get-tuple-element.253, f32[512]{0:T(512)S(1)} %get-tuple-element.254, f32[2048]{0:T(1024)S(1)} %get-tuple-element.251, f32[512]{0:T(512)S(1)} %get-tuple-element.252, f32[2048]{0:T(1024)S(1)} %get-tuple-element.249, ...), kind=kLoop, calls=%fused_computation.33.clone.1 | loop fusion | flops 14680064 | bytes 2144260 | tf_op jit(solution)/shard_map/while/body/eval_jaxpr/neg | solution.py:70
  409.6 17.2 %fusion.114 = (bf16[512,2048]{1,0:T(8,128)(2,1)S(1)}, bf16[512,2048]{1,0:T(8,128)(2,1)S(1)}) fusion(f32[2048]{0:T(1024)S(1)} %get-tuple-element.253, f32[512]{0:T(512)S(1)} %get-tuple-element.254, f32[2048]{0:T(1024)S(1)} %get-tuple-element.251, f32[512]{0:T(512)S(1)} %get-tuple-element.252, f32[2048]{0:T(1024)S(1)} %get-tuple-element.249, ...), kind=kLoop, calls=%fused_computation.23.clone.2 | loop fusion | flops 16777216 | bytes 4241412 | tf_op jit(solution)/shard_map/while/body/eval_jaxpr/convert_element_type | solution.py:69
  426.8 16.6 %fusion.115 = bf16[512,2048]{1,0:T(8,128)(2,1)S(1)} fusion(f32[2048]{0:T(1024)S(1)} %bitcast.51, f32[2048]{0:T(1024)S(1)} %get-tuple-element.253, f32[512]{0:T(512)S(1)} %get-tuple-element.254, f32[2048]{0:T(1024)S(1)} %get-tuple-element.251, f32[512]{0:T(512)S(1)} %get-tuple-element.252, f32[2048]{0:T(1024)S(1)} %get-tuple-element.249, ...), kind=kLoop, calls=%fused_computation.33.clone.1 | loop fusion | flops 14680064 | bytes 2144260 | tf_op jit(solution)/shard_map/while/body/eval_jaxpr/neg | solution.py:70
  449.3 17.2 %fusion.114 = (bf16[512,2048]{1,0:T(8,128)(2,1)S(1)}, bf16[512,2048]{1,0:T(8,128)(2,1)S(1)}) fusion(f32[2048]{0:T(1024)S(1)} %get-tuple-element.253, f32[512]{0:T(512)S(1)} %get-tuple-element.254, f32[2048]{0:T(1024)S(1)} %get-tuple-element.251, f32[512]{0:T(512)S(1)} %get-tuple-element.252, f32[2048]{0:T(1024)S(1)} %get-tuple-element.249, ...), kind=kLoop, calls=%fused_computation.23.clone.2 | loop fusion | flops 16777216 | bytes 4241412 | tf_op jit(solution)/shard_map/while/body/eval_jaxpr/convert_element_type | solution.py:69
  466.5 16.6 %fusion.115 = bf16[512,2048]{1,0:T(8,128)(2,1)S(1)} fusion(f32[2048]{0:T(1024)S(1)} %bitcast.51, f32[2048]{0:T(1024)S(1)} %get-tuple-element.253, f32[512]{0:T(512)S(1)} %get-tuple-element.254, f32[2048]{0:T(1024)S(1)} %get-tuple-element.251, f32[512]{0:T(512)S(1)} %get-tuple-element.252, f32[2048]{0:T(1024)S(1)} %get-tuple-element.249, ...), kind=kLoop, calls=%fused_computation.33.clone.1 | loop fusion | flops 14680064 | bytes 2144260 | tf_op jit(solution)/shard_map/while/body/eval_jaxpr/neg | solution.py:70
  489.0 17.2 %fusion.114 = (bf16[512,2048]{1,0:T(8,128)(2,1)S(1)}, bf16[512,2048]{1,0:T(8,128)(2,1)S(1)}) fusion(f32[2048]{0:T(1024)S(1)} %get-tuple-element.253, f32[512]{0:T(512)S(1)} %get-tuple-element.254, f32[2048]{0:T(1024)S(1)} %get-tuple-element.251, f32[512]{0:T(512)S(1)} %get-tuple-element.252, f32[2048]{0:T(1024)S(1)} %get-tuple-element.249, ...), kind=kLoop, calls=%fused_computation.23.clone.2 | loop fusion | flops 16777216 | bytes 4241412 | tf_op jit(solution)/shard_map/while/body/eval_jaxpr/convert_element_type | solution.py:69
  506.2 16.6 %fusion.115 = bf16[512,2048]{1,0:T(8,128)(2,1)S(1)} fusion(f32[2048]{0:T(1024)S(1)} %bitcast.51, f32[2048]{0:T(1024)S(1)} %get-tuple-element.253, f32[512]{0:T(512)S(1)} %get-tuple-element.254, f32[2048]{0:T(1024)S(1)} %get-tuple-element.251, f32[512]{0:T(512)S(1)} %get-tuple-element.252, f32[2048]{0:T(1024)S(1)} %get-tuple-element.249, ...), kind=kLoop, calls=%fused_computation.33.clone.1 | loop fusion | flops 14680064 | bytes 2144260 | tf_op jit(solution)/shard_map/while/body/eval_jaxpr/neg | solution.py:70
  528.7 17.2 %fusion.114 = (bf16[512,2048]{1,0:T(8,128)(2,1)S(1)}, bf16[512,2048]{1,0:T(8,128)(2,1)S(1)}) fusion(f32[2048]{0:T(1024)S(1)} %get-tuple-element.253, f32[512]{0:T(512)S(1)} %get-tuple-element.254, f32[2048]{0:T(1024)S(1)} %get-tuple-element.251, f32[512]{0:T(512)S(1)} %get-tuple-element.252, f32[2048]{0:T(1024)S(1)} %get-tuple-element.249, ...), kind=kLoop, calls=%fused_computation.23.clone.2 | loop fusion | flops 16777216 | bytes 4241412 | tf_op jit(solution)/shard_map/while/body/eval_jaxpr/convert_element_type | solution.py:69
  545.9 16.6 %fusion.115 = bf16[512,2048]{1,0:T(8,128)(2,1)S(1)} fusion(f32[2048]{0:T(1024)S(1)} %bitcast.51, f32[2048]{0:T(1024)S(1)} %get-tuple-element.253, f32[512]{0:T(512)S(1)} %get-tuple-element.254, f32[2048]{0:T(1024)S(1)} %get-tuple-element.251, f32[512]{0:T(512)S(1)} %get-tuple-element.252, f32[2048]{0:T(1024)S(1)} %get-tuple-element.249, ...), kind=kLoop, calls=%fused_computation.33.clone.1 | loop fusion | flops 14680064 | bytes 2144260 | tf_op jit(solution)/shard_map/while/body/eval_jaxpr/neg | solution.py:70
  568.5 17.2 %fusion.114 = (bf16[512,2048]{1,0:T(8,128)(2,1)S(1)}, bf16[512,2048]{1,0:T(8,128)(2,1)S(1)}) fusion(f32[2048]{0:T(1024)S(1)} %get-tuple-element.253, f32[512]{0:T(512)S(1)} %get-tuple-element.254, f32[2048]{0:T(1024)S(1)} %get-tuple-element.251, f32[512]{0:T(512)S(1)} %get-tuple-element.252, f32[2048]{0:T(1024)S(1)} %get-tuple-element.249, ...), kind=kLoop, calls=%fused_computation.23.clone.2 | loop fusion | flops 16777216 | bytes 4241412 | tf_op jit(solution)/shard_map/while/body/eval_jaxpr/convert_element_type | solution.py:69
  608.2 17.2 %fusion.114 = (bf16[512,2048]{1,0:T(8,128)(2,1)S(1)}, bf16[512,2048]{1,0:T(8,128)(2,1)S(1)}) fusion(f32[2048]{0:T(1024)S(1)} %get-tuple-element.253, f32[512]{0:T(512)S(1)} %get-tuple-element.254, f32[2048]{0:T(1024)S(1)} %get-tuple-element.251, f32[512]{0:T(512)S(1)} %get-tuple-element.252, f32[2048]{0:T(1024)S(1)} %get-tuple-element.249, ...), kind=kLoop, calls=%fused_computation.23.clone.2 | loop fusion | flops 16777216 | bytes 4241412 | tf_op jit(solution)/shard_map/while/body/eval_jaxpr/convert_element_type | solution.py:69
  625.3 16.6 %fusion.115 = bf16[512,2048]{1,0:T(8,128)(2,1)S(1)} fusion(f32[2048]{0:T(1024)S(1)} %bitcast.51, f32[2048]{0:T(1024)S(1)} %get-tuple-element.253, f32[512]{0:T(512)S(1)} %get-tuple-element.254, f32[2048]{0:T(1024)S(1)} %get-tuple-element.251, f32[512]{0:T(512)S(1)} %get-tuple-element.252, f32[2048]{0:T(1024)S(1)} %get-tuple-element.249, ...), kind=kLoop, calls=%fused_computation.33.clone.1 | loop fusion | flops 14680064 | bytes 2144260 | tf_op jit(solution)/shard_map/while/body/eval_jaxpr/neg | solution.py:70
  647.9 17.2 %fusion.114 = (bf16[512,2048]{1,0:T(8,128)(2,1)S(1)}, bf16[512,2048]{1,0:T(8,128)(2,1)S(1)}) fusion(f32[2048]{0:T(1024)S(1)} %get-tuple-element.253, f32[512]{0:T(512)S(1)} %get-tuple-element.254, f32[2048]{0:T(1024)S(1)} %get-tuple-element.251, f32[512]{0:T(512)S(1)} %get-tuple-element.252, f32[2048]{0:T(1024)S(1)} %get-tuple-element.249, ...), kind=kLoop, calls=%fused_computation.23.clone.2 | loop fusion | flops 16777216 | bytes 4241412 | tf_op jit(solution)/shard_map/while/body/eval_jaxpr/convert_element_type | solution.py:69
  665.0 16.6 %fusion.115 = bf16[512,2048]{1,0:T(8,128)(2,1)S(1)} fusion(f32[2048]{0:T(1024)S(1)} %bitcast.51, f32[2048]{0:T(1024)S(1)} %get-tuple-element.253, f32[512]{0:T(512)S(1)} %get-tuple-element.254, f32[2048]{0:T(1024)S(1)} %get-tuple-element.251, f32[512]{0:T(512)S(1)} %get-tuple-element.252, f32[2048]{0:T(1024)S(1)} %get-tuple-element.249, ...), kind=kLoop, calls=%fused_computation.33.clone.1 | loop fusion | flops 14680064 | bytes 2144260 | tf_op jit(solution)/shard_map/while/body/eval_jaxpr/neg | solution.py:70
  687.6 17.2 %fusion.114 = (bf16[512,2048]{1,0:T(8,128)(2,1)S(1)}, bf16[512,2048]{1,0:T(8,128)(2,1)S(1)}) fusion(f32[2048]{0:T(1024)S(1)} %get-tuple-element.253, f32[512]{0:T(512)S(1)} %get-tuple-element.254, f32[2048]{0:T(1024)S(1)} %get-tuple-element.251, f32[512]{0:T(512)S(1)} %get-tuple-element.252, f32[2048]{0:T(1024)S(1)} %get-tuple-element.249, ...), kind=kLoop, calls=%fused_computation.23.clone.2 | loop fusion | flops 16777216 | bytes 4241412 | tf_op jit(solution)/shard_map/while/body/eval_jaxpr/convert_element_type | solution.py:69
  704.7 16.6 %fusion.115 = bf16[512,2048]{1,0:T(8,128)(2,1)S(1)} fusion(f32[2048]{0:T(1024)S(1)} %bitcast.51, f32[2048]{0:T(1024)S(1)} %get-tuple-element.253, f32[512]{0:T(512)S(1)} %get-tuple-element.254, f32[2048]{0:T(1024)S(1)} %get-tuple-element.251, f32[512]{0:T(512)S(1)} %get-tuple-element.252, f32[2048]{0:T(1024)S(1)} %get-tuple-element.249, ...), kind=kLoop, calls=%fused_computation.33.clone.1 | loop fusion | flops 14680064 | bytes 2144260 | tf_op jit(solution)/shard_map/while/body/eval_jaxpr/neg | solution.py:70
  727.3 17.2 %fusion.114 = (bf16[512,2048]{1,0:T(8,128)(2,1)S(1)}, bf16[512,2048]{1,0:T(8,128)(2,1)S(1)}) fusion(f32[2048]{0:T(1024)S(1)} %get-tuple-element.253, f32[512]{0:T(512)S(1)} %get-tuple-element.254, f32[2048]{0:T(1024)S(1)} %get-tuple-element.251, f32[512]{0:T(512)S(1)} %get-tuple-element.252, f32[2048]{0:T(1024)S(1)} %get-tuple-element.249, ...), kind=kLoop, calls=%fused_computation.23.clone.2 | loop fusion | flops 16777216 | bytes 4241412 | tf_op jit(solution)/shard_map/while/body/eval_jaxpr/convert_element_type | solution.py:69
  771.7 45.6 %all_gather.3 = f32[256,16,32]{2,1,0:T(8,128)S(1)} all-gather(f32[16,16,32]{2,1,0:T(8,128)S(1)} %fusion.56), channel_id=1, replica_groups=mesh['groups'=2,'crate'=16] {'crate'}, dimensions={0}, use_global_device_ids=true | all-gather | bytes 557056 | tf_op jit(solution)/shard_map/all_gather | solution.py:133
  (138 shorter events, 226.5 us)
Async XLA Ops:
  0.6 38.5 %copy-start = (s32[1024,256]{1,0:T(8,128)S(1)}, s32[1024,256]{1,0:T(8,128)}, u32[]{:S(2)}) copy-start(s32[1024,256]{1,0:T(8,128)} %param.14) | copy-start | bytes 3145732
  25.5 7.6 copy-start.3
  25.5 8.0 copy-start.4
  25.5 13.5 %copy-start.6 = (s32[16]{0:T(128)S(1)}, s32[16]{0:T(128)}, u32[]{:S(2)}) copy-start(s32[16]{0:T(128)} %param.15) | copy-start | bytes 196
  25.5 85.1 %all-to-all-start = ((bf16[256,2,128,32]{2,1,3,0:T(2,128)(2,1)}), bf16[256,2,128,32]{2,1,3,0:T(2,128)(2,1)}, u32[]{:S(2)}, u32[]{:S(2)}) async-start(bf16[256,2,128,32]{2,1,3,0:T(2,128)(2,1)} %copy.56), calls=%async_computation | async-start | bytes 8388608 | tf_op jit(solution)/shard_map/all_to_all | solution.py:105
  33.1 7.8 copy-start.5
  110.7 18.8 %copy-start.1 = (f32[16,512,32]{1,2,0:T(8,128)S(1)}, f32[16,512,32]{1,2,0:T(8,128)}, u32[]{:S(2)}) copy-start(f32[16,512,32]{1,2,0:T(8,128)} %custom-call.4) | copy-start | bytes 3145732
  764.9 6.8 copy-start.2
  834.5 6.3 copy-start.7
where the time goes:
time: 857 us; the launch traced here: 847 us
  other arithmetic  544 us (63%)
  local copies, waits for them, and re-layouts  96.2 us (11%)
  matrix products  71.6 us (8%)
  waiting for transfers between devices  69.6 us (8%)
  blocking collectives  45.6 us (5%)
  loops' own time  11.3 us (1%)
    convert_element_type x16, other arithmetic, steering(): ((gain_row[1] * cosine - gain_row[0] * sine_part) * weight_norm).astype(j...  275 us
    neg x16, other arithmetic, steering(): upper_rows = jnp.concatenate([w_real, -w_imag], axis=1)  266 us
    all_to_all x1, waiting for transfers between devices, on_device(): lax.all_to_all(spectra, 'crate', split_axis=0, concat_axis=2, tiled=True)  69.6 us
    all_gather x1, blocking collectives, on_device(): lax.all_gather(power_spectra, 'crate', axis=0, tiled=True)  45.6 us
    dot_general x16, matrix products, one_channel(): jnp.dot(weights, channel_data.reshape(2 * INPUTS, channel_data.shape[-1])...  40.2 us
    dynamic_slice x32, local copies, waits for them, and re-layouts, on_device(): lax.map(one_channel, (jnp.arange(local_count, dtype=jnp.int32), turned, g...  30.2 us
    all_to_all x1, local copies, waits for them, and re-layouts, on_device(): lax.all_to_all(spectra, 'crate', split_axis=0, concat_axis=2, tiled=True)  18.8 us
  transfers between devices with their start and end apart: 1, of which 1 were waited for; matrix products, arithmetic and copies ran while one was open for 1% of the time, Pallas kernels for 0%

commit v1 on v0

v1 whole, which is shorter than its diff:
```python
import functools
import math

import jax
import jax.numpy as jnp
import numpy as np
from jax import lax
from jax.experimental import pallas as pl
from jax.experimental.pallas import tpu as pltpu
from jax.sharding import PartitionSpec as P

CH = 256
TAPS = 4
TIME = 32
FFTLEN = 512
HALF_BINS = TIME // 2
TWO_PI = 2.0 * math.pi
F32 = jnp.float32
BF16 = jnp.bfloat16
NT = (((1,), (1,)), ((), ()))

SIN_POLY = (
    6.283185302511503,
    -41.34170040531769,
    81.60513138580204,
    -76.7030153539128,
    42.02592698618416,
    -14.899846668691637,
    3.238137510515757,
)
COS_POLY = (
    0.9999999890590228,
    -19.739204499454026,
    64.93911745990036,
    -85.45013953095037,
    60.16763093136588,
    -25.96759924965491,
    6.528658162567069,
)


def pfb_window():
    n = np.arange(TAPS * FFTLEN, dtype=np.float64)
    offsets = (n - 0.5 * TAPS * FFTLEN + 0.5) / FFTLEN
    tapering = 0.54 - 0.46 * np.cos(TWO_PI * n / (TAPS * FFTLEN - 1))
    return (np.sinc(offsets) * tapering).reshape(TAPS, FFTLEN).astype(np.float32)


def dft_table():
    turns = np.arange(CH)[:, None] * np.arange(FFTLEN)[None, :] % FFTLEN
    angles = TWO_PI * turns / FFTLEN
    stacked = np.stack([np.cos(angles), -np.sin(angles)], axis=1) / math.sqrt(FFTLEN)
    return stacked.reshape(2 * CH, FFTLEN).astype(np.float32)


def time_table(search):
    turns = np.arange(TIME)[:, None] * np.arange(1, HALF_BINS + 1)[None, :] % TIME
    angles = TWO_PI * turns / TIME
    table = np.concatenate([np.cos(angles), -np.sin(angles)], axis=1) / math.sqrt(TIME)
    full = np.einsum("tk,qp->tqpk", table, np.eye(search))
    return full.reshape(TIME * search, search * TIME).astype(np.float32)


def polynomial(z, coefficients):
    total = jnp.full_like(z, coefficients[-1])
    for value in coefficients[-2::-1]:
        total = total * z + value
    return total


def cos_sin_turns(turns):
    r = turns - jnp.round(turns)
    z = r * r
    return polynomial(z, COS_POLY), polynomial(z, SIN_POLY) * r


def split_bf16(x):
    high = x.astype(BF16)
    return high, (x - high.astype(F32)).astype(BF16)


def transform_rows(table, folded_ref, spread_ref, out_ref):
    inputs = out_ref.shape[-1]
    rows = table.shape[0]
    group = 2 if inputs % 128 == 0 else 1

    def step(index, carry):
        start = pl.multiple_of(index * (group * inputs), group * inputs)
        frames = folded_ref[pl.ds(start, group * inputs), :]
        out = lax.dot_general(table, frames, NT, preferred_element_type=F32)
        for part in range(group):
            piece = out[:, part * inputs : (part + 1) * inputs]
            spread_ref[pl.ds(index * group + part, rows, stride=TIME), :] = piece
        return carry

    lax.fori_loop(0, TIME // group, step, 0, unroll=2)
    dests, chans = out_ref.shape[:2]
    per_chan = 2 * TIME

    def pack(dest, carry):
        for chan in range(chans):
            start = pl.multiple_of((dest * chans + chan) * per_chan, per_chan)
            out_ref[dest, chan] = spread_ref[pl.ds(start, per_chan), :].astype(BF16)
        return carry

    lax.fori_loop(0, dests, pack, 0)


def fold_kernel(half_ref, volt_ref, window_ref, table_ref, out_ref, folded_ref, spread_ref):
    step = pl.program_id(0)
    rows = volt_ref.shape[0]
    inputs = out_ref.shape[-1]
    lanes = 256
    for lane in range(0, FFTLEN, lanes):
        taps = [window_ref[j : j + 1, lane : lane + lanes] for j in range(TAPS)]
        for row in range(0, rows, 16):
            frames = []
            for t in range(TIME + TAPS - 1):
                start = t * FFTLEN + lane
                frames.append(volt_ref[row : row + 16, start : start + lanes].astype(F32))
                if t >= TAPS - 1:
                    first = t - TAPS + 1
                    total = taps[0] * frames[first]
                    for j in range(1, TAPS):
                        total = total + taps[j] * frames[first + j]
                    place = pl.multiple_of(first * inputs + step * rows + row, 16)
                    folded_ref[pl.ds(place, 16), lane : lane + lanes] = total.astype(BF16)

    @pl.when(step == pl.num_programs(0) - 1)
    def _():
        transform_rows(table_ref[...], folded_ref, spread_ref, out_ref)


def near_kernel(half_ref, folded_ref, table_ref, out_ref, spread_ref):
    transform_rows(table_ref[...], folded_ref, spread_ref, out_ref)


def beam_kernel(
    first_ref, x_ref, gain_ref, place_ref, dir_ref, out_ref, weight_ref, sum_ref
):
    step = pl.program_id(0)
    tiles = pl.num_programs(0) - 1
    chans, _, beams = out_ref.shape
    depth = place_ref.shape[0]
    wide = 256
    chunk = depth // chans
    now = lax.rem(step, 2)
    before = 1 - now

    def generate(part):
        for sub in range(0, chunk, 16):
            row = pl.multiple_of(part * chunk + sub, 16)
            place = place_ref[pl.ds(row, 16), :]
            for lane in range(0, beams, wide):
                lanes = slice(lane, lane + wide)
                direction = dir_ref[:, lanes]
                geometry = place[:, 0:1] * direction[0:1, :]
                geometry = geometry + place[:, 1:2] * direction[1:2, :]
                geometry = geometry + place[:, 2:3] * direction[2:3, :]
                first = 1.0 + first_ref[0].astype(F32) * (1.0 / CH)
                c, s = cos_sin_turns(geometry * first)
                dc, ds = cos_sin_turns(geometry * (1.0 / CH))
                for chan in range(chans):
                    weight_ref[now, chan, pl.ds(row, 16), lanes] = c.astype(BF16)
                    weight_ref[now, chan, pl.ds(depth + row, 16), lanes] = s.astype(BF16)
                    if chan + 1 < chans:
                        c, s = c * dc - s * ds, c * ds + s * dc

    def accumulate(chan):
        blocks = x_ref.shape[0]
        data = jnp.concatenate([x_ref[k, chan] for k in range(blocks)], axis=1).astype(F32)
        real, imag = data[:TIME], data[TIME:]
        gain = gain_ref[chan]
        x0 = (gain[0:1] * real - gain[1:2] * imag).astype(BF16)
        x1 = (gain[0:1] * imag + gain[1:2] * real).astype(BF16)
        top = jnp.concatenate([x0, x1], axis=1)
        bottom = jnp.concatenate([x1, -x0], axis=1)
        both = jnp.concatenate([top, bottom], axis=0)
        return jnp.dot(both, weight_ref[before, chan], preferred_element_type=F32)

    @pl.when(step == 0)
    def _():
        sum_ref[...] = jnp.zeros_like(sum_ref)
        lax.fori_loop(0, chans, lambda m, v: (generate(m), v)[1], 0)

    @pl.when((step > 0) & (step < tiles))
    def _():
        def both(m, v):
            sum_ref[m] += accumulate(m)
            generate(m)
            return v

        lax.fori_loop(0, chans, both, 0)

    @pl.when(step == tiles)
    def _():
        def last(m, v):
            out_ref[m] = (sum_ref[m] + accumulate(m)).astype(out_ref.dtype)
            return v

        lax.fori_loop(0, chans, last, 0)


def power_kernel(
    own_ref, far_ref, pick_ref, high_ref, low_ref, power_ref, spec_ref, chosen_ref
):
    step = pl.program_id(0)
    block, _, beams = own_ref.shape
    search = chosen_ref.shape[1] // TIME
    per = 128 // search
    total = own_ref[...] + far_ref[...].astype(F32)
    real, imag = total[:, :TIME], total[:, TIME:]
    power = (real * real + imag * imag) * (1.0 / 2048)
    power_ref[...] = power
    rows = power.reshape(block * TIME, beams)
    hit = lax.broadcasted_iota(jnp.int32, (beams, 128), 0) == pick_ref[...]
    hot = jnp.where(hit, 1.0, 0.0).astype(BF16)
    high, low = split_bf16(rows)
    picked = jnp.dot(high, hot, preferred_element_type=F32)
    picked = picked + jnp.dot(low, hot, preferred_element_type=F32)
    row_id = lax.broadcasted_iota(jnp.int32, (per, 128), 0)
    lane_id = lax.broadcasted_iota(jnp.int32, (per, 128), 1) // search
    for chan in range(block):
        pieces = []
        for j in range(TIME // per):
            start = chan * TIME + j * per
            piece = jnp.where(row_id == lane_id, picked[start : start + per], 0.0)
            pieces.append(jnp.sum(piece, axis=0, keepdims=True))
        chosen_ref[pl.ds(step * block + chan, 1), :] = jnp.concatenate(pieces, axis=1)

    @pl.when(step == pl.num_programs(0) - 1)
    def _():
        g_high, g_low = split_bf16(chosen_ref[...])
        spectrum = jnp.dot(g_high, high_ref[...], preferred_element_type=F32)
        spectrum = spectrum + jnp.dot(g_low, high_ref[...], preferred_element_type=F32)
        spectrum = spectrum + jnp.dot(g_high, low_ref[...], preferred_element_type=F32)
        spectrum = spectrum.astype(BF16)
        for dest in range(spec_ref.shape[0]):
            spec_ref[dest] = spectrum


def turn_kernel(delay_ref, high_ref, low_ref):
    trials, chans = delay_ref.shape
    dc, ds = cos_sin_turns(delay_ref[...].astype(F32) * (1.0 / TIME))
    c, s = dc, ds
    for k in range(HALF_BINS):
        rows = slice(k * trials, (k + 1) * trials)
        for value, start in ((c, 0), (s, chans)):
            high, low = split_bf16(value)
            high_ref[rows, start : start + chans] = high
            low_ref[rows, start : start + chans] = low
        c, s = c * dc - s * ds, c * ds + s * dc


def plane_kernel(spec_ref, high_ref, low_ref, out_ref):
    chans, width = spec_ref.shape
    search, _, trials = out_ref.shape
    spec = spec_ref[...].astype(F32)
    lane = lax.broadcasted_iota(jnp.int32, (chans, width), 1)
    is_real = lane % TIME < HALF_BINS
    ahead = pltpu.roll(spec, width - HALF_BINS, 1)
    behind = pltpu.roll(spec, HALF_BINS, 1)
    turned = jnp.where(is_real, -ahead, behind)
    both = jnp.concatenate([spec.astype(BF16), turned.astype(BF16)], axis=0)
    bin_id = lax.broadcasted_iota(jnp.int32, (trials, width), 1) % HALF_BINS
    plane = jnp.zeros((trials, width), F32)
    for k in range(HALF_BINS):
        rows = slice(k * trials, (k + 1) * trials)
        part = jnp.dot(high_ref[rows], both, preferred_element_type=F32)
        part = part + jnp.dot(low_ref[rows], both, preferred_element_type=F32)
        plane = jnp.where(bin_id == k, part, plane)
    out_ref[...] = (plane.T * (1.0 / math.sqrt(CH))).reshape(out_ref.shape)


PARAMS = pltpu.CompilerParams(vmem_limit_bytes=60 << 20)


def channelize(voltages, half_id, halves, chans):
    inputs, samples = voltages.shape
    rows = 2 * CH // halves
    dests = rows // 2 // chans
    window = jnp.asarray(pfb_window())
    table = jnp.asarray(dft_table()).astype(BF16)
    block = min(32, inputs)
    out = jax.ShapeDtypeStruct((dests, chans, 2 * TIME, inputs), BF16)
    folded = jax.ShapeDtypeStruct((TIME * inputs, FFTLEN), BF16)
    spread = pltpu.VMEM((rows * TIME, inputs), F32)
    whole4 = pl.BlockSpec(out.shape, lambda i, h: (0, 0, 0, 0))
    whole2 = pl.BlockSpec(folded.shape, lambda i, h: (0, 0))
    far, folded = pl.pallas_call(
        fold_kernel,
        out_shape=(out, folded),
        grid_spec=pltpu.PrefetchScalarGridSpec(
            num_scalar_prefetch=1,
            grid=(inputs // block,),
            in_specs=[
                pl.BlockSpec((block, samples), lambda i, h: (i, 0)),
                pl.BlockSpec(window.shape, lambda i, h: (0, 0)),
                pl.BlockSpec((rows, FFTLEN), lambda i, h: (halves - 1 - h[0], 0)),
            ],
            out_specs=(whole4, whole2),
            scratch_shapes=[spread],
        ),
        compiler_params=PARAMS,
        cost_estimate=pl.CostEstimate(
            flops=4 * rows * FFTLEN * TIME * inputs, bytes_accessed=14 << 20, transcendentals=0
        ),
        name="fold",
    )(half_id, voltages, window, table)
    near = pl.pallas_call(
        near_kernel,
        out_shape=out,
        grid_spec=pltpu.PrefetchScalarGridSpec(
            num_scalar_prefetch=1,
            grid=(1,),
            in_specs=[whole2, pl.BlockSpec((rows, FFTLEN), lambda i, h: (h[0], 0))],
            out_specs=whole4,
            scratch_shapes=[spread],
        ),
        compiler_params=PARAMS,
        cost_estimate=pl.CostEstimate(
            flops=2 * rows * FFTLEN * TIME * inputs, bytes_accessed=8 << 20, transcendentals=0
        ),
        name="near",
    )(half_id, folded, table)
    return far, near


def form_beams(x, gains, places, directions, first, out_type):
    sources, chans, rows, inputs = x.shape
    beams = directions.shape[1]
    total = sources * inputs
    if inputs != 128:
        x = x.transpose(1, 2, 0, 3).reshape(chans, rows, total // 128, 128)
        x = x.transpose(2, 0, 1, 3)
    depth = 256
    blocks = depth // 128
    tiles = total // depth
    return pl.pallas_call(
        beam_kernel,
        out_shape=jax.ShapeDtypeStruct((chans, rows, beams), out_type),
        grid_spec=pltpu.PrefetchScalarGridSpec(
            num_scalar_prefetch=1,
            grid=(tiles + 1,),
            in_specs=[
                pl.BlockSpec(
                    (blocks, chans, rows, 128), lambda i, f: (jnp.maximum(i - 1, 0), 0, 0, 0)
                ),
                pl.BlockSpec((chans, 2, depth), lambda i, f: (0, 0, jnp.maximum(i - 1, 0))),
                pl.BlockSpec((depth, 3), lambda i, f: (jnp.minimum(i, tiles - 1), 0)),
                pl.BlockSpec(directions.shape, lambda i, f: (0, 0)),
            ],
            out_specs=pl.BlockSpec((chans, rows, beams), lambda i, f: (0, 0, 0)),
            scratch_shapes=[
                pltpu.VMEM((2, chans, 2 * depth, beams), BF16),
                pltpu.VMEM((chans, rows, beams), F32),
            ],
        ),
        compiler_params=PARAMS,
        cost_estimate=pl.CostEstimate(
            flops=32 * chans * rows * total * beams, bytes_accessed=6 << 20, transcendentals=0
        ),
        name="beams",
    )(first, x, gains, places, directions)


def powers(own, far, search_beams, copies):
    chans, rows, beams = own.shape
    search = search_beams.shape[0]
    width = TIME * search
    pick = jnp.tile(search_beams, 128 // search)[None, :]
    table = time_table(search)
    high = jnp.asarray(table).astype(BF16)
    low = (jnp.asarray(table) - high.astype(F32)).astype(BF16)
    block = min(4, chans)
    cube = pl.BlockSpec((block, rows, beams), lambda i: (i, 0, 0))
    flat = lambda shape: pl.BlockSpec(shape, lambda i: (0,) * len(shape))
    return pl.pallas_call(
        power_kernel,
        out_shape=(
            jax.ShapeDtypeStruct((chans, TIME, beams), F32),
            jax.ShapeDtypeStruct((copies, chans, width), BF16),
        ),
        grid=(chans // block,),
        in_specs=[cube, cube, flat(pick.shape), flat(high.shape), flat(low.shape)],
        out_specs=(
            pl.BlockSpec((block, TIME, beams), lambda i: (i, 0, 0)),
            flat((copies, chans, width)),
        ),
        scratch_shapes=[pltpu.VMEM((chans, width), F32)],
        compiler_params=PARAMS,
        name="power",
    )(own, far, pick, high, low)


def on_device(voltages, gains, positions, directions, input_order, delays, search_beams):
    devices = lax.axis_size("crate")
    position = lax.axis_index("crate")
    chans = gains.shape[0]
    halves = 2
    per_half = devices // halves
    half_id = position // per_half
    members = [list(range(h * per_half, (h + 1) * per_half)) for h in range(halves)]
    partners = [(d, (d + per_half) % devices) for d in range(devices)]
    inputs = gains.shape[2] // halves

    own_inputs = half_id * inputs
    other_inputs = inputs - own_inputs
    far_gains = lax.ppermute(
        lax.dynamic_slice_in_dim(gains, other_inputs, inputs, 2), "crate", partners
    )
    near_gains = lax.dynamic_slice_in_dim(gains, own_inputs, inputs, 2)
    half_scalar = half_id.astype(jnp.int32).reshape(1)
    far, near = channelize(voltages, half_scalar, halves, chans)

    def exchange(x):
        return lax.all_to_all(
            x, "crate", split_axis=0, concat_axis=0, axis_index_groups=members, tiled=True
        )

    far = exchange(far)
    far, near = lax.optimization_barrier((far, near))
    near = exchange(near)

    order = lax.dynamic_slice_in_dim(input_order, own_inputs, inputs, 0)
    places = jnp.take(positions.T, order, axis=0)
    own_first = (position * chans).astype(jnp.int32).reshape(1)
    far_first = ((position + per_half) % devices * chans).astype(jnp.int32).reshape(1)
    far_sums = form_beams(far, far_gains, places, directions, far_first, BF16)
    far_sums = lax.ppermute(far_sums, "crate", partners)
    near_sums = form_beams(near, near_gains, places, directions, own_first, F32)

    beam_power, spectrum = powers(near_sums, far_sums, search_beams, devices)
    spectrum = lax.all_to_all(spectrum, "crate", split_axis=0, concat_axis=0, tiled=True)
    width = spectrum.shape[-1]
    trials = delays.shape[0] // devices
    own_delays = lax.dynamic_slice_in_dim(delays, position * trials, trials, 0)
    turns = jax.ShapeDtypeStruct((HALF_BINS * trials, 2 * CH), BF16)
    high, low = pl.pallas_call(
        turn_kernel, out_shape=(turns, turns), compiler_params=PARAMS, name="turns"
    )(own_delays)
    dm_plane = pl.pallas_call(
        plane_kernel,
        out_shape=jax.ShapeDtypeStruct((search_beams.shape[0], TIME, trials), F32),
        compiler_params=PARAMS,
        name="plane",
    )(spectrum.reshape(CH, width), high, low)
    return beam_power.transpose(0, 2, 1), dm_plane.transpose(2, 0, 1)


def solution(mesh):
    in_specs = (P(("groups", "crate"), None), P("crate", None, None), P(), P(), P(), P(), P())
    out_specs = (P(("groups", "crate"), None, None), P(("groups", "crate"), None, None))
    return jax.shard_map(
        on_device, mesh=mesh, in_specs=in_specs, out_specs=out_specs, check_vma=False
    )
```

time: 857 us -> 178 us (0.21); the launches traced: 847 us -> 178 us
  other arithmetic: 544 us -> 1.02 us
  local copies, waits for them, and re-layouts: 96.2 us -> 7.52 us
  Pallas kernels: 0 us -> 84.8 us
  matrix products: 71.6 us -> 0 us
  blocking collectives: 45.6 us -> 0 us
  starting transfers between devices: 7.6 us -> 21.2 us
  loops' own time: 11.3 us -> 0 us
    convert_element_type x16 -> x0, other arithmetic: 275 us -> none  [steering(): ((gain_row[1] * cosine - gain_row[0] * sine_part) * weight_norm).astype(j...]
    neg x16 -> x0, other arithmetic: 266 us -> none  [steering(): upper_rows = jnp.concatenate([w_real, -w_imag], axis=1)]
    pallas_call x0 -> x7, Pallas kernels: none -> 84.8 us  [the longest x2 50.9 us: form_beams(): pl.pallas_call(beam_kernel, out_shape=jax.ShapeDtypeStruct((chans, rows,...]
    dot_general x22 -> x0, matrix products: 71.6 us -> none  [the longest x16 40.2 us: one_channel(): jnp.dot(weights, channel_data.reshape(2 * INPUTS, channel_data.shape[-1])...]
    all_to_all x1 -> x3, waiting for transfers between devices: 69.6 us -> 23.9 us  [the longest x2 17.3 us: exchange(): lax.all_to_all(x, 'crate', split_axis=0, concat_axis=0, axis_index_groups...]
    all_gather x1 -> x0, blocking collectives: 45.6 us -> none  [on_device(): lax.all_gather(power_spectra, 'crate', axis=0, tiled=True)]
    ppermute x0 -> x2, waiting for transfers between devices: none -> 38.3 us  [the longest x1 20.3 us: on_device(): far_sums = lax.ppermute(far_sums, 'crate', partners)]
    dynamic_slice x33 -> x2, local copies, waits for them, and re-layouts: 30.2 us -> 1.32 us  [the longest x1 0.68 us: on_device(): lax.dynamic_slice_in_dim(gains, other_inputs, inputs, 2)]
  transfers between devices with their start and end apart: 1 -> 5, of which waited for: 1 -> 4; matrix products, arithmetic and copies ran while one was open for 1% -> 3% of each run, Pallas kernels for 0% -> 35%
where the time goes in v1:
time: 178 us
  Pallas kernels  84.8 us (48%)
  waiting for transfers between devices  62.2 us (35%)
  starting transfers between devices  21.2 us (12%)
  local copies, waits for them, and re-layouts  7.52 us (4%)
    pallas_call x2, Pallas kernels, form_beams(): pl.pallas_call(beam_kernel, out_shape=jax.ShapeDtypeStruct((chans, rows,...  50.9 us
    ppermute x1, waiting for transfers between devices, on_device(): far_sums = lax.ppermute(far_sums, 'crate', partners)  20.3 us
    ppermute x1, waiting for transfers between devices, on_device(): lax.ppermute(lax.dynamic_slice_in_dim(gains, other_inputs, inputs, 2), 'c...  18.1 us
    all_to_all x2, waiting for transfers between devices, exchange(): lax.all_to_all(x, 'crate', split_axis=0, concat_axis=0, axis_index_groups...  17.3 us
    pallas_call x1, Pallas kernels, channelize(): pl.pallas_call(fold_kernel, out_shape=(out, folded), grid_spec=pltpu.Pref...  12 us
    all_to_all x2, starting transfers between devices, exchange(): lax.all_to_all(x, 'crate', split_axis=0, concat_axis=0, axis_index_groups...  9.63 us
    pallas_call x1, Pallas kernels, channelize(): pl.pallas_call(near_kernel, out_shape=out, grid_spec=pltpu.PrefetchScalar...  8.44 us
    all_to_all x1, waiting for transfers between devices, on_device(): lax.all_to_all(spectrum, 'crate', split_axis=0, concat_axis=0, tiled=True)  6.62 us
  transfers between devices with their start and end apart: 5, of which 4 were waited for; matrix products, arithmetic and copies ran while one was open for 3% of the time, Pallas kernels for 35%

profile of v1, /device:TPU:0, one launch (start us, length us, event | category | flops | bytes accessed | tf_op | source)
XLA Modules:
  0.0 177.6 jit_solution(17579790837804505740)
XLA Ops:
  0.6 0.0 copy-start
  0.7 12.0 %fold.1 = (bf16[8,16,64,128]{3,2,1,0:T(8,128)(2,1)}, bf16[4096,512]{1,0:T(8,128)(2,1)}) custom-call(s32[1]{0:T(128)} %bitcast.1.half_ref, bf16[128,17920]{1,0:T(8,128)(2,1)} %volt_ref.1, f32[4,512]{1,0:T(4,128)} %constant.62.clone.window_ref, bf16[512,512]{1,0:T(8,128)(2,1)} %constant.65.table_ref), custom_call_target="tpu_custom_call" | custom-call | flops 2147483648 | bytes 14680064 | tf_op jit(solution)/shard_map/fold/pallas_call | solution.py:290
  12.7 5.3 %all-to-all-start = ((bf16[8,16,64,128]{3,2,1,0:T(8,128)(2,1)}), bf16[8,16,64,128]{3,2,1,0:T(8,128)(2,1)S(1)}, u32[]{:S(2)}, u32[]{:S(2)}) async-start(bf16[8,16,64,128]{3,2,1,0:T(8,128)(2,1)} %get-tuple-element.10), calls=%async_computation | async-start | bytes 4194304 | tf_op jit(solution)/shard_map/all_to_all | solution.py:417
  18.0 8.4 %near.1 = bf16[8,16,64,128]{3,2,1,0:T(8,128)(2,1)} custom-call(s32[1]{0:T(128)} %bitcast.1.half_ref, bf16[4096,512]{1,0:T(8,128)(2,1)} %get-tuple-element.11.folded_ref, bf16[512,512]{1,0:T(8,128)(2,1)} %constant.65.table_ref), custom_call_target="tpu_custom_call" | custom-call | flops 1073741824 | bytes 8388608 | tf_op jit(solution)/shard_map/near/pallas_call | solution.py:310
  26.4 17.3 %all-to-all-done.x_ref = bf16[8,16,64,128]{3,2,1,0:T(8,128)(2,1)S(1)} async-done(((bf16[8,16,64,128]{3,2,1,0:T(8,128)(2,1)}), bf16[8,16,64,128]{3,2,1,0:T(8,128)(2,1)S(1)}, u32[]{:S(2)}, u32[]{:S(2)}) %all-to-all-start) | async-done | bytes 2097184 | tf_op jit(solution)/shard_map/all_to_all | solution.py:417
  43.7 4.3 %all-to-all-start.1 = ((bf16[8,16,64,128]{3,2,1,0:T(8,128)(2,1)}), bf16[8,16,64,128]{3,2,1,0:T(8,128)(2,1)}, u32[]{:S(2)}, u32[]{:S(2)}) async-start(bf16[8,16,64,128]{3,2,1,0:T(8,128)(2,1)} %near.1), calls=%async_computation.1 | async-start | bytes 4194304 | tf_op jit(solution)/shard_map/all_to_all | solution.py:417
  48.1 0.0 copy-done.1
  48.1 0.0 copy-done.4
  48.1 0.7 constant_dynamic-slice_fusion.1
  48.8 2.6 %collective-permute-start = (f32[16,2,1024]{2,1,0:T(2,128)S(1)}, f32[16,2,1024]{2,1,0:T(2,128)S(1)}, u32[]{:S(2)}, u32[]{:S(2)}) collective-permute-start(f32[16,2,1024]{2,1,0:T(2,128)S(1)} %get-tuple-element.18), channel_id=1, source_target_pairs={{0,8},{1,9},{2,10},{3,11},{4,12},{5,13},{6,14},{7,15},{8,0},{9,1},... | collective-permute-start | bytes 393224 | tf_op jit(solution)/shard_map/ppermute | solution.py:409
  51.4 0.0 copy-done.5
  51.4 0.4 copy.12
  51.7 0.0 copy-done.7
  51.8 0.7 broadcast_in_dim_tile.3.pick_ref
  52.4 0.0 copy-done.6
  52.4 2.8 %gather_fusion = f32[1024,3]{1,0:T(8,128)S(1)} fusion(f32[2048,3]{1,0:T(8,128)S(1)} %bitcast.7, s32[1024]{0:T(1024)S(1)} %fusion), kind=kCustom, calls=%fused_computation | custom fusion | bytes 28672 | tf_op jit(solution)/shard_map/jit(_take)/gather | solution.py:426
  55.3 1.0 broadcast_select_fusion.place_ref
  56.3 18.1 %collective-permute-done.gain_ref = f32[16,2,1024]{2,1,0:T(2,128)S(1)} collective-permute-done((f32[16,2,1024]{2,1,0:T(2,128)S(1)}, f32[16,2,1024]{2,1,0:T(2,128)S(1)}, u32[]{:S(2)}, u32[]{:S(2)}) %collective-permute-start) | collective-permute-done | bytes 131104 | tf_op jit(solution)/shard_map/ppermute | solution.py:409
  74.4 0.7 copy-done.8
  75.0 25.3 %beams.3 = bf16[16,64,512]{2,1,0:T(8,128)(2,1)} custom-call(s32[1]{0:T(128)} %bitcast.3.first_ref, bf16[8,16,64,128]{3,2,1,0:T(8,128)(2,1)} %copy-done.1, f32[16,2,1024]{2,1,0:T(2,128)} %copy-done.8, f32[1024,3]{1,0:T(8,128)} %broadcast_select_fusion.place_ref, f32[3,512]{1,0:T(4,128)} %dir_ref.3), custom_call_target="tpu_custom_call" | custom-call | flops 17179869184 | bytes 6291456 | tf_op jit(solution)/shard_map/beams/pallas_call | solution.py:339
  100.3 3.4 %collective-permute-start.1 = (bf16[16,64,512]{2,1,0:T(8,128)(2,1)}, bf16[16,64,512]{2,1,0:T(8,128)(2,1)S(1)}, u32[]{:S(2)}, u32[]{:S(2)}) collective-permute-start(bf16[16,64,512]{2,1,0:T(8,128)(2,1)} %beams.3), channel_id=1, source_target_pairs={{0,8},{1,9},{2,10},{3,11},{4,12},{5,13},{6,14},{7,15},{8,0},{9,1},... | collective-permute-start | bytes 3145736 | tf_op jit(solution)/shard_map/ppermute | solution.py:430
  103.7 0.0 all-to-all-done.1.x_ref
  103.7 25.6 %beams.2.own_ref = f32[16,64,512]{2,1,0:T(8,128)} custom-call(s32[1]{0:T(128)} %bitcast.first_ref, bf16[8,16,64,128]{3,2,1,0:T(8,128)(2,1)} %all-to-all-done.1.x_ref, f32[16,2,1024]{2,1,0:T(2,128)} %get-tuple-element.19.gain_ref, f32[1024,3]{1,0:T(8,128)} %broadcast_select_fusion.place_ref, f32[3,512]{1,0:T(4,128)} %dir_ref.3), custom_call_target="tpu_custom_call" | custom-call | flops 17179869184 | bytes 6291456 | tf_op jit(solution)/shard_map/beams/pallas_call | solution.py:339
  129.3 20.3 %collective-permute-done.1.far_ref = bf16[16,64,512]{2,1,0:T(8,128)(2,1)S(1)} collective-permute-done((bf16[16,64,512]{2,1,0:T(8,128)(2,1)}, bf16[16,64,512]{2,1,0:T(8,128)(2,1)S(1)}, u32[]{:S(2)}, u32[]{:S(2)}) %collective-permute-start.1) | collective-permute-done | bytes 1048608 | tf_op jit(solution)/shard_map/ppermute | solution.py:430
  149.6 1.0 copy-done.2
  150.6 5.0 %power.1 = (f32[16,32,512]{2,1,0:T(8,128)}, bf16[16,16,512]{2,1,0:T(8,128)(2,1)}) custom-call(f32[16,64,512]{2,1,0:T(8,128)} %beams.2.own_ref, bf16[16,64,512]{2,1,0:T(8,128)(2,1)} %copy-done.2, s32[1,128]{1,0:T(1,128)} %broadcast_in_dim_tile.3.pick_ref, bf16[512,512]{1,0:T(8,128)(2,1)} %constant.66.high_ref, bf16[512,512]{1,0:T(8,128)(2,1)} %constant.69.low_ref), custom_call_target="tpu_custom_call" | custom-call | tf_op jit(solution)/shard_map/power/pallas_call | solution.py:378
  155.6 5.6 %all-to-all-start.2 = ((bf16[16,16,512]{2,1,0:T(8,128)(2,1)}), bf16[16,16,512]{2,1,0:T(8,128)(2,1)S(1)}, u32[]{:S(2)}, u32[]{:S(2)}) async-start(bf16[16,16,512]{2,1,0:T(8,128)(2,1)} %get-tuple-element.15), calls=%async_computation.2 | async-start | bytes 524288 | tf_op jit(solution)/shard_map/all_to_all | solution.py:434
  161.3 0.6 constant_dynamic-slice_fusion.delay_ref
  161.9 2.7 %turns.1 = (bf16[1024,512]{1,0:T(8,128)(2,1)}, bf16[1024,512]{1,0:T(8,128)(2,1)}) custom-call(s32[64,256]{1,0:T(8,128)} %constant_dynamic-slice_fusion.delay_ref), custom_call_target="tpu_custom_call" | custom-call | tf_op jit(solution)/shard_map/turns/pallas_call | solution.py:439
  164.7 6.6 %all-to-all-done.2 = bf16[16,16,512]{2,1,0:T(8,128)(2,1)S(1)} async-done(((bf16[16,16,512]{2,1,0:T(8,128)(2,1)}), bf16[16,16,512]{2,1,0:T(8,128)(2,1)S(1)}, u32[]{:S(2)}, u32[]{:S(2)}) %all-to-all-start.2) | async-done | bytes 262176 | tf_op jit(solution)/shard_map/all_to_all | solution.py:434
  171.3 0.7 copy-done.3
  172.0 5.6 %plane.1 = f32[16,32,64]{2,1,0:T(8,128)} custom-call(bf16[256,512]{1,0:T(8,128)(2,1)} %bitcast.8, bf16[1024,512]{1,0:T(8,128)(2,1)} %get-tuple-element.16.high_ref, bf16[1024,512]{1,0:T(8,128)(2,1)} %get-tuple-element.17.low_ref), custom_call_target="tpu_custom_call" | custom-call | tf_op jit(solution)/shard_map/plane/pallas_call | solution.py:442
  (12 shorter events, 0.0 us)
Async XLA Ops:
  0.6 160.7 %copy-start = (s32[1024,256]{1,0:T(8,128)S(1)}, s32[1024,256]{1,0:T(8,128)}, u32[]{:S(2)}) copy-start(s32[1024,256]{1,0:T(8,128)} %param.15) | copy-start | bytes 3145732
  12.7 31.0 %all-to-all-start = ((bf16[8,16,64,128]{3,2,1,0:T(8,128)(2,1)}), bf16[8,16,64,128]{3,2,1,0:T(8,128)(2,1)S(1)}, u32[]{:S(2)}, u32[]{:S(2)}) async-start(bf16[8,16,64,128]{3,2,1,0:T(8,128)(2,1)} %get-tuple-element.10), calls=%async_computation | async-start | bytes 4194304 | tf_op jit(solution)/shard_map/all_to_all | solution.py:417
  26.4 21.7 %copy-start.4 = (f32[16,2,2048]{2,1,0:T(2,128)S(1)}, f32[16,2,2048]{2,1,0:T(2,128)}, u32[]{:S(2)}) copy-start(f32[16,2,2048]{2,1,0:T(2,128)} %param.11) | copy-start | bytes 786436
  26.4 24.9 %copy-start.5 = (f32[3,2048]{1,0:T(4,128)S(1)}, f32[3,2048]{1,0:T(4,128)}, u32[]{:S(2)}) copy-start(f32[3,2048]{1,0:T(4,128)} %param.12) | copy-start | bytes 73732
  26.4 25.3 %copy-start.7 = (s32[16]{0:T(128)S(1)}, s32[16]{0:T(128)}, u32[]{:S(2)}) copy-start(s32[16]{0:T(128)} %param.16) | copy-start | bytes 196
  26.4 26.0 %copy-start.6 = (s32[2048]{0:T(1024)S(1)}, s32[2048]{0:T(1024)}, u32[]{:S(2)}) copy-start(s32[2048]{0:T(1024)} %param.14) | copy-start | bytes 24580
  43.7 4.4 %copy-start.1 = (bf16[8,16,64,128]{3,2,1,0:T(8,128)(2,1)}, bf16[8,16,64,128]{3,2,1,0:T(8,128)(2,1)S(1)}, u32[]{:S(2)}) copy-start(bf16[8,16,64,128]{3,2,1,0:T(8,128)(2,1)S(1)} %all-to-all-done.x_ref) | copy-start | bytes 6291460
  43.7 60.0 %all-to-all-start.1 = ((bf16[8,16,64,128]{3,2,1,0:T(8,128)(2,1)}), bf16[8,16,64,128]{3,2,1,0:T(8,128)(2,1)}, u32[]{:S(2)}, u32[]{:S(2)}) async-start(bf16[8,16,64,128]{3,2,1,0:T(8,128)(2,1)} %near.1), calls=%async_computation.1 | async-start | bytes 4194304 | tf_op jit(solution)/shard_map/all_to_all | solution.py:417
  48.8 25.6 %collective-permute-start = (f32[16,2,1024]{2,1,0:T(2,128)S(1)}, f32[16,2,1024]{2,1,0:T(2,128)S(1)}, u32[]{:S(2)}, u32[]{:S(2)}) collective-permute-start(f32[16,2,1024]{2,1,0:T(2,128)S(1)} %get-tuple-element.18), channel_id=1, source_target_pairs={{0,8},{1,9},{2,10},{3,11},{4,12},{5,13},{6,14},{7,15},{8,0},{9,1},... | collective-permute-start | bytes 393224 | tf_op jit(solution)/shard_map/ppermute | solution.py:409
  74.4 0.7 copy-start.8
  100.3 49.3 %collective-permute-start.1 = (bf16[16,64,512]{2,1,0:T(8,128)(2,1)}, bf16[16,64,512]{2,1,0:T(8,128)(2,1)S(1)}, u32[]{:S(2)}, u32[]{:S(2)}) collective-permute-start(bf16[16,64,512]{2,1,0:T(8,128)(2,1)} %beams.3), channel_id=1, source_target_pairs={{0,8},{1,9},{2,10},{3,11},{4,12},{5,13},{6,14},{7,15},{8,0},{9,1},... | collective-permute-start | bytes 3145736 | tf_op jit(solution)/shard_map/ppermute | solution.py:430
  149.6 1.0 copy-start.2
  155.6 15.7 %all-to-all-start.2 = ((bf16[16,16,512]{2,1,0:T(8,128)(2,1)}), bf16[16,16,512]{2,1,0:T(8,128)(2,1)S(1)}, u32[]{:S(2)}, u32[]{:S(2)}) async-start(bf16[16,16,512]{2,1,0:T(8,128)(2,1)} %get-tuple-element.15), calls=%async_computation.2 | async-start | bytes 524288 | tf_op jit(solution)/shard_map/all_to_all | solution.py:434
  171.3 0.7 copy-start.3

commit v2 on v1

--- a/solution.py
+++ b/solution.py
@@ -93,7 +93,7 @@
             spread_ref[pl.ds(index * group + part, rows, stride=TIME), :] = piece
         return carry
 
-    lax.fori_loop(0, TIME // group, step, 0, unroll=2)
+    lax.fori_loop(0, TIME // group, step, 0, unroll=4)
     dests, chans = out_ref.shape[:2]
     per_chan = 2 * TIME
 
@@ -103,7 +103,7 @@
             out_ref[dest, chan] = spread_ref[pl.ds(start, per_chan), :].astype(BF16)
         return carry
 
-    lax.fori_loop(0, dests, pack, 0)
+    lax.fori_loop(0, dests, pack, 0, unroll=2)
 
 
 def fold_kernel(half_ref, volt_ref, window_ref, table_ref, out_ref, folded_ref, spread_ref):
@@ -136,7 +136,7 @@
 
 
 def beam_kernel(
-    first_ref, x_ref, gain_ref, place_ref, dir_ref, out_ref, weight_ref, sum_ref
+    first_ref, x_ref, gain_ref, place_ref, dir_ref, out_ref, even_ref, odd_ref, sum_ref
 ):
     step = pl.program_id(0)
     tiles = pl.num_programs(0) - 1
@@ -144,10 +144,8 @@
     depth = place_ref.shape[0]
     wide = 256
     chunk = depth // chans
-    now = lax.rem(step, 2)
-    before = 1 - now
-
-    def generate(part):
+
+    def generate(part, weight_ref):
         for sub in range(0, chunk, 16):
             row = pl.multiple_of(part * chunk + sub, 16)
             place = place_ref[pl.ds(row, 16), :]
@@ -160,13 +158,18 @@
                 first = 1.0 + first_ref[0].astype(F32) * (1.0 / CH)
                 c, s = cos_sin_turns(geometry * first)
                 dc, ds = cos_sin_turns(geometry * (1.0 / CH))
+                next_c, next_s = c * dc - s * ds, c * ds + s * dc
+                twice = dc + dc
                 for chan in range(chans):
-                    weight_ref[now, chan, pl.ds(row, 16), lanes] = c.astype(BF16)
-                    weight_ref[now, chan, pl.ds(depth + row, 16), lanes] = s.astype(BF16)
-                    if chan + 1 < chans:
-                        c, s = c * dc - s * ds, c * ds + s * dc
-
-    def accumulate(chan):
+                    weight_ref[chan, pl.ds(row, 16), lanes] = c.astype(BF16)
+                    weight_ref[chan, pl.ds(depth + row, 16), lanes] = s.astype(BF16)
+                    if chan + 2 < chans:
+                        c, next_c = next_c, twice * next_c - c
+                        s, next_s = next_s, twice * next_s - s
+                    else:
+                        c, s = next_c, next_s
+
+    def accumulate(chan, weight_ref):
         blocks = x_ref.shape[0]
         data = jnp.concatenate([x_ref[k, chan] for k in range(blocks)], axis=1).astype(F32)
         real, imag = data[:TIME], data[TIME:]
@@ -176,39 +179,43 @@
         top = jnp.concatenate([x0, x1], axis=1)
         bottom = jnp.concatenate([x1, -x0], axis=1)
         both = jnp.concatenate([top, bottom], axis=0)
-        return jnp.dot(both, weight_ref[before, chan], preferred_element_type=F32)
+        return jnp.dot(both, weight_ref[chan], preferred_element_type=F32)
+
+    def both(m, weights):
+        sum_ref[m] += accumulate(m, weights[0])
+        generate(m, weights[1])
+
+    def last(m, weights):
+        out_ref[m] = (sum_ref[m] + accumulate(m, weights[0])).astype(out_ref.dtype)
+
+    def over_channels(body, weights):
+        lax.fori_loop(0, chans, lambda m, v: (body(m, weights), v)[1], 0, unroll=min(8, chans))
 
     @pl.when(step == 0)
     def _():
         sum_ref[...] = jnp.zeros_like(sum_ref)
-        lax.fori_loop(0, chans, lambda m, v: (generate(m), v)[1], 0)
-
-    @pl.when((step > 0) & (step < tiles))
-    def _():
-        def both(m, v):
-            sum_ref[m] += accumulate(m)
-            generate(m)
-            return v
-
-        lax.fori_loop(0, chans, both, 0)
-
-    @pl.when(step == tiles)
-    def _():
-        def last(m, v):
-            out_ref[m] = (sum_ref[m] + accumulate(m)).astype(out_ref.dtype)
-            return v
-
-        lax.fori_loop(0, chans, last, 0)
+        over_channels(lambda m, w: generate(m, w), even_ref)
+
+    for parity, weights in ((1, (even_ref, odd_ref)), (0, (odd_ref, even_ref))):
+
+        @pl.when((step > 0) & (step < tiles) & (lax.rem(step, 2) == parity))
+        def _(weights=weights):
+            over_channels(both, weights)
+
+        @pl.when((step == tiles) & (lax.rem(step, 2) == parity))
+        def _(weights=weights):
+            over_channels(last, weights)
 
 
 def power_kernel(
-    own_ref, far_ref, pick_ref, high_ref, low_ref, power_ref, spec_ref, chosen_ref
+    own_ref, far0_ref, far1_ref, pick_ref, high_ref, low_ref, power_ref, spec_ref, chosen_ref
 ):
     step = pl.program_id(0)
     block, _, beams = own_ref.shape
     search = chosen_ref.shape[1] // TIME
     per = 128 // search
-    total = own_ref[...] + far_ref[...].astype(F32)
+    far = jnp.concatenate([far0_ref[...], far1_ref[...]], axis=2)
+    total = own_ref[...] + far.astype(F32)
     real, imag = total[:, :TIME], total[:, TIME:]
     power = (real * real + imag * imag) * (1.0 / 2048)
     power_ref[...] = power
@@ -352,7 +359,8 @@
             ],
             out_specs=pl.BlockSpec((chans, rows, beams), lambda i, f: (0, 0, 0)),
             scratch_shapes=[
-                pltpu.VMEM((2, chans, 2 * depth, beams), BF16),
+                pltpu.VMEM((chans, 2 * depth, beams), BF16),
+                pltpu.VMEM((chans, 2 * depth, beams), BF16),
                 pltpu.VMEM((chans, rows, beams), F32),
             ],
         ),
@@ -364,16 +372,15 @@
     )(first, x, gains, places, directions)
 
 
-def powers(own, far, search_beams, copies):
+def powers(own, far, pick, search, copies):
     chans, rows, beams = own.shape
-    search = search_beams.shape[0]
     width = TIME * search
-    pick = jnp.tile(search_beams, 128 // search)[None, :]
     table = time_table(search)
     high = jnp.asarray(table).astype(BF16)
     low = (jnp.asarray(table) - high.astype(F32)).astype(BF16)
     block = min(4, chans)
     cube = pl.BlockSpec((block, rows, beams), lambda i: (i, 0, 0))
+    far_cubes = [pl.BlockSpec((block, rows, x.shape[2]), lambda i: (i, 0, 0)) for x in far]
     flat = lambda shape: pl.BlockSpec(shape, lambda i: (0,) * len(shape))
     return pl.pallas_call(
         power_kernel,
@@ -382,7 +389,7 @@
             jax.ShapeDtypeStruct((copies, chans, width), BF16),
         ),
         grid=(chans // block,),
-        in_specs=[cube, cube, flat(pick.shape), flat(high.shape), flat(low.shape)],
+        in_specs=[cube, *far_cubes, flat(pick.shape), flat(high.shape), flat(low.shape)],
         out_specs=(
             pl.BlockSpec((block, TIME, beams), lambda i: (i, 0, 0)),
             flat((copies, chans, width)),
@@ -390,7 +397,7 @@
         scratch_shapes=[pltpu.VMEM((chans, width), F32)],
         compiler_params=PARAMS,
         name="power",
-    )(own, far, pick, high, low)
+    )(own, *far, pick, high, low)
 
 
 def on_device(voltages, gains, positions, directions, input_order, delays, search_beams):
@@ -403,13 +410,7 @@
     members = [list(range(h * per_half, (h + 1) * per_half)) for h in range(halves)]
     partners = [(d, (d + per_half) % devices) for d in range(devices)]
     inputs = gains.shape[2] // halves
-
     own_inputs = half_id * inputs
-    other_inputs = inputs - own_inputs
-    far_gains = lax.ppermute(
-        lax.dynamic_slice_in_dim(gains, other_inputs, inputs, 2), "crate", partners
-    )
-    near_gains = lax.dynamic_slice_in_dim(gains, own_inputs, inputs, 2)
     half_scalar = half_id.astype(jnp.int32).reshape(1)
     far, near = channelize(voltages, half_scalar, halves, chans)
 
@@ -419,18 +420,32 @@
         )
 
     far = exchange(far)
-    far, near = lax.optimization_barrier((far, near))
-    near = exchange(near)
-
+    near, gains, positions = lax.optimization_barrier((near, gains, positions))
+    far_gains = lax.ppermute(
+        lax.dynamic_slice_in_dim(gains, inputs - own_inputs, inputs, 2), "crate", partners
+    )
+    near_gains = lax.dynamic_slice_in_dim(gains, own_inputs, inputs, 2)
     order = lax.dynamic_slice_in_dim(input_order, own_inputs, inputs, 0)
     places = jnp.take(positions.T, order, axis=0)
+    search = search_beams.shape[0]
+    pick = jnp.tile(search_beams, 128 // search)[None, :]
     own_first = (position * chans).astype(jnp.int32).reshape(1)
     far_first = ((position + per_half) % devices * chans).astype(jnp.int32).reshape(1)
-    far_sums = form_beams(far, far_gains, places, directions, far_first, BF16)
-    far_sums = lax.ppermute(far_sums, "crate", partners)
+    far, near, far_gains, near_gains, places, pick = lax.optimization_barrier(
+        (far, near, far_gains, near_gains, places, pick)
+    )
+    near = exchange(near)
+
+    beams = directions.shape[1]
+    cut = beams // 2
+    far_sums = []
+    for start in range(0, beams, cut):
+        some = lax.slice_in_dim(directions, start, start + cut, axis=1)
+        part = form_beams(far, far_gains, places, some, far_first, BF16)
+        far_sums.append(lax.ppermute(part, "crate", partners))
     near_sums = form_beams(near, near_gains, places, directions, own_first, F32)
 
-    beam_power, spectrum = powers(near_sums, far_sums, search_beams, devices)
+    beam_power, spectrum = powers(near_sums, far_sums, pick, search, devices)
     spectrum = lax.all_to_all(spectrum, "crate", split_axis=0, concat_axis=0, tiled=True)
     width = spectrum.shape[-1]
     trials = delays.shape[0] // devices

time: 178 us -> 138 us (0.78)
  waiting for transfers between devices: 62.2 us -> 35.6 us
  Pallas kernels: 84.8 us -> 70.8 us
    ppermute x2 -> x3, waiting for transfers between devices: 38.3 us -> 14.5 us  [the longest x1 10.1 us: on_device(): lax.ppermute(lax.dynamic_slice_in_dim(gains, inputs - own_inputs, inputs,...]
    pallas_call x2 -> x3, Pallas kernels: 50.9 us -> 38.7 us  [form_beams(): pl.pallas_call(beam_kernel, out_shape=jax.ShapeDtypeStruct((chans, rows,...]
    all_to_all x2, waiting for transfers between devices: 17.3 us -> 14.4 us  [exchange(): lax.all_to_all(x, 'crate', split_axis=0, concat_axis=0, axis_index_groups...]
    ppermute x2 -> x3, starting transfers between devices: 5.97 us -> 6.08 us  [the longest x1 3.16 us: on_device(): lax.ppermute(lax.dynamic_slice_in_dim(gains, inputs - own_inputs, inputs,...]
  transfers between devices with their start and end apart: 5 -> 6, of which waited for: 4 -> 5; matrix products, arithmetic and copies ran while one was open for 3% -> 5% of each run, Pallas kernels for 35% -> 36%
where the time goes in v2:
time: 138 us; the launch traced here: 137 us
  Pallas kernels  70.8 us (51%)
  waiting for transfers between devices  35.6 us (26%)
  starting transfers between devices  21.2 us (15%)
  local copies, waits for them, and re-layouts  7.76 us (6%)
    pallas_call x3, Pallas kernels, form_beams(): pl.pallas_call(beam_kernel, out_shape=jax.ShapeDtypeStruct((chans, rows,...  38.7 us
    all_to_all x2, waiting for transfers between devices, exchange(): lax.all_to_all(x, 'crate', split_axis=0, concat_axis=0, axis_index_groups...  14.4 us
    pallas_call x1, Pallas kernels, channelize(): pl.pallas_call(fold_kernel, out_shape=(out, folded), grid_spec=pltpu.Pref...  11.1 us
    all_to_all x2, starting transfers between devices, exchange(): lax.all_to_all(x, 'crate', split_axis=0, concat_axis=0, axis_index_groups...  11 us
    ppermute x1, waiting for transfers between devices, on_device(): lax.ppermute(lax.dynamic_slice_in_dim(gains, inputs - own_inputs, inputs,...  10.1 us
    pallas_call x1, Pallas kernels, channelize(): pl.pallas_call(near_kernel, out_shape=out, grid_spec=pltpu.PrefetchScalar...  7.56 us
    all_to_all x1, waiting for transfers between devices, on_device(): lax.all_to_all(spectrum, 'crate', split_axis=0, concat_axis=0, tiled=True)  6.64 us
    pallas_call x1, Pallas kernels, on_device(): pl.pallas_call(plane_kernel, out_shape=jax.ShapeDtypeStruct((search_beams...  5.62 us
  transfers between devices with their start and end apart: 6, of which 5 were waited for; matrix products, arithmetic and copies ran while one was open for 5% of the time, Pallas kernels for 36%

profile of v2, /device:TPU:0, one launch (start us, length us, event | category | flops | bytes accessed | tf_op | source)
XLA Modules:
  0.0 137.1 jit_solution(7935524442058926126)
XLA Ops:
  0.6 0.0 copy-start
  0.7 11.1 %fold.1 = (bf16[8,16,64,128]{3,2,1,0:T(8,128)(2,1)}, bf16[4096,512]{1,0:T(8,128)(2,1)}) custom-call(s32[1]{0:T(128)} %bitcast.1.half_ref, bf16[128,17920]{1,0:T(8,128)(2,1)} %volt_ref.1, f32[4,512]{1,0:T(4,128)} %constant.62.clone.window_ref, bf16[512,512]{1,0:T(8,128)(2,1)} %constant.65.table_ref), custom_call_target="tpu_custom_call" | custom-call | flops 2147483648 | bytes 14680064 | tf_op jit(solution)/shard_map/fold/pallas_call | solution.py:297
  11.8 5.3 %all-to-all-start = ((bf16[8,16,64,128]{3,2,1,0:T(8,128)(2,1)}), bf16[8,16,64,128]{3,2,1,0:T(8,128)(2,1)}, u32[]{:S(2)}, u32[]{:S(2)}) async-start(bf16[8,16,64,128]{3,2,1,0:T(8,128)(2,1)} %get-tuple-element.17), calls=%async_computation | async-start | bytes 4194304 | tf_op jit(solution)/shard_map/all_to_all | solution.py:418
  17.1 0.0 copy-start.4
  17.1 0.0 copy-start.7
  17.1 0.0 copy-start.5
  17.1 7.6 %near.1 = bf16[8,16,64,128]{3,2,1,0:T(8,128)(2,1)} custom-call(s32[1]{0:T(128)} %bitcast.1.half_ref, bf16[4096,512]{1,0:T(8,128)(2,1)} %get-tuple-element.18.folded_ref, bf16[512,512]{1,0:T(8,128)(2,1)} %constant.65.table_ref), custom_call_target="tpu_custom_call" | custom-call | flops 1073741824 | bytes 8388608 | tf_op jit(solution)/shard_map/near/pallas_call | solution.py:317
  24.7 0.7 constant_dynamic-slice_fusion.1
  25.3 3.2 %collective-permute-start = (f32[16,2,1024]{2,1,0:T(2,128)S(1)}, f32[16,2,1024]{2,1,0:T(2,128)S(1)}, u32[]{:S(2)}, u32[]{:S(2)}) collective-permute-start(f32[16,2,1024]{2,1,0:T(2,128)S(1)} %get-tuple-element.33), channel_id=1, source_target_pairs={{0,8},{1,9},{2,10},{3,11},{4,12},{5,13},{6,14},{7,15},{8,0},{9,1},... | collective-permute-start | bytes 393224 | tf_op jit(solution)/shard_map/ppermute | solution.py:424
  28.5 0.4 copy.12
  28.9 0.6 broadcast_in_dim_tile.3.pick_ref
  29.6 2.8 %gather_fusion = f32[1024,3]{1,0:T(8,128)S(1)} fusion(f32[2048,3]{1,0:T(8,128)S(1)} %bitcast.7, s32[1024]{0:T(1024)S(1)} %fusion), kind=kCustom, calls=%fused_computation | custom fusion | bytes 28672 | tf_op jit(solution)/shard_map/jit(_take)/gather | solution.py:429
  32.4 1.0 broadcast_select_fusion.place_ref
  33.4 10.1 %collective-permute-done.gain_ref = f32[16,2,1024]{2,1,0:T(2,128)S(1)} collective-permute-done((f32[16,2,1024]{2,1,0:T(2,128)S(1)}, f32[16,2,1024]{2,1,0:T(2,128)S(1)}, u32[]{:S(2)}, u32[]{:S(2)}) %collective-permute-start) | collective-permute-done | bytes 131104 | tf_op jit(solution)/shard_map/ppermute | solution.py:424
  43.5 2.2 %all-to-all-done.x_ref = bf16[8,16,64,128]{3,2,1,0:T(8,128)(2,1)} async-done(((bf16[8,16,64,128]{3,2,1,0:T(8,128)(2,1)}), bf16[8,16,64,128]{3,2,1,0:T(8,128)(2,1)}, u32[]{:S(2)}, u32[]{:S(2)}) %all-to-all-start) | async-done | bytes 2097184 | tf_op jit(solution)/shard_map/all_to_all | solution.py:418
  45.7 5.7 %all-to-all-start.1 = ((bf16[8,16,64,128]{3,2,1,0:T(8,128)(2,1)}), bf16[8,16,64,128]{3,2,1,0:T(8,128)(2,1)S(1)}, u32[]{:S(2)}, u32[]{:S(2)}) async-start(bf16[8,16,64,128]{3,2,1,0:T(8,128)(2,1)} %near.1), calls=%async_computation.1 | async-start | bytes 4194304 | tf_op jit(solution)/shard_map/all_to_all | solution.py:418
  51.5 0.6 fusion.1
  52.1 10.2 %beams.5 = bf16[16,64,256]{2,1,0:T(8,128)(2,1)} custom-call(s32[1]{0:T(128)} %bitcast.3.first_ref, bf16[8,16,64,128]{3,2,1,0:T(8,128)(2,1)} %all-to-all-done.x_ref, f32[16,2,1024]{2,1,0:T(2,128)} %copy-done.8, f32[1024,3]{1,0:T(8,128)} %broadcast_select_fusion.place_ref, f32[3,256]{1,0:T(4,128)} %get-tuple-element.34.dir_ref), custom_call_target="tpu_custom_call" | custom-call | flops 8589934592 | bytes 6291456 | tf_op jit(solution)/shard_map/beams/pallas_call | solution.py:346
  62.3 0.2 collective-permute-start.2
  62.5 10.2 %beams.4 = bf16[16,64,256]{2,1,0:T(8,128)(2,1)} custom-call(s32[1]{0:T(128)} %bitcast.3.first_ref, bf16[8,16,64,128]{3,2,1,0:T(8,128)(2,1)} %all-to-all-done.x_ref, f32[16,2,1024]{2,1,0:T(2,128)} %copy-done.8, f32[1024,3]{1,0:T(8,128)} %broadcast_select_fusion.place_ref, f32[3,256]{1,0:T(4,128)} %get-tuple-element.35.dir_ref), custom_call_target="tpu_custom_call" | custom-call | flops 8589934592 | bytes 6291456 | tf_op jit(solution)/shard_map/beams/pallas_call | solution.py:346
  72.7 2.7 %collective-permute-start.1 = (bf16[16,64,256]{2,1,0:T(8,128)(2,1)}, bf16[16,64,256]{2,1,0:T(8,128)(2,1)}, u32[]{:S(2)}, u32[]{:S(2)}) collective-permute-start(bf16[16,64,256]{2,1,0:T(8,128)(2,1)} %beams.4), channel_id=1, source_target_pairs={{0,8},{1,9},{2,10},{3,11},{4,12},{5,13},{6,14},{7,15},{8,0},{9,1},... | collective-permute-start | bytes 1572872 | tf_op jit(solution)/shard_map/ppermute | solution.py:445
  75.4 12.2 %all-to-all-done.1.x_ref = bf16[8,16,64,128]{3,2,1,0:T(8,128)(2,1)S(1)} async-done(((bf16[8,16,64,128]{3,2,1,0:T(8,128)(2,1)}), bf16[8,16,64,128]{3,2,1,0:T(8,128)(2,1)S(1)}, u32[]{:S(2)}, u32[]{:S(2)}) %all-to-all-start.1) | async-done | bytes 2097184 | tf_op jit(solution)/shard_map/all_to_all | solution.py:418
  87.6 1.3 copy-done.1
  88.9 18.3 %beams.3.own_ref = f32[16,64,512]{2,1,0:T(8,128)} custom-call(s32[1]{0:T(128)} %bitcast.first_ref, bf16[8,16,64,128]{3,2,1,0:T(8,128)(2,1)} %copy-done.1, f32[16,2,1024]{2,1,0:T(2,128)} %get-tuple-element.23.gain_ref, f32[1024,3]{1,0:T(8,128)} %broadcast_select_fusion.place_ref, f32[3,512]{1,0:T(4,128)} %dir_ref.1), custom_call_target="tpu_custom_call" | custom-call | flops 17179869184 | bytes 6291456 | tf_op jit(solution)/shard_map/beams/pallas_call | solution.py:346
  107.2 4.4 %collective-permute-done.1.far0_ref = bf16[16,64,256]{2,1,0:T(8,128)(2,1)} collective-permute-done((bf16[16,64,256]{2,1,0:T(8,128)(2,1)}, bf16[16,64,256]{2,1,0:T(8,128)(2,1)}, u32[]{:S(2)}, u32[]{:S(2)}) %collective-permute-start.1) | collective-permute-done | bytes 524320 | tf_op jit(solution)/shard_map/ppermute | solution.py:445
  111.6 5.1 %power.1 = (f32[16,32,512]{2,1,0:T(8,128)}, bf16[16,16,512]{2,1,0:T(8,128)(2,1)}) custom-call(f32[16,64,512]{2,1,0:T(8,128)} %beams.3.own_ref, bf16[16,64,256]{2,1,0:T(8,128)(2,1)} %collective-permute-done.1.far0_ref, bf16[16,64,256]{2,1,0:T(8,128)(2,1)} %collective-permute-done.2.far1_ref, s32[1,128]{1,0:T(1,128)} %broadcast_in_dim_tile.3.pick_ref, ...), custom_call_target="tpu_custom_call" | custom-call | tf_op jit(solution)/shard_map/power/pallas_call | solution.py:385
  116.7 4.1 %all-to-all-start.2 = ((bf16[16,16,512]{2,1,0:T(8,128)(2,1)}), bf16[16,16,512]{2,1,0:T(8,128)(2,1)S(1)}, u32[]{:S(2)}, u32[]{:S(2)}) async-start(bf16[16,16,512]{2,1,0:T(8,128)(2,1)} %get-tuple-element.29), calls=%async_computation.2 | async-start | bytes 524288 | tf_op jit(solution)/shard_map/all_to_all | solution.py:449
  120.8 0.6 constant_dynamic-slice_fusion.delay_ref
  121.4 2.7 %turns.1 = (bf16[1024,512]{1,0:T(8,128)(2,1)}, bf16[1024,512]{1,0:T(8,128)(2,1)}) custom-call(s32[64,256]{1,0:T(8,128)} %constant_dynamic-slice_fusion.delay_ref), custom_call_target="tpu_custom_call" | custom-call | tf_op jit(solution)/shard_map/turns/pallas_call | solution.py:454
  124.2 6.6 %all-to-all-done.2 = bf16[16,16,512]{2,1,0:T(8,128)(2,1)S(1)} async-done(((bf16[16,16,512]{2,1,0:T(8,128)(2,1)}), bf16[16,16,512]{2,1,0:T(8,128)(2,1)S(1)}, u32[]{:S(2)}, u32[]{:S(2)}) %all-to-all-start.2) | async-done | bytes 262176 | tf_op jit(solution)/shard_map/all_to_all | solution.py:449
  130.8 0.7 copy-done.2
  131.5 5.6 %plane.1 = f32[16,32,64]{2,1,0:T(8,128)} custom-call(bf16[256,512]{1,0:T(8,128)(2,1)} %bitcast.8, bf16[1024,512]{1,0:T(8,128)(2,1)} %get-tuple-element.30.high_ref, bf16[1024,512]{1,0:T(8,128)(2,1)} %get-tuple-element.31.low_ref), custom_call_target="tpu_custom_call" | custom-call | tf_op jit(solution)/shard_map/plane/pallas_call | solution.py:457
  (16 shorter events, 0.0 us)
Async XLA Ops:
  0.6 120.2 %copy-start = (s32[1024,256]{1,0:T(8,128)S(1)}, s32[1024,256]{1,0:T(8,128)}, u32[]{:S(2)}) copy-start(s32[1024,256]{1,0:T(8,128)} %param.15) | copy-start | bytes 3145732
  11.8 34.0 %all-to-all-start = ((bf16[8,16,64,128]{3,2,1,0:T(8,128)(2,1)}), bf16[8,16,64,128]{3,2,1,0:T(8,128)(2,1)}, u32[]{:S(2)}, u32[]{:S(2)}) async-start(bf16[8,16,64,128]{3,2,1,0:T(8,128)(2,1)} %get-tuple-element.17), calls=%async_computation | async-start | bytes 4194304 | tf_op jit(solution)/shard_map/all_to_all | solution.py:418
  17.1 7.6 %copy-start.3 = (f32[16,2,2048]{2,1,0:T(2,128)S(1)}, f32[16,2,2048]{2,1,0:T(2,128)}, u32[]{:S(2)}) copy-start(f32[16,2,2048]{2,1,0:T(2,128)} %param.11) | copy-start | bytes 786436
  17.1 11.4 %copy-start.4 = (f32[3,2048]{1,0:T(4,128)S(1)}, f32[3,2048]{1,0:T(4,128)}, u32[]{:S(2)}) copy-start(f32[3,2048]{1,0:T(4,128)} %param.12) | copy-start | bytes 73732
  17.1 11.8 %copy-start.7 = (s32[16]{0:T(128)S(1)}, s32[16]{0:T(128)}, u32[]{:S(2)}) copy-start(s32[16]{0:T(128)} %param.16) | copy-start | bytes 196
  17.1 12.4 %copy-start.5 = (s32[2048]{0:T(1024)S(1)}, s32[2048]{0:T(1024)}, u32[]{:S(2)}) copy-start(s32[2048]{0:T(1024)} %param.14) | copy-start | bytes 24580
  25.3 18.2 %collective-permute-start = (f32[16,2,1024]{2,1,0:T(2,128)S(1)}, f32[16,2,1024]{2,1,0:T(2,128)S(1)}, u32[]{:S(2)}, u32[]{:S(2)}) collective-permute-start(f32[16,2,1024]{2,1,0:T(2,128)S(1)} %get-tuple-element.33), channel_id=1, source_target_pairs={{0,8},{1,9},{2,10},{3,11},{4,12},{5,13},{6,14},{7,15},{8,0},{9,1},... | collective-permute-start | bytes 393224 | tf_op jit(solution)/shard_map/ppermute | solution.py:424
  43.5 2.2 %copy-start.8 = (f32[16,2,1024]{2,1,0:T(2,128)}, f32[16,2,1024]{2,1,0:T(2,128)S(1)}, u32[]{:S(2)}) copy-start(f32[16,2,1024]{2,1,0:T(2,128)S(1)} %collective-permute-done.gain_ref) | copy-start | bytes 393220
  45.7 5.7 %copy-start.6 = (f32[3,512]{1,0:T(4,128)S(1)}, f32[3,512]{1,0:T(4,128)}, u32[]{:S(2)}) copy-start(f32[3,512]{1,0:T(4,128)} %dir_ref.1) | copy-start | bytes 18436
  45.7 41.8 %all-to-all-start.1 = ((bf16[8,16,64,128]{3,2,1,0:T(8,128)(2,1)}), bf16[8,16,64,128]{3,2,1,0:T(8,128)(2,1)S(1)}, u32[]{:S(2)}, u32[]{:S(2)}) async-start(bf16[8,16,64,128]{3,2,1,0:T(8,128)(2,1)} %near.1), calls=%async_computation.1 | async-start | bytes 4194304 | tf_op jit(solution)/shard_map/all_to_all | solution.py:418
  62.3 44.9 %collective-permute-start.2 = (bf16[16,64,256]{2,1,0:T(8,128)(2,1)}, bf16[16,64,256]{2,1,0:T(8,128)(2,1)}, u32[]{:S(2)}, u32[]{:S(2)}) collective-permute-start(bf16[16,64,256]{2,1,0:T(8,128)(2,1)} %beams.5), channel_id=1, source_target_pairs={{0,8},{1,9},{2,10},{3,11},{4,12},{5,13},{6,14},{7,15},{8,0},{9,1},... | collective-permute-start | bytes 1572872 | tf_op jit(solution)/shard_map/ppermute | solution.py:445
  72.7 38.9 %collective-permute-start.1 = (bf16[16,64,256]{2,1,0:T(8,128)(2,1)}, bf16[16,64,256]{2,1,0:T(8,128)(2,1)}, u32[]{:S(2)}, u32[]{:S(2)}) collective-permute-start(bf16[16,64,256]{2,1,0:T(8,128)(2,1)} %beams.4), channel_id=1, source_target_pairs={{0,8},{1,9},{2,10},{3,11},{4,12},{5,13},{6,14},{7,15},{8,0},{9,1},... | collective-permute-start | bytes 1572872 | tf_op jit(solution)/shard_map/ppermute | solution.py:445
  87.6 1.3 copy-start.1
  116.7 14.1 %all-to-all-start.2 = ((bf16[16,16,512]{2,1,0:T(8,128)(2,1)}), bf16[16,16,512]{2,1,0:T(8,128)(2,1)S(1)}, u32[]{:S(2)}, u32[]{:S(2)}) async-start(bf16[16,16,512]{2,1,0:T(8,128)(2,1)} %get-tuple-element.29), calls=%async_computation.2 | async-start | bytes 524288 | tf_op jit(solution)/shard_map/all_to_all | solution.py:449
  130.8 0.7 copy-start.2

commit v3 on v2

--- a/solution.py
+++ b/solution.py
@@ -12,6 +12,8 @@
 CH = 256
 TAPS = 4
 TIME = 32
+PITCH = 40
+PARTS = 2
 FFTLEN = 512
 HALF_BINS = TIME // 2
 TWO_PI = 2.0 * math.pi
@@ -46,9 +48,10 @@
     return (np.sinc(offsets) * tapering).reshape(TAPS, FFTLEN).astype(np.float32)
 
 
-def dft_table():
-    turns = np.arange(CH)[:, None] * np.arange(FFTLEN)[None, :] % FFTLEN
-    angles = TWO_PI * turns / FFTLEN
+def dft_table(halves, dests, chans):
+    ids = np.arange(CH).reshape(halves, dests, PARTS, chans // PARTS)
+    ids = ids.transpose(0, 2, 1, 3).reshape(CH)
+    angles = TWO_PI * (ids[:, None] * np.arange(FFTLEN)[None, :] % FFTLEN) / FFTLEN
     stacked = np.stack([np.cos(angles), -np.sin(angles)], axis=1) / math.sqrt(FFTLEN)
     return stacked.reshape(2 * CH, FFTLEN).astype(np.float32)
 
@@ -79,8 +82,8 @@
     return high, (x - high.astype(F32)).astype(BF16)
 
 
-def transform_rows(table, folded_ref, spread_ref, out_ref):
-    inputs = out_ref.shape[-1]
+def transform_rows(table, folded_ref, spread_ref, out_ref, first_chan, chans):
+    dests, inputs = out_ref.shape[0], out_ref.shape[-1]
     rows = table.shape[0]
     group = 2 if inputs % 128 == 0 else 1
 
@@ -90,20 +93,20 @@
         out = lax.dot_general(table, frames, NT, preferred_element_type=F32)
         for part in range(group):
             piece = out[:, part * inputs : (part + 1) * inputs]
-            spread_ref[pl.ds(index * group + part, rows, stride=TIME), :] = piece
+            spread_ref[pl.ds(index * group + part, rows, stride=PITCH), :] = piece
         return carry
 
-    lax.fori_loop(0, TIME // group, step, 0, unroll=4)
-    dests, chans = out_ref.shape[:2]
-    per_chan = 2 * TIME
+    lax.fori_loop(0, TIME // group, step, 0, unroll=8)
 
     def pack(dest, carry):
         for chan in range(chans):
-            start = pl.multiple_of((dest * chans + chan) * per_chan, per_chan)
-            out_ref[dest, chan] = spread_ref[pl.ds(start, per_chan), :].astype(BF16)
+            for part in range(2):
+                start = pl.multiple_of(((dest * chans + chan) * 2 + part) * PITCH, 8)
+                block = spread_ref[pl.ds(start, TIME), :].astype(BF16)
+                out_ref[dest, first_chan + chan, part * TIME : (part + 1) * TIME] = block
         return carry
 
-    lax.fori_loop(0, dests, pack, 0, unroll=2)
+    lax.fori_loop(0, dests, pack, 0, unroll=4)
 
 
 def fold_kernel(half_ref, volt_ref, window_ref, table_ref, out_ref, folded_ref, spread_ref):
@@ -128,46 +131,66 @@
 
     @pl.when(step == pl.num_programs(0) - 1)
     def _():
-        transform_rows(table_ref[...], folded_ref, spread_ref, out_ref)
-
-
-def near_kernel(half_ref, folded_ref, table_ref, out_ref, spread_ref):
-    transform_rows(table_ref[...], folded_ref, spread_ref, out_ref)
-
-
-def beam_kernel(
-    first_ref, x_ref, gain_ref, place_ref, dir_ref, out_ref, even_ref, odd_ref, sum_ref
-):
+        transform_rows(table_ref[...], folded_ref, spread_ref, out_ref, 0, out_ref.shape[1])
+
+
+def spectra_kernel(base_ref, folded_ref, table_ref, out_ref, spread_ref):
+    chans = out_ref.shape[1] // table_ref.shape[0]
+    for part in range(table_ref.shape[0]):
+        table = table_ref[part]
+        transform_rows(table, folded_ref, spread_ref, out_ref, part * chans, chans)
+
+
+def beam_kernel(mode, first_ref, x_ref, gain_ref, *refs):
+    if mode == "start":
+        place_ref, dir_ref, out_ref, dc_ref, ds_ref, c_ref, s_ref = refs[:-3]
+    elif mode == "more":
+        dc_ref, ds_ref, c_ref, s_ref, out_ref = refs[:-3]
+    else:
+        place_ref, dir_ref, dc_ref, ds_ref, out_ref = refs[:-3]
+    even_ref, odd_ref, sum_ref = refs[-3:]
     step = pl.program_id(0)
     tiles = pl.num_programs(0) - 1
     chans, _, beams = out_ref.shape
-    depth = place_ref.shape[0]
+    depth = dc_ref.shape[0]
     wide = 256
     chunk = depth // chans
 
     def generate(part, weight_ref):
         for sub in range(0, chunk, 16):
             row = pl.multiple_of(part * chunk + sub, 16)
-            place = place_ref[pl.ds(row, 16), :]
+            rows = pl.ds(row, 16)
             for lane in range(0, beams, wide):
                 lanes = slice(lane, lane + wide)
-                direction = dir_ref[:, lanes]
-                geometry = place[:, 0:1] * direction[0:1, :]
-                geometry = geometry + place[:, 1:2] * direction[1:2, :]
-                geometry = geometry + place[:, 2:3] * direction[2:3, :]
-                first = 1.0 + first_ref[0].astype(F32) * (1.0 / CH)
-                c, s = cos_sin_turns(geometry * first)
-                dc, ds = cos_sin_turns(geometry * (1.0 / CH))
+                if mode != "more":
+                    place = place_ref[rows, :]
+                    direction = dir_ref[:, lanes]
+                    geometry = place[:, 0:1] * direction[0:1, :]
+                    geometry = geometry + place[:, 1:2] * direction[1:2, :]
+                    geometry = geometry + place[:, 2:3] * direction[2:3, :]
+                    first = 1.0 + first_ref[0].astype(F32) * (1.0 / CH)
+                    c, s = cos_sin_turns(geometry * first)
+                else:
+                    c, s = c_ref[rows, lanes], s_ref[rows, lanes]
+                if mode == "start":
+                    dc, ds = cos_sin_turns(geometry * (1.0 / CH))
+                    dc_ref[rows, lanes] = dc
+                    ds_ref[rows, lanes] = ds
+                else:
+                    dc, ds = dc_ref[rows, lanes], ds_ref[rows, lanes]
                 next_c, next_s = c * dc - s * ds, c * ds + s * dc
                 twice = dc + dc
                 for chan in range(chans):
-                    weight_ref[chan, pl.ds(row, 16), lanes] = c.astype(BF16)
+                    weight_ref[chan, rows, lanes] = c.astype(BF16)
                     weight_ref[chan, pl.ds(depth + row, 16), lanes] = s.astype(BF16)
-                    if chan + 2 < chans:
+                    if chan + 2 < chans + (mode == "start"):
                         c, next_c = next_c, twice * next_c - c
                         s, next_s = next_s, twice * next_s - s
                     else:
                         c, s = next_c, next_s
+                if mode == "start":
+                    c_ref[rows, lanes] = c
+                    s_ref[rows, lanes] = s
 
     def accumulate(chan, weight_ref):
         blocks = x_ref.shape[0]
@@ -189,12 +212,13 @@
         out_ref[m] = (sum_ref[m] + accumulate(m, weights[0])).astype(out_ref.dtype)
 
     def over_channels(body, weights):
-        lax.fori_loop(0, chans, lambda m, v: (body(m, weights), v)[1], 0, unroll=min(8, chans))
+        unroll = min(4, chans)
+        lax.fori_loop(0, chans, lambda m, v: (body(m, weights), v)[1], 0, unroll=unroll)
 
     @pl.when(step == 0)
     def _():
         sum_ref[...] = jnp.zeros_like(sum_ref)
-        over_channels(lambda m, w: generate(m, w), even_ref)
+        over_channels(generate, even_ref)
 
     for parity, weights in ((1, (even_ref, odd_ref)), (0, (odd_ref, even_ref))):
 
@@ -214,8 +238,9 @@
     block, _, beams = own_ref.shape
     search = chosen_ref.shape[1] // TIME
     per = 128 // search
-    far = jnp.concatenate([far0_ref[...], far1_ref[...]], axis=2)
-    total = own_ref[...] + far.astype(F32)
+    early = step < pl.num_programs(0) // PARTS
+    far = jnp.where(early, far0_ref[...].astype(F32), far1_ref[...].astype(F32))
+    total = own_ref[...] + far
     real, imag = total[:, :TIME], total[:, TIME:]
     power = (real * real + imag * imag) * (1.0 / 2048)
     power_ref[...] = power
@@ -261,7 +286,7 @@
 
 def plane_kernel(spec_ref, high_ref, low_ref, out_ref):
     chans, width = spec_ref.shape
-    search, _, trials = out_ref.shape
+    _, _, trials = out_ref.shape
     spec = spec_ref[...].astype(F32)
     lane = lax.broadcasted_iota(jnp.int32, (chans, width), 1)
     is_real = lane % TIME < HALF_BINS
@@ -282,58 +307,69 @@
 PARAMS = pltpu.CompilerParams(vmem_limit_bytes=60 << 20)
 
 
-def channelize(voltages, half_id, halves, chans):
+def channel_table(halves, dests, chans):
+    table = dft_table(halves, dests, chans).reshape(halves * PARTS, -1, FFTLEN)
+    return jnp.asarray(table).astype(BF16)
+
+
+def fold(voltages, table, block_id, dests, chans):
     inputs, samples = voltages.shape
-    rows = 2 * CH // halves
-    dests = rows // 2 // chans
+    rows = table.shape[1]
     window = jnp.asarray(pfb_window())
-    table = jnp.asarray(dft_table()).astype(BF16)
     block = min(32, inputs)
-    out = jax.ShapeDtypeStruct((dests, chans, 2 * TIME, inputs), BF16)
+    spectra = jax.ShapeDtypeStruct((dests, chans, 2 * TIME, inputs), BF16)
     folded = jax.ShapeDtypeStruct((TIME * inputs, FFTLEN), BF16)
-    spread = pltpu.VMEM((rows * TIME, inputs), F32)
-    whole4 = pl.BlockSpec(out.shape, lambda i, h: (0, 0, 0, 0))
-    whole2 = pl.BlockSpec(folded.shape, lambda i, h: (0, 0))
-    far, folded = pl.pallas_call(
+    whole = lambda x: pl.BlockSpec(x.shape, lambda i, k: (0,) * len(x.shape))
+    return pl.pallas_call(
         fold_kernel,
-        out_shape=(out, folded),
+        out_shape=(spectra, folded),
         grid_spec=pltpu.PrefetchScalarGridSpec(
             num_scalar_prefetch=1,
             grid=(inputs // block,),
             in_specs=[
-                pl.BlockSpec((block, samples), lambda i, h: (i, 0)),
-                pl.BlockSpec(window.shape, lambda i, h: (0, 0)),
-                pl.BlockSpec((rows, FFTLEN), lambda i, h: (halves - 1 - h[0], 0)),
+                pl.BlockSpec((block, samples), lambda i, k: (i, 0)),
+                whole(window),
+                pl.BlockSpec((None, rows, FFTLEN), lambda i, k: (k[0], 0, 0)),
             ],
-            out_specs=(whole4, whole2),
-            scratch_shapes=[spread],
+            out_specs=(whole(spectra), whole(folded)),
+            scratch_shapes=[pltpu.VMEM((rows * PITCH, inputs), F32)],
         ),
         compiler_params=PARAMS,
         cost_estimate=pl.CostEstimate(
-            flops=4 * rows * FFTLEN * TIME * inputs, bytes_accessed=14 << 20, transcendentals=0
+            flops=8 * rows * FFTLEN * TIME * inputs, bytes_accessed=12 << 20, transcendentals=0
         ),
         name="fold",
-    )(half_id, voltages, window, table)
-    near = pl.pallas_call(
-        near_kernel,
+    )(block_id, voltages, window, table)
+
+
+def more_spectra(folded, table, block_id, blocks, dests, chans):
+    rows = table.shape[1]
+    inputs = folded.shape[0] // TIME
+    out = jax.ShapeDtypeStruct((dests, chans * blocks, 2 * TIME, inputs), BF16)
+    return pl.pallas_call(
+        spectra_kernel,
         out_shape=out,
         grid_spec=pltpu.PrefetchScalarGridSpec(
             num_scalar_prefetch=1,
             grid=(1,),
-            in_specs=[whole2, pl.BlockSpec((rows, FFTLEN), lambda i, h: (h[0], 0))],
-            out_specs=whole4,
-            scratch_shapes=[spread],
+            in_specs=[
+                pl.BlockSpec(folded.shape, lambda i, k: (0, 0)),
+                pl.BlockSpec((blocks, rows, FFTLEN), lambda i, k: (k[0], 0, 0)),
+            ],
+            out_specs=pl.BlockSpec(out.shape, lambda i, k: (0, 0, 0, 0)),
+            scratch_shapes=[pltpu.VMEM((rows * PITCH, inputs), F32)],
         ),
         compiler_params=PARAMS,
         cost_estimate=pl.CostEstimate(
-            flops=2 * rows * FFTLEN * TIME * inputs, bytes_accessed=8 << 20, transcendentals=0
-        ),
-        name="near",
-    )(half_id, folded, table)
-    return far, near
-
-
-def form_beams(x, gains, places, directions, first, out_type):
+            flops=2 * blocks * rows * FFTLEN * TIME * inputs,
+            bytes_accessed=6 << 20,
+            transcendentals=0,
+        ),
+        name="spectra",
+    )(block_id, folded, table)
+
+
+def form_beams(mode, x, gains, part, first, places, directions, state, out_type):
     sources, chans, rows, inputs = x.shape
     beams = directions.shape[1]
     total = sources * inputs
@@ -343,21 +379,33 @@
     depth = 256
     blocks = depth // 128
     tiles = total // depth
+    late = lambda i: jnp.maximum(i - 1, 0)
+    now = lambda i: jnp.minimum(i, tiles - 1)
+    state_spec = pl.BlockSpec((depth, beams), lambda i, f: (now(i), 0))
+    in_specs = [
+        pl.BlockSpec((blocks, chans, rows, 128), lambda i, f: (late(i), 0, 0, 0)),
+        pl.BlockSpec((chans, 2, depth), lambda i, f: (part, 0, late(i))),
+    ]
+    operands = [x, gains]
+    if mode != "more":
+        in_specs.append(pl.BlockSpec((depth, 3), lambda i, f: (now(i), 0)))
+        in_specs.append(pl.BlockSpec(directions.shape, lambda i, f: (0, 0)))
+        operands += [places, directions]
+    in_specs += [state_spec] * len(state)
+    operands += state
+    out_shape = [jax.ShapeDtypeStruct((chans, rows, beams), out_type)]
+    out_specs = [pl.BlockSpec((chans, rows, beams), lambda i, f: (0, 0, 0))]
+    if mode == "start":
+        out_shape += [jax.ShapeDtypeStruct((total, beams), F32)] * 4
+        out_specs += [state_spec] * 4
     return pl.pallas_call(
-        beam_kernel,
-        out_shape=jax.ShapeDtypeStruct((chans, rows, beams), out_type),
+        functools.partial(beam_kernel, mode),
+        out_shape=out_shape,
         grid_spec=pltpu.PrefetchScalarGridSpec(
             num_scalar_prefetch=1,
             grid=(tiles + 1,),
-            in_specs=[
-                pl.BlockSpec(
-                    (blocks, chans, rows, 128), lambda i, f: (jnp.maximum(i - 1, 0), 0, 0, 0)
-                ),
-                pl.BlockSpec((chans, 2, depth), lambda i, f: (0, 0, jnp.maximum(i - 1, 0))),
-                pl.BlockSpec((depth, 3), lambda i, f: (jnp.minimum(i, tiles - 1), 0)),
-                pl.BlockSpec(directions.shape, lambda i, f: (0, 0)),
-            ],
-            out_specs=pl.BlockSpec((chans, rows, beams), lambda i, f: (0, 0, 0)),
+            in_specs=in_specs,
+            out_specs=out_specs,
             scratch_shapes=[
                 pltpu.VMEM((chans, 2 * depth, beams), BF16),
                 pltpu.VMEM((chans, 2 * depth, beams), BF16),
@@ -366,10 +414,9 @@
         ),
         compiler_params=PARAMS,
         cost_estimate=pl.CostEstimate(
-            flops=32 * chans * rows * total * beams, bytes_accessed=6 << 20, transcendentals=0
-        ),
-        name="beams",
-    )(first, x, gains, places, directions)
+            flops=16 * chans * rows * total * beams, bytes_accessed=12 << 20, transcendentals=0
+        ),
+    )(first, *operands)
 
 
 def powers(own, far, pick, search, copies):
@@ -378,9 +425,13 @@
     table = time_table(search)
     high = jnp.asarray(table).astype(BF16)
     low = (jnp.asarray(table) - high.astype(F32)).astype(BF16)
-    block = min(4, chans)
+    block = min(4, chans // PARTS)
     cube = pl.BlockSpec((block, rows, beams), lambda i: (i, 0, 0))
-    far_cubes = [pl.BlockSpec((block, rows, x.shape[2]), lambda i: (i, 0, 0)) for x in far]
+    half = chans // block // PARTS
+    far_cubes = [
+        pl.BlockSpec((block, rows, beams), lambda i: (jnp.minimum(i, half - 1), 0, 0)),
+        pl.BlockSpec((block, rows, beams), lambda i: (jnp.maximum(i - half, 0), 0, 0)),
+    ]
     flat = lambda shape: pl.BlockSpec(shape, lambda i: (0,) * len(shape))
     return pl.pallas_call(
         power_kernel,
@@ -412,15 +463,19 @@
     inputs = gains.shape[2] // halves
     own_inputs = half_id * inputs
     half_scalar = half_id.astype(jnp.int32).reshape(1)
-    far, near = channelize(voltages, half_scalar, halves, chans)
+    some = chans // PARTS
+    table = channel_table(halves, per_half, chans)
+    far_block = (1 - half_scalar) * PARTS
+    far0, folded = fold(voltages, table, far_block, per_half, some)
 
     def exchange(x):
         return lax.all_to_all(
             x, "crate", split_axis=0, concat_axis=0, axis_index_groups=members, tiled=True
         )
 
-    far = exchange(far)
-    near, gains, positions = lax.optimization_barrier((near, gains, positions))
+    far0 = exchange(far0)
+    far1 = more_spectra(folded, table, far_block + 1, 1, per_half, some)
+    far1, gains, positions = lax.optimization_barrier((far1, gains, positions))
     far_gains = lax.ppermute(
         lax.dynamic_slice_in_dim(gains, inputs - own_inputs, inputs, 2), "crate", partners
     )
@@ -431,21 +486,26 @@
     pick = jnp.tile(search_beams, 128 // search)[None, :]
     own_first = (position * chans).astype(jnp.int32).reshape(1)
     far_first = ((position + per_half) % devices * chans).astype(jnp.int32).reshape(1)
-    far, near, far_gains, near_gains, places, pick = lax.optimization_barrier(
-        (far, near, far_gains, near_gains, places, pick)
+    far0, far1, far_gains, near_gains, places, pick = lax.optimization_barrier(
+        (far0, far1, far_gains, near_gains, places, pick)
     )
+    far1 = exchange(far1)
+    beams = functools.partial(form_beams, places=places, directions=directions)
+    sums0, dc, ds, c, s = beams(
+        "start", far0, far_gains, 0, far_first, state=[], out_type=BF16
+    )
+    sums0, folded = lax.optimization_barrier((sums0, folded))
+    sums0 = lax.ppermute(sums0, "crate", partners)
+    near = more_spectra(folded, table, half_scalar, PARTS, per_half, some)
+    far1, near = lax.optimization_barrier((far1, near))
     near = exchange(near)
-
-    beams = directions.shape[1]
-    cut = beams // 2
-    far_sums = []
-    for start in range(0, beams, cut):
-        some = lax.slice_in_dim(directions, start, start + cut, axis=1)
-        part = form_beams(far, far_gains, places, some, far_first, BF16)
-        far_sums.append(lax.ppermute(part, "crate", partners))
-    near_sums = form_beams(near, near_gains, places, directions, own_first, F32)
-
-    beam_power, spectrum = powers(near_sums, far_sums, pick, search, devices)
+    (sums1,) = beams(
+        "more", far1, far_gains, 1, far_first, state=[dc, ds, c, s], out_type=BF16
+    )
+    sums1 = lax.ppermute(sums1, "crate", partners)
+    (near_sums,) = beams("step", near, near_gains, 0, own_first, state=[dc, ds], out_type=F32)
+
+    beam_power, spectrum = powers(near_sums, [sums0, sums1], pick, search, devices)
     spectrum = lax.all_to_all(spectrum, "crate", split_axis=0, concat_axis=0, tiled=True)
     width = spectrum.shape[-1]
     trials = delays.shape[0] // devices

time: 138 us -> 154 us (1.12)
  waiting for transfers between devices: 35.6 us -> 44.9 us
  Pallas kernels: 70.8 us -> 74.3 us
  starting transfers between devices: 21.2 us -> 24 us
    all_to_all x2 -> x3, waiting for transfers between devices: 14.4 us -> 36.8 us  [exchange(): lax.all_to_all(x, 'crate', split_axis=0, concat_axis=0, axis_index_groups...]
    ppermute x1, waiting for transfers between devices: 10.1 us -> 1.5 us  [on_device(): lax.ppermute(lax.dynamic_slice_in_dim(gains, inputs - own_inputs, inputs,...]
    ppermute x2, waiting for transfers between devices: 4.42 us -> 0.01 us  [the longest x1 0.01 us: on_device(): sums0 = lax.ppermute(sums0, 'crate', partners)]
    all_to_all x2 -> x3, starting transfers between devices: 11 us -> 14.5 us  [exchange(): lax.all_to_all(x, 'crate', split_axis=0, concat_axis=0, axis_index_groups...]
    pallas_call x5 -> x6, Pallas kernels: 57.4 us -> 60.7 us  [the longest x3 40 us: form_beams(): pl.pallas_call(functools.partial(beam_kernel, mode), out_shape=out_shape,...]
  transfers between devices with their start and end apart: 6 -> 7, of which waited for: 5 -> 4; matrix products, arithmetic and copies ran while one was open for 5% -> 4% of each run, Pallas kernels for 36% -> 36%
where the time goes in v3:
time: 154 us; the launch traced here: 153 us
  Pallas kernels  74.3 us (48%)
  waiting for transfers between devices  44.9 us (29%)
  starting transfers between devices  24 us (16%)
  local copies, waits for them, and re-layouts  8.17 us (5%)
    pallas_call x3, Pallas kernels, form_beams(): pl.pallas_call(functools.partial(beam_kernel, mode), out_shape=out_shape,...  40 us
    all_to_all x3, waiting for transfers between devices, exchange(): lax.all_to_all(x, 'crate', split_axis=0, concat_axis=0, axis_index_groups...  36.8 us
    all_to_all x3, starting transfers between devices, exchange(): lax.all_to_all(x, 'crate', split_axis=0, concat_axis=0, axis_index_groups...  14.5 us
    pallas_call x2, Pallas kernels, more_spectra(): pl.pallas_call(spectra_kernel, out_shape=out, grid_spec=pltpu.PrefetchSca...  12.1 us
    pallas_call x1, Pallas kernels, fold(): pl.pallas_call(fold_kernel, out_shape=(spectra, folded), grid_spec=pltpu....  8.6 us
    all_to_all x1, waiting for transfers between devices, on_device(): lax.all_to_all(spectrum, 'crate', split_axis=0, concat_axis=0, tiled=True)  6.58 us
    pallas_call x1, Pallas kernels, on_device(): pl.pallas_call(plane_kernel, out_shape=jax.ShapeDtypeStruct((search_beams...  5.62 us
    pallas_call x1, Pallas kernels, powers(): pl.pallas_call(power_kernel, out_shape=(jax.ShapeDtypeStruct((chans, TIME...  5.3 us
  transfers between devices with their start and end apart: 7, of which 4 were waited for; matrix products, arithmetic and copies ran while one was open for 4% of the time, Pallas kernels for 36%

profile of v3, /device:TPU:0, one launch (start us, length us, event | category | flops | bytes accessed | tf_op | source)
XLA Modules:
  0.0 153.2 jit_solution(13920095135065240388)
XLA Ops:
  0.6 0.0 copy-start
  0.7 8.6 %fold.1 = (bf16[8,8,64,128]{3,2,1,0:T(8,128)(2,1)}, bf16[4096,512]{1,0:T(8,128)(2,1)}) custom-call(s32[1]{0:T(128)S(6)} %mul.16.half_ref, bf16[128,17920]{1,0:T(8,128)(2,1)} %volt_ref.1, f32[4,512]{1,0:T(4,128)} %constant.67.clone.window_ref, bf16[4,128,512]{2,1,0:T(8,128)(2,1)} %constant.69.table_ref), custom_call_target="tpu_custom_call" | custom-call | flops 2147483648 | bytes 12582912 | tf_op jit(solution)/shard_map/fold/pallas_call | solution.py:323
  9.3 5.3 %all-to-all-start = ((bf16[8,8,64,128]{3,2,1,0:T(8,128)(2,1)}), bf16[8,8,64,128]{3,2,1,0:T(8,128)(2,1)}, u32[]{:S(2)}, u32[]{:S(2)}) async-start(bf16[8,8,64,128]{3,2,1,0:T(8,128)(2,1)} %get-tuple-element.26), calls=%async_computation | async-start | bytes 2097152 | tf_op jit(solution)/shard_map/all_to_all | solution.py:472
  14.5 0.0 copy-start.5
  14.5 0.0 copy-start.7
  14.6 5.0 %spectra.2 = bf16[8,8,64,128]{3,2,1,0:T(8,128)(2,1)} custom-call(s32[1]{0:T(128)S(6)} %add.30.base_ref, bf16[4096,512]{1,0:T(8,128)(2,1)} %get-tuple-element.36.folded_ref, bf16[4,128,512]{2,1,0:T(8,128)(2,1)} %constant.69.table_ref), custom_call_target="tpu_custom_call" | custom-call | flops 536870912 | bytes 6291456 | tf_op jit(solution)/shard_map/spectra/pallas_call | solution.py:349
  19.6 0.7 constant_dynamic-slice_fusion.1
  20.2 3.1 %collective-permute-start = (f32[16,2,1024]{2,1,0:T(2,128)S(1)}, f32[16,2,1024]{2,1,0:T(2,128)S(1)}, u32[]{:S(2)}, u32[]{:S(2)}) collective-permute-start(f32[16,2,1024]{2,1,0:T(2,128)S(1)} %get-tuple-element.51), channel_id=1, source_target_pairs={{0,8},{1,9},{2,10},{3,11},{4,12},{5,13},{6,14},{7,15},{8,0},{9,1},... | collective-permute-start | bytes 393224 | tf_op jit(solution)/shard_map/ppermute | solution.py:479
  23.3 0.4 copy.12
  23.7 0.7 broadcast_in_dim_tile.3.pick_ref
  24.4 2.8 %gather_fusion = f32[1024,3]{1,0:T(8,128)S(1)} fusion(f32[2048,3]{1,0:T(8,128)S(1)} %bitcast.7, s32[1024]{0:T(1024)S(1)} %fusion), kind=kCustom, calls=%fused_computation | custom fusion | bytes 28672 | tf_op jit(solution)/shard_map/jit(_take)/gather | solution.py:484
  27.2 1.0 broadcast_select_fusion.refs_0_
  28.2 1.5 collective-permute-done.gain_ref
  29.7 2.2 %all-to-all-done.x_ref = bf16[8,8,64,128]{3,2,1,0:T(8,128)(2,1)} async-done(((bf16[8,8,64,128]{3,2,1,0:T(8,128)(2,1)}), bf16[8,8,64,128]{3,2,1,0:T(8,128)(2,1)}, u32[]{:S(2)}, u32[]{:S(2)}) %all-to-all-start) | async-done | bytes 1048608 | tf_op jit(solution)/shard_map/all_to_all | solution.py:472
  31.9 5.0 %all-to-all-start.1 = ((bf16[8,8,64,128]{3,2,1,0:T(8,128)(2,1)}), bf16[8,8,64,128]{3,2,1,0:T(8,128)(2,1)S(1)}, u32[]{:S(2)}, u32[]{:S(2)}) async-start(bf16[8,8,64,128]{3,2,1,0:T(8,128)(2,1)} %spectra.2), calls=%async_computation.1 | async-start | bytes 2097152 | tf_op jit(solution)/shard_map/all_to_all | solution.py:472
  37.0 13.3 %shard_map.113 = (bf16[8,64,512]{2,1,0:T(8,128)(2,1)}, f32[1024,512]{1,0:T(8,128)}, f32[1024,512]{1,0:T(8,128)}, f32[1024,512]{1,0:T(8,128)}, f32[1024,512]{1,0:T(8,128)}) custom-call(s32[1]{0:T(128)} %bitcast.3.first_ref, bf16[8,8,64,128]{3,2,1,0:T(8,128)(2,1)} %all-to-all-done.x_ref, f32[16,2,1024]{2,1,0:T(2,128)} %copy-done.8, ...), custom_call_target="tpu_custom_call" | custom-call | flops 4294967296 | bytes 12582912 | tf_op jit(solution)/shard_map/pallas_call | solution.py:401
  50.2 7.1 %spectra.3 = bf16[8,16,64,128]{3,2,1,0:T(8,128)(2,1)} custom-call(s32[1]{0:T(128)} %bitcast.1.base_ref, bf16[4096,512]{1,0:T(8,128)(2,1)} %get-tuple-element.36.folded_ref, bf16[4,128,512]{2,1,0:T(8,128)(2,1)} %constant.69.table_ref), custom_call_target="tpu_custom_call" | custom-call | flops 1073741824 | bytes 6291456 | tf_op jit(solution)/shard_map/spectra/pallas_call | solution.py:349
  57.3 1.0 copy-done.3
  58.3 4.2 %all-to-all-start.2 = ((bf16[8,16,64,128]{3,2,1,0:T(8,128)(2,1)}), bf16[8,16,64,128]{3,2,1,0:T(8,128)(2,1)S(1)}, u32[]{:S(2)}, u32[]{:S(2)}) async-start(bf16[8,16,64,128]{3,2,1,0:T(8,128)(2,1)} %spectra.3), calls=%async_computation.2 | async-start | bytes 4194304 | tf_op jit(solution)/shard_map/all_to_all | solution.py:472
  62.5 0.6 collective-permute-start.1
  63.1 9.8 %shard_map.115 = bf16[8,64,512]{2,1,0:T(8,128)(2,1)} custom-call(s32[1]{0:T(128)} %bitcast.3.first_ref, bf16[8,8,64,128]{3,2,1,0:T(8,128)(2,1)} %copy-done.3, f32[16,2,1024]{2,1,0:T(2,128)} %copy-done.8, f32[1024,512]{1,0:T(8,128)} %get-tuple-element.39.refs_2_.refs_0_, f32[1024,512]{1,0:T(8,128)} %get-tuple-element.40.refs_3_.refs_1_, ...), custom_call_target="tpu_custom_call" | custom-call | flops 4294967296 | bytes 12582912 | tf_op jit(solution)/shard_map/pallas_call | solution.py:401
  72.9 2.3 %collective-permute-start.2 = (bf16[8,64,512]{2,1,0:T(8,128)(2,1)}, bf16[8,64,512]{2,1,0:T(8,128)(2,1)}, u32[]{:S(2)}, u32[]{:S(2)}) collective-permute-start(bf16[8,64,512]{2,1,0:T(8,128)(2,1)} %shard_map.115), channel_id=1, source_target_pairs={{0,8},{1,9},{2,10},{3,11},{4,12},{5,13},{6,14},{7,15},{8,0},{9,1},... | collective-permute-start | bytes 1572872 | tf_op jit(solution)/shard_map/ppermute | solution.py:505
  75.2 34.6 %all-to-all-done.2.x_ref = bf16[8,16,64,128]{3,2,1,0:T(8,128)(2,1)S(1)} async-done(((bf16[8,16,64,128]{3,2,1,0:T(8,128)(2,1)}), bf16[8,16,64,128]{3,2,1,0:T(8,128)(2,1)S(1)}, u32[]{:S(2)}, u32[]{:S(2)}) %all-to-all-start.2) | async-done | bytes 2097184 | tf_op jit(solution)/shard_map/all_to_all | solution.py:472
  109.8 1.3 copy-done.1
  111.1 17.0 %shard_map.114.own_ref = f32[16,64,512]{2,1,0:T(8,128)} custom-call(s32[1]{0:T(128)} %bitcast.first_ref, bf16[8,16,64,128]{3,2,1,0:T(8,128)(2,1)} %copy-done.1, f32[16,2,1024]{2,1,0:T(2,128)} %get-tuple-element.38.gain_ref, f32[1024,3]{1,0:T(8,128)} %broadcast_select_fusion.refs_0_, f32[3,512]{1,0:T(4,128)} %refs_1_.3, ...), custom_call_target="tpu_custom_call" | custom-call | flops 8589934592 | bytes 12582912 | tf_op jit(solution)/shard_map/pallas_call | solution.py:401
  128.1 5.3 %power.1 = (f32[16,32,512]{2,1,0:T(8,128)}, bf16[16,16,512]{2,1,0:T(8,128)(2,1)}) custom-call(f32[16,64,512]{2,1,0:T(8,128)} %shard_map.114.own_ref, bf16[8,64,512]{2,1,0:T(8,128)(2,1)} %collective-permute-done.1.far0_ref, bf16[8,64,512]{2,1,0:T(8,128)(2,1)} %collective-permute-done.2.far1_ref, s32[1,128]{1,0:T(1,128)} %broadcast_in_dim_tile.3.pick_ref, ...), custom_call_target="tpu_custom_call" | custom-call | tf_op jit(solution)/shard_map/power/pallas_call | solution.py:436
  133.4 3.5 %all-to-all-start.3 = ((bf16[16,16,512]{2,1,0:T(8,128)(2,1)}), bf16[16,16,512]{2,1,0:T(8,128)(2,1)S(1)}, u32[]{:S(2)}, u32[]{:S(2)}) async-start(bf16[16,16,512]{2,1,0:T(8,128)(2,1)} %get-tuple-element.47), calls=%async_computation.3 | async-start | bytes 524288 | tf_op jit(solution)/shard_map/all_to_all | solution.py:509
  136.9 0.6 constant_dynamic-slice_fusion.delay_ref
  137.6 2.7 %turns.1 = (bf16[1024,512]{1,0:T(8,128)(2,1)}, bf16[1024,512]{1,0:T(8,128)(2,1)}) custom-call(s32[64,256]{1,0:T(8,128)} %constant_dynamic-slice_fusion.delay_ref), custom_call_target="tpu_custom_call" | custom-call | tf_op jit(solution)/shard_map/turns/pallas_call | solution.py:514
  140.3 6.6 %all-to-all-done.3 = bf16[16,16,512]{2,1,0:T(8,128)(2,1)S(1)} async-done(((bf16[16,16,512]{2,1,0:T(8,128)(2,1)}), bf16[16,16,512]{2,1,0:T(8,128)(2,1)S(1)}, u32[]{:S(2)}, u32[]{:S(2)}) %all-to-all-start.3) | async-done | bytes 262176 | tf_op jit(solution)/shard_map/all_to_all | solution.py:509
  146.9 0.7 copy-done.2
  147.6 5.6 %plane.1 = f32[16,32,64]{2,1,0:T(8,128)} custom-call(bf16[256,512]{1,0:T(8,128)(2,1)} %bitcast.8, bf16[1024,512]{1,0:T(8,128)(2,1)} %get-tuple-element.48.high_ref, bf16[1024,512]{1,0:T(8,128)(2,1)} %get-tuple-element.49.low_ref), custom_call_target="tpu_custom_call" | custom-call | tf_op jit(solution)/shard_map/plane/pallas_call | solution.py:517
  (18 shorter events, 0.1 us)
Async XLA Ops:
  0.6 136.3 %copy-start = (s32[1024,256]{1,0:T(8,128)S(1)}, s32[1024,256]{1,0:T(8,128)}, u32[]{:S(2)}) copy-start(s32[1024,256]{1,0:T(8,128)} %param.15) | copy-start | bytes 3145732
  9.3 22.7 %all-to-all-start = ((bf16[8,8,64,128]{3,2,1,0:T(8,128)(2,1)}), bf16[8,8,64,128]{3,2,1,0:T(8,128)(2,1)}, u32[]{:S(2)}, u32[]{:S(2)}) async-start(bf16[8,8,64,128]{3,2,1,0:T(8,128)(2,1)} %get-tuple-element.26), calls=%async_computation | async-start | bytes 2097152 | tf_op jit(solution)/shard_map/all_to_all | solution.py:472
  14.5 5.0 %copy-start.4 = (f32[16,2,2048]{2,1,0:T(2,128)S(1)}, f32[16,2,2048]{2,1,0:T(2,128)}, u32[]{:S(2)}) copy-start(f32[16,2,2048]{2,1,0:T(2,128)} %param.11) | copy-start | bytes 786436
  14.5 8.8 %copy-start.5 = (f32[3,2048]{1,0:T(4,128)S(1)}, f32[3,2048]{1,0:T(4,128)}, u32[]{:S(2)}) copy-start(f32[3,2048]{1,0:T(4,128)} %param.12) | copy-start | bytes 73732
  14.5 9.1 %copy-start.7 = (s32[16]{0:T(128)S(1)}, s32[16]{0:T(128)}, u32[]{:S(2)}) copy-start(s32[16]{0:T(128)} %param.16) | copy-start | bytes 196
  14.6 9.8 %copy-start.6 = (s32[2048]{0:T(1024)S(1)}, s32[2048]{0:T(1024)}, u32[]{:S(2)}) copy-start(s32[2048]{0:T(1024)} %param.14) | copy-start | bytes 24580
  20.2 9.5 %collective-permute-start = (f32[16,2,1024]{2,1,0:T(2,128)S(1)}, f32[16,2,1024]{2,1,0:T(2,128)S(1)}, u32[]{:S(2)}, u32[]{:S(2)}) collective-permute-start(f32[16,2,1024]{2,1,0:T(2,128)S(1)} %get-tuple-element.51), channel_id=1, source_target_pairs={{0,8},{1,9},{2,10},{3,11},{4,12},{5,13},{6,14},{7,15},{8,0},{9,1},... | collective-permute-start | bytes 393224 | tf_op jit(solution)/shard_map/ppermute | solution.py:479
  29.7 7.2 %copy-start.8 = (f32[16,2,1024]{2,1,0:T(2,128)}, f32[16,2,1024]{2,1,0:T(2,128)S(1)}, u32[]{:S(2)}) copy-start(f32[16,2,1024]{2,1,0:T(2,128)S(1)} %collective-permute-done.gain_ref) | copy-start | bytes 393220
  31.9 25.4 %all-to-all-start.1 = ((bf16[8,8,64,128]{3,2,1,0:T(8,128)(2,1)}), bf16[8,8,64,128]{3,2,1,0:T(8,128)(2,1)S(1)}, u32[]{:S(2)}, u32[]{:S(2)}) async-start(bf16[8,8,64,128]{3,2,1,0:T(8,128)(2,1)} %spectra.2), calls=%async_computation.1 | async-start | bytes 2097152 | tf_op jit(solution)/shard_map/all_to_all | solution.py:472
  57.3 1.0 copy-start.3
  58.3 51.5 %all-to-all-start.2 = ((bf16[8,16,64,128]{3,2,1,0:T(8,128)(2,1)}), bf16[8,16,64,128]{3,2,1,0:T(8,128)(2,1)S(1)}, u32[]{:S(2)}, u32[]{:S(2)}) async-start(bf16[8,16,64,128]{3,2,1,0:T(8,128)(2,1)} %spectra.3), calls=%async_computation.2 | async-start | bytes 4194304 | tf_op jit(solution)/shard_map/all_to_all | solution.py:472
  62.5 65.6 %collective-permute-start.1 = (bf16[8,64,512]{2,1,0:T(8,128)(2,1)}, bf16[8,64,512]{2,1,0:T(8,128)(2,1)}, u32[]{:S(2)}, u32[]{:S(2)}) collective-permute-start(bf16[8,64,512]{2,1,0:T(8,128)(2,1)} %get-tuple-element.41), channel_id=1, source_target_pairs={{0,8},{1,9},{2,10},{3,11},{4,12},{5,13},{6,14},{7,15},{8,0},{9,1},... | collective-permute-start | bytes 1572872 | tf_op jit(solution)/shard_map/ppermute | solution.py:498
  72.9 55.2 %collective-permute-start.2 = (bf16[8,64,512]{2,1,0:T(8,128)(2,1)}, bf16[8,64,512]{2,1,0:T(8,128)(2,1)}, u32[]{:S(2)}, u32[]{:S(2)}) collective-permute-start(bf16[8,64,512]{2,1,0:T(8,128)(2,1)} %shard_map.115), channel_id=1, source_target_pairs={{0,8},{1,9},{2,10},{3,11},{4,12},{5,13},{6,14},{7,15},{8,0},{9,1},... | collective-permute-start | bytes 1572872 | tf_op jit(solution)/shard_map/ppermute | solution.py:505
  109.8 1.3 copy-start.1
  133.4 13.5 %all-to-all-start.3 = ((bf16[16,16,512]{2,1,0:T(8,128)(2,1)}), bf16[16,16,512]{2,1,0:T(8,128)(2,1)S(1)}, u32[]{:S(2)}, u32[]{:S(2)}) async-start(bf16[16,16,512]{2,1,0:T(8,128)(2,1)} %get-tuple-element.47), calls=%async_computation.3 | async-start | bytes 524288 | tf_op jit(solution)/shard_map/all_to_all | solution.py:509
  146.9 0.7 copy-start.2

commit v4 on v2

--- a/solution.py
+++ b/solution.py
@@ -1,4 +1,3 @@
-import functools
 import math
 
 import jax
@@ -12,6 +11,7 @@
 CH = 256
 TAPS = 4
 TIME = 32
+PITCH = 40
 FFTLEN = 512
 HALF_BINS = TIME // 2
 TWO_PI = 2.0 * math.pi
@@ -47,8 +47,7 @@
 
 
 def dft_table():
-    turns = np.arange(CH)[:, None] * np.arange(FFTLEN)[None, :] % FFTLEN
-    angles = TWO_PI * turns / FFTLEN
+    angles = TWO_PI * (np.arange(CH)[:, None] * np.arange(FFTLEN)[None, :] % FFTLEN) / FFTLEN
     stacked = np.stack([np.cos(angles), -np.sin(angles)], axis=1) / math.sqrt(FFTLEN)
     return stacked.reshape(2 * CH, FFTLEN).astype(np.float32)
 
@@ -80,7 +79,7 @@
 
 
 def transform_rows(table, folded_ref, spread_ref, out_ref):
-    inputs = out_ref.shape[-1]
+    dests, chans, _, inputs = out_ref.shape
     rows = table.shape[0]
     group = 2 if inputs % 128 == 0 else 1
 
@@ -90,17 +89,17 @@
         out = lax.dot_general(table, frames, NT, preferred_element_type=F32)
         for part in range(group):
             piece = out[:, part * inputs : (part + 1) * inputs]
-            spread_ref[pl.ds(index * group + part, rows, stride=TIME), :] = piece
+            spread_ref[pl.ds(index * group + part, rows, stride=PITCH), :] = piece
         return carry
 
     lax.fori_loop(0, TIME // group, step, 0, unroll=4)
-    dests, chans = out_ref.shape[:2]
-    per_chan = 2 * TIME
 
     def pack(dest, carry):
         for chan in range(chans):
-            start = pl.multiple_of((dest * chans + chan) * per_chan, per_chan)
-            out_ref[dest, chan] = spread_ref[pl.ds(start, per_chan), :].astype(BF16)
+            for part in range(2):
+                start = pl.multiple_of(((dest * chans + chan) * 2 + part) * PITCH, 8)
+                block = spread_ref[pl.ds(start, TIME), :].astype(BF16)
+                out_ref[dest, chan, part * TIME : (part + 1) * TIME] = block
         return carry
 
     lax.fori_loop(0, dests, pack, 0, unroll=2)
@@ -131,37 +130,55 @@
         transform_rows(table_ref[...], folded_ref, spread_ref, out_ref)
 
 
-def near_kernel(half_ref, folded_ref, table_ref, out_ref, spread_ref):
+def spectra_kernel(block_ref, folded_ref, table_ref, out_ref, spread_ref):
     transform_rows(table_ref[...], folded_ref, spread_ref, out_ref)
 
 
+def phasor_kernel(first_ref, place_ref, dir_ref, dc_ref, ds_ref, *start_refs):
+    depth, beams = dc_ref.shape
+    wide = 256
+
+    def block(index, carry):
+        rows = pl.ds(pl.multiple_of(index * 16, 16), 16)
+        place = place_ref[rows, :]
+        for lane in range(0, beams, wide):
+            lanes = slice(lane, lane + wide)
+            direction = dir_ref[:, lanes]
+            geometry = place[:, 0:1] * direction[0:1, :]
+            geometry = geometry + place[:, 1:2] * direction[1:2, :]
+            geometry = geometry + place[:, 2:3] * direction[2:3, :]
+            dc_ref[rows, lanes], ds_ref[rows, lanes] = cos_sin_turns(geometry * (1.0 / CH))
+            for k in range(len(start_refs) // 2):
+                first = 1.0 + first_ref[k].astype(F32) * (1.0 / CH)
+                c, s = cos_sin_turns(geometry * first)
+                start_refs[2 * k][rows, lanes], start_refs[2 * k + 1][rows, lanes] = c, s
+        return carry
+
+    lax.fori_loop(0, depth // 16, block, 0, unroll=2)
+
+
 def beam_kernel(
-    first_ref, x_ref, gain_ref, place_ref, dir_ref, out_ref, even_ref, odd_ref, sum_ref
+    x_ref, gain_ref, dc_ref, ds_ref, c_ref, s_ref, out_ref, even_ref, odd_ref, sum_ref
 ):
     step = pl.program_id(0)
     tiles = pl.num_programs(0) - 1
     chans, _, beams = out_ref.shape
-    depth = place_ref.shape[0]
+    depth = dc_ref.shape[0]
     wide = 256
     chunk = depth // chans
 
     def generate(part, weight_ref):
         for sub in range(0, chunk, 16):
             row = pl.multiple_of(part * chunk + sub, 16)
-            place = place_ref[pl.ds(row, 16), :]
+            rows = pl.ds(row, 16)
             for lane in range(0, beams, wide):
                 lanes = slice(lane, lane + wide)
-                direction = dir_ref[:, lanes]
-                geometry = place[:, 0:1] * direction[0:1, :]
-                geometry = geometry + place[:, 1:2] * direction[1:2, :]
-                geometry = geometry + place[:, 2:3] * direction[2:3, :]
-                first = 1.0 + first_ref[0].astype(F32) * (1.0 / CH)
-                c, s = cos_sin_turns(geometry * first)
-                dc, ds = cos_sin_turns(geometry * (1.0 / CH))
+                c, s = c_ref[rows, lanes], s_ref[rows, lanes]
+                dc, ds = dc_ref[rows, lanes], ds_ref[rows, lanes]
                 next_c, next_s = c * dc - s * ds, c * ds + s * dc
                 twice = dc + dc
                 for chan in range(chans):
-                    weight_ref[chan, pl.ds(row, 16), lanes] = c.astype(BF16)
+                    weight_ref[chan, rows, lanes] = c.astype(BF16)
                     weight_ref[chan, pl.ds(depth + row, 16), lanes] = s.astype(BF16)
                     if chan + 2 < chans:
                         c, next_c = next_c, twice * next_c - c
@@ -189,12 +206,13 @@
         out_ref[m] = (sum_ref[m] + accumulate(m, weights[0])).astype(out_ref.dtype)
 
     def over_channels(body, weights):
-        lax.fori_loop(0, chans, lambda m, v: (body(m, weights), v)[1], 0, unroll=min(8, chans))
+        unroll = min(8, chans)
+        lax.fori_loop(0, chans, lambda m, v: (body(m, weights), v)[1], 0, unroll=unroll)
 
     @pl.when(step == 0)
     def _():
         sum_ref[...] = jnp.zeros_like(sum_ref)
-        over_channels(lambda m, w: generate(m, w), even_ref)
+        over_channels(generate, even_ref)
 
     for parity, weights in ((1, (even_ref, odd_ref)), (0, (odd_ref, even_ref))):
 
@@ -261,7 +279,7 @@
 
 def plane_kernel(spec_ref, high_ref, low_ref, out_ref):
     chans, width = spec_ref.shape
-    search, _, trials = out_ref.shape
+    _, _, trials = out_ref.shape
     spec = spec_ref[...].astype(F32)
     lane = lax.broadcasted_iota(jnp.int32, (chans, width), 1)
     is_real = lane % TIME < HALF_BINS
@@ -282,60 +300,87 @@
 PARAMS = pltpu.CompilerParams(vmem_limit_bytes=60 << 20)
 
 
-def channelize(voltages, half_id, halves, chans):
+def fold(voltages, table, block_id, dests, chans):
     inputs, samples = voltages.shape
-    rows = 2 * CH // halves
-    dests = rows // 2 // chans
+    rows = 2 * dests * chans
     window = jnp.asarray(pfb_window())
-    table = jnp.asarray(dft_table()).astype(BF16)
     block = min(32, inputs)
-    out = jax.ShapeDtypeStruct((dests, chans, 2 * TIME, inputs), BF16)
+    spectra = jax.ShapeDtypeStruct((dests, chans, 2 * TIME, inputs), BF16)
     folded = jax.ShapeDtypeStruct((TIME * inputs, FFTLEN), BF16)
-    spread = pltpu.VMEM((rows * TIME, inputs), F32)
-    whole4 = pl.BlockSpec(out.shape, lambda i, h: (0, 0, 0, 0))
-    whole2 = pl.BlockSpec(folded.shape, lambda i, h: (0, 0))
-    far, folded = pl.pallas_call(
+    whole = lambda x: pl.BlockSpec(x.shape, lambda i, k: (0,) * len(x.shape))
+    return pl.pallas_call(
         fold_kernel,
-        out_shape=(out, folded),
+        out_shape=(spectra, folded),
         grid_spec=pltpu.PrefetchScalarGridSpec(
             num_scalar_prefetch=1,
             grid=(inputs // block,),
             in_specs=[
-                pl.BlockSpec((block, samples), lambda i, h: (i, 0)),
-                pl.BlockSpec(window.shape, lambda i, h: (0, 0)),
-                pl.BlockSpec((rows, FFTLEN), lambda i, h: (halves - 1 - h[0], 0)),
+                pl.BlockSpec((block, samples), lambda i, k: (i, 0)),
+                whole(window),
+                pl.BlockSpec((rows, FFTLEN), lambda i, k: (k[0], 0)),
             ],
-            out_specs=(whole4, whole2),
-            scratch_shapes=[spread],
+            out_specs=(whole(spectra), whole(folded)),
+            scratch_shapes=[pltpu.VMEM((rows * PITCH, inputs), F32)],
         ),
         compiler_params=PARAMS,
         cost_estimate=pl.CostEstimate(
-            flops=4 * rows * FFTLEN * TIME * inputs, bytes_accessed=14 << 20, transcendentals=0
+            flops=8 * rows * FFTLEN * TIME * inputs, bytes_accessed=12 << 20, transcendentals=0
         ),
         name="fold",
-    )(half_id, voltages, window, table)
-    near = pl.pallas_call(
-        near_kernel,
+    )(block_id, voltages, window, table)
+
+
+def more_spectra(folded, table, block_id, dests, chans):
+    rows = 2 * dests * chans
+    inputs = folded.shape[0] // TIME
+    out = jax.ShapeDtypeStruct((dests, chans, 2 * TIME, inputs), BF16)
+    return pl.pallas_call(
+        spectra_kernel,
         out_shape=out,
         grid_spec=pltpu.PrefetchScalarGridSpec(
             num_scalar_prefetch=1,
             grid=(1,),
-            in_specs=[whole2, pl.BlockSpec((rows, FFTLEN), lambda i, h: (h[0], 0))],
-            out_specs=whole4,
-            scratch_shapes=[spread],
+            in_specs=[
+                pl.BlockSpec(folded.shape, lambda i, k: (0, 0)),
+                pl.BlockSpec((rows, FFTLEN), lambda i, k: (k[0], 0)),
+            ],
+            out_specs=pl.BlockSpec(out.shape, lambda i, k: (0, 0, 0, 0)),
+            scratch_shapes=[pltpu.VMEM((rows * PITCH, inputs), F32)],
         ),
         compiler_params=PARAMS,
         cost_estimate=pl.CostEstimate(
-            flops=2 * rows * FFTLEN * TIME * inputs, bytes_accessed=8 << 20, transcendentals=0
-        ),
-        name="near",
-    )(half_id, folded, table)
-    return far, near
-
-
-def form_beams(x, gains, places, directions, first, out_type):
+            flops=4 * rows * FFTLEN * TIME * inputs, bytes_accessed=6 << 20, transcendentals=0
+        ),
+        name="spectra",
+    )(block_id, folded, table)
+
+
+def phasors(firsts, places, directions):
+    total, beams = places.shape[0], directions.shape[1]
+    depth = 128
+    count = 2 + 2 * firsts.shape[0]
+    return pl.pallas_call(
+        phasor_kernel,
+        out_shape=[jax.ShapeDtypeStruct((total, beams), F32)] * count,
+        grid_spec=pltpu.PrefetchScalarGridSpec(
+            num_scalar_prefetch=1,
+            grid=(total // depth,),
+            in_specs=[
+                pl.BlockSpec((depth, 3), lambda i, f: (i, 0)),
+                pl.BlockSpec(directions.shape, lambda i, f: (0, 0)),
+            ],
+            out_specs=[pl.BlockSpec((depth, beams), lambda i, f: (i, 0))] * count,
+        ),
+        compiler_params=PARAMS,
+        cost_estimate=pl.CostEstimate(
+            flops=8000 * total * beams, bytes_accessed=count * 4 * total * beams, transcendentals=0
+        ),
+        name="phasors",
+    )(firsts, places, directions)
+
+
+def form_beams(x, gains, state, start, beams, out_type):
     sources, chans, rows, inputs = x.shape
-    beams = directions.shape[1]
     total = sources * inputs
     if inputs != 128:
         x = x.transpose(1, 2, 0, 3).reshape(chans, rows, total // 128, 128)
@@ -343,33 +388,29 @@
     depth = 256
     blocks = depth // 128
     tiles = total // depth
+    late = lambda i: jnp.maximum(i - 1, 0)
+    state_spec = pl.BlockSpec((depth, beams), lambda i: (jnp.minimum(i, tiles - 1), start))
     return pl.pallas_call(
         beam_kernel,
         out_shape=jax.ShapeDtypeStruct((chans, rows, beams), out_type),
-        grid_spec=pltpu.PrefetchScalarGridSpec(
-            num_scalar_prefetch=1,
-            grid=(tiles + 1,),
-            in_specs=[
-                pl.BlockSpec(
-                    (blocks, chans, rows, 128), lambda i, f: (jnp.maximum(i - 1, 0), 0, 0, 0)
-                ),
-                pl.BlockSpec((chans, 2, depth), lambda i, f: (0, 0, jnp.maximum(i - 1, 0))),
-                pl.BlockSpec((depth, 3), lambda i, f: (jnp.minimum(i, tiles - 1), 0)),
-                pl.BlockSpec(directions.shape, lambda i, f: (0, 0)),
-            ],
-            out_specs=pl.BlockSpec((chans, rows, beams), lambda i, f: (0, 0, 0)),
-            scratch_shapes=[
-                pltpu.VMEM((chans, 2 * depth, beams), BF16),
-                pltpu.VMEM((chans, 2 * depth, beams), BF16),
-                pltpu.VMEM((chans, rows, beams), F32),
-            ],
-        ),
+        grid=(tiles + 1,),
+        in_specs=[
+            pl.BlockSpec((blocks, chans, rows, 128), lambda i: (late(i), 0, 0, 0)),
+            pl.BlockSpec((chans, 2, depth), lambda i: (0, 0, late(i))),
+        ]
+        + [state_spec] * 4,
+        out_specs=pl.BlockSpec((chans, rows, beams), lambda i: (0, 0, 0)),
+        scratch_shapes=[
+            pltpu.VMEM((chans, 2 * depth, beams), BF16),
+            pltpu.VMEM((chans, 2 * depth, beams), BF16),
+            pltpu.VMEM((chans, rows, beams), F32),
+        ],
         compiler_params=PARAMS,
         cost_estimate=pl.CostEstimate(
-            flops=32 * chans * rows * total * beams, bytes_accessed=6 << 20, transcendentals=0
+            flops=16 * chans * rows * total * beams, bytes_accessed=12 << 20, transcendentals=0
         ),
         name="beams",
-    )(first, x, gains, places, directions)
+    )(x, gains, *state)
 
 
 def powers(own, far, pick, search, copies):
@@ -412,7 +453,8 @@
     inputs = gains.shape[2] // halves
     own_inputs = half_id * inputs
     half_scalar = half_id.astype(jnp.int32).reshape(1)
-    far, near = channelize(voltages, half_scalar, halves, chans)
+    table = jnp.asarray(dft_table()).astype(BF16)
+    far, folded = fold(voltages, table, 1 - half_scalar, per_half, chans)
 
     def exchange(x):
         return lax.all_to_all(
@@ -420,30 +462,31 @@
         )
 
     far = exchange(far)
+    near = more_spectra(folded, table, half_scalar, per_half, chans)
     near, gains, positions = lax.optimization_barrier((near, gains, positions))
-    far_gains = lax.ppermute(
-        lax.dynamic_slice_in_dim(gains, inputs - own_inputs, inputs, 2), "crate", partners
-    )
+    far_gains = lax.dynamic_slice_in_dim(gains, inputs - own_inputs, inputs, 2)
+    far_gains = lax.ppermute(far_gains, "crate", partners)
     near_gains = lax.dynamic_slice_in_dim(gains, own_inputs, inputs, 2)
     order = lax.dynamic_slice_in_dim(input_order, own_inputs, inputs, 0)
     places = jnp.take(positions.T, order, axis=0)
     search = search_beams.shape[0]
     pick = jnp.tile(search_beams, 128 // search)[None, :]
-    own_first = (position * chans).astype(jnp.int32).reshape(1)
-    far_first = ((position + per_half) % devices * chans).astype(jnp.int32).reshape(1)
-    far, near, far_gains, near_gains, places, pick = lax.optimization_barrier(
-        (far, near, far_gains, near_gains, places, pick)
+    firsts = jnp.stack([(position + per_half) % devices, position]) * chans
+    dc, ds, far_c, far_s, near_c, near_s = phasors(
+        firsts.astype(jnp.int32), places, directions
+    )
+    near, near_gains, pick, dc, ds, far_c, far_s = lax.optimization_barrier(
+        (near, near_gains, pick, dc, ds, far_c, far_s)
     )
     near = exchange(near)
 
     beams = directions.shape[1]
     cut = beams // 2
     far_sums = []
-    for start in range(0, beams, cut):
-        some = lax.slice_in_dim(directions, start, start + cut, axis=1)
-        part = form_beams(far, far_gains, places, some, far_first, BF16)
-        far_sums.append(lax.ppermute(part, "crate", partners))
-    near_sums = form_beams(near, near_gains, places, directions, own_first, F32)
+    for part in range(2):
+        sums = form_beams(far, far_gains, (dc, ds, far_c, far_s), part, cut, BF16)
+        far_sums.append(lax.ppermute(sums, "crate", partners))
+    near_sums = form_beams(near, near_gains, (dc, ds, near_c, near_s), 0, beams, F32)
 
     beam_power, spectrum = powers(near_sums, far_sums, pick, search, devices)
     spectrum = lax.all_to_all(spectrum, "crate", split_axis=0, concat_axis=0, tiled=True)

time: 138 us -> 158 us (1.14)
  waiting for transfers between devices: 35.6 us -> 50.4 us
  Pallas kernels: 70.8 us -> 75.6 us
    ppermute x3, waiting for transfers between devices: 14.5 us -> 41.7 us  [the longest x1 23.1 us: on_device(): far_gains = lax.ppermute(far_gains, 'crate', partners)]
    all_to_all x2, waiting for transfers between devices: 14.4 us -> 2.06 us  [exchange(): lax.all_to_all(x, 'crate', split_axis=0, concat_axis=0, axis_index_groups...]
    pallas_call x2 -> x3, Pallas kernels: 18.7 us -> 26.9 us  [the longest x1 11.7 us: phasors(): pl.pallas_call(phasor_kernel, out_shape=[jax.ShapeDtypeStruct((total, bea...]
    pallas_call x3, Pallas kernels: 38.7 us -> 35.2 us  [form_beams(): pl.pallas_call(beam_kernel, out_shape=jax.ShapeDtypeStruct((chans, rows,...]
    all_to_all x2, starting transfers between devices: 11 us -> 9.07 us  [exchange(): lax.all_to_all(x, 'crate', split_axis=0, concat_axis=0, axis_index_groups...]
    all_to_all x1, starting transfers between devices: 4.07 us -> 5.86 us  [on_device(): lax.all_to_all(spectrum, 'crate', split_axis=0, concat_axis=0, tiled=True)]
  transfers between devices with their start and end apart: 6 -> 6, of which waited for: 5 -> 5; matrix products, arithmetic and copies ran while one was open for 5% -> 4% of each run, Pallas kernels for 36% -> 35%
where the time goes in v4:
time: 158 us
  Pallas kernels  75.6 us (48%)
  waiting for transfers between devices  50.4 us (32%)
  starting transfers between devices  21.4 us (14%)
  local copies, waits for them, and re-layouts  7.8 us (5%)
  other arithmetic  1.67 us (1%)
    pallas_call x3, Pallas kernels, form_beams(): pl.pallas_call(beam_kernel, out_shape=jax.ShapeDtypeStruct((chans, rows,...  35.2 us
    ppermute x1, waiting for transfers between devices, on_device(): far_gains = lax.ppermute(far_gains, 'crate', partners)  23.1 us
    ppermute x2, waiting for transfers between devices, on_device(): far_sums.append(lax.ppermute(sums, 'crate', partners))  18.6 us
    pallas_call x1, Pallas kernels, phasors(): pl.pallas_call(phasor_kernel, out_shape=[jax.ShapeDtypeStruct((total, bea...  11.7 us
    pallas_call x1, Pallas kernels, fold(): pl.pallas_call(fold_kernel, out_shape=(spectra, folded), grid_spec=pltpu....  9.39 us
    all_to_all x2, starting transfers between devices, exchange(): lax.all_to_all(x, 'crate', split_axis=0, concat_axis=0, axis_index_groups...  9.07 us
    all_to_all x1, waiting for transfers between devices, on_device(): lax.all_to_all(spectrum, 'crate', split_axis=0, concat_axis=0, tiled=True)  6.63 us
    all_to_all x1, starting transfers between devices, on_device(): lax.all_to_all(spectrum, 'crate', split_axis=0, concat_axis=0, tiled=True)  5.86 us
  transfers between devices with their start and end apart: 6, of which 5 were waited for; matrix products, arithmetic and copies ran while one was open for 4% of the time, Pallas kernels for 35%

profile of v4, /device:TPU:0, one launch (start us, length us, event | category | flops | bytes accessed | tf_op | source)
XLA Modules:
  0.0 157.7 jit_solution(17503096233297439484)
XLA Ops:
  0.6 0.0 copy-start
  0.7 9.4 %fold.1 = (bf16[8,16,64,128]{3,2,1,0:T(8,128)(2,1)}, bf16[4096,512]{1,0:T(8,128)(2,1)}) custom-call(s32[1]{0:T(128)S(6)} %sub.14.half_ref, bf16[128,17920]{1,0:T(8,128)(2,1)} %volt_ref.1, f32[4,512]{1,0:T(4,128)} %constant.66.clone.window_ref, bf16[512,512]{1,0:T(8,128)(2,1)} %constant.68.table_ref), custom_call_target="tpu_custom_call" | custom-call | flops 4294967296 | bytes 12582912 | tf_op jit(solution)/shard_map/fold/pallas_call | solution.py:311
  10.1 5.3 %all-to-all-start.1 = ((bf16[8,16,64,128]{3,2,1,0:T(8,128)(2,1)}), bf16[8,16,64,128]{3,2,1,0:T(8,128)(2,1)}, u32[]{:S(2)}, u32[]{:S(2)}) async-start(bf16[8,16,64,128]{3,2,1,0:T(8,128)(2,1)} %get-tuple-element.38), calls=%async_computation.1 | async-start | bytes 4194304 | tf_op jit(solution)/shard_map/all_to_all | solution.py:460
  15.3 0.0 copy-start.6
  15.4 5.8 %spectra.1 = bf16[8,16,64,128]{3,2,1,0:T(8,128)(2,1)} custom-call(s32[1]{0:T(128)} %bitcast.block_ref, bf16[4096,512]{1,0:T(8,128)(2,1)} %get-tuple-element.24.folded_ref, bf16[512,512]{1,0:T(8,128)(2,1)} %constant.68.table_ref), custom_call_target="tpu_custom_call" | custom-call | flops 2147483648 | bytes 6291456 | tf_op jit(solution)/shard_map/spectra/pallas_call | solution.py:337
  21.2 0.4 copy.12
  21.6 0.6 broadcast_in_dim_tile.3.pick_ref
  22.2 2.8 %gather_fusion = f32[1024,3]{1,0:T(8,128)S(1)} fusion(f32[2048,3]{1,0:T(8,128)S(1)} %bitcast.7, s32[1024]{0:T(1024)S(1)} %fusion), kind=kCustom, calls=%fused_computation | custom fusion | bytes 28672 | tf_op jit(solution)/shard_map/jit(_take)/gather | solution.py:471
  25.1 0.7 add_multiply_fusion.first_ref
  25.7 0.7 constant_dynamic-slice_fusion.1
  26.4 1.0 broadcast_select_fusion.place_ref
  27.4 11.7 %phasors.1 = (f32[1024,512]{1,0:T(8,128)}, f32[1024,512]{1,0:T(8,128)}, f32[1024,512]{1,0:T(8,128)}, f32[1024,512]{1,0:T(8,128)}, f32[1024,512]{1,0:T(8,128)}, /*index=5*/f32[1024,512]{1,0:T(8,128)}) custom-call(s32[2]{0:T(128)} %add_multiply_fusion.first_ref, f32[1024,3]{1,0:T(8,128)} %broadcast_select_fusion.place_ref, f32[3,512]{1,0:T(4,128)} %dir_ref.1), custom_call_target="tpu_custom_call" | custom-call | flops 4194304000 | bytes 12582912 | tf_op jit(solution)/shard_map/phasors/pallas_call | solution.py:362
  39.1 2.1 %all-to-all-done.1.x_ref = bf16[8,16,64,128]{3,2,1,0:T(8,128)(2,1)} async-done(((bf16[8,16,64,128]{3,2,1,0:T(8,128)(2,1)}), bf16[8,16,64,128]{3,2,1,0:T(8,128)(2,1)}, u32[]{:S(2)}, u32[]{:S(2)}) %all-to-all-start.1) | async-done | bytes 2097184 | tf_op jit(solution)/shard_map/all_to_all | solution.py:460
  41.2 3.8 %all-to-all-start = ((bf16[8,16,64,128]{3,2,1,0:T(8,128)(2,1)}), bf16[8,16,64,128]{3,2,1,0:T(8,128)(2,1)S(1)}, u32[]{:S(2)}, u32[]{:S(2)}) async-start(bf16[8,16,64,128]{3,2,1,0:T(8,128)(2,1)} %spectra.1), calls=%async_computation | async-start | bytes 4194304 | tf_op jit(solution)/shard_map/all_to_all | solution.py:460
  44.9 3.1 %collective-permute-start = (f32[16,2,1024]{2,1,0:T(2,128)S(1)}, f32[16,2,1024]{2,1,0:T(2,128)S(1)}, u32[]{:S(2)}, u32[]{:S(2)}) collective-permute-start(f32[16,2,1024]{2,1,0:T(2,128)S(1)} %get-tuple-element.46), channel_id=1, source_target_pairs={{0,8},{1,9},{2,10},{3,11},{4,12},{5,13},{6,14},{7,15},{8,0},{9,1},... | collective-permute-start | bytes 393224 | tf_op jit(solution)/shard_map/ppermute | solution.py:468
  48.0 23.1 %collective-permute-done.gain_ref = f32[16,2,1024]{2,1,0:T(2,128)S(1)} collective-permute-done((f32[16,2,1024]{2,1,0:T(2,128)S(1)}, f32[16,2,1024]{2,1,0:T(2,128)S(1)}, u32[]{:S(2)}, u32[]{:S(2)}) %collective-permute-start) | collective-permute-done | bytes 131104 | tf_op jit(solution)/shard_map/ppermute | solution.py:468
  71.1 0.6 copy-done.7
  71.7 9.4 %beams.5 = bf16[16,64,256]{2,1,0:T(8,128)(2,1)} custom-call(bf16[8,16,64,128]{3,2,1,0:T(8,128)(2,1)} %all-to-all-done.1.x_ref, f32[16,2,1024]{2,1,0:T(2,128)} %copy-done.7, f32[1024,512]{1,0:T(8,128)} %get-tuple-element.34.dc_ref, f32[1024,512]{1,0:T(8,128)} %get-tuple-element.35.ds_ref, f32[1024,512]{1,0:T(8,128)} %get-tuple-element.39.c_ref, ...), custom_call_target="tpu_custom_call" | custom-call | flops 4294967296 | bytes 12582912 | tf_op jit(solution)/shard_map/beams/pallas_call | solution.py:393
  81.2 3.4 %collective-permute-start.2 = (bf16[16,64,256]{2,1,0:T(8,128)(2,1)}, bf16[16,64,256]{2,1,0:T(8,128)(2,1)}, u32[]{:S(2)}, u32[]{:S(2)}) collective-permute-start(bf16[16,64,256]{2,1,0:T(8,128)(2,1)} %beams.5), channel_id=1, source_target_pairs={{0,8},{1,9},{2,10},{3,11},{4,12},{5,13},{6,14},{7,15},{8,0},{9,1},... | collective-permute-start | bytes 1572872 | tf_op jit(solution)/shard_map/ppermute | solution.py:488
  84.5 9.4 %beams.4 = bf16[16,64,256]{2,1,0:T(8,128)(2,1)} custom-call(bf16[8,16,64,128]{3,2,1,0:T(8,128)(2,1)} %all-to-all-done.1.x_ref, f32[16,2,1024]{2,1,0:T(2,128)} %copy-done.7, f32[1024,512]{1,0:T(8,128)} %get-tuple-element.34.dc_ref, f32[1024,512]{1,0:T(8,128)} %get-tuple-element.35.ds_ref, f32[1024,512]{1,0:T(8,128)} %get-tuple-element.39.c_ref, ...), custom_call_target="tpu_custom_call" | custom-call | flops 4294967296 | bytes 12582912 | tf_op jit(solution)/shard_map/beams/pallas_call | solution.py:393
  93.9 0.0 collective-permute-start.1
  94.0 1.3 copy-done.1
  95.3 16.4 %beams.3.own_ref = f32[16,64,512]{2,1,0:T(8,128)} custom-call(bf16[8,16,64,128]{3,2,1,0:T(8,128)(2,1)} %copy-done.1, f32[16,2,1024]{2,1,0:T(2,128)} %get-tuple-element.33.gain_ref, f32[1024,512]{1,0:T(8,128)} %get-tuple-element.34.dc_ref, f32[1024,512]{1,0:T(8,128)} %get-tuple-element.35.ds_ref, f32[1024,512]{1,0:T(8,128)} %get-tuple-element.36.c_ref, ...), custom_call_target="tpu_custom_call" | custom-call | flops 8589934592 | bytes 12582912 | tf_op jit(solution)/shard_map/beams/pallas_call | solution.py:393
  111.7 8.4 %collective-permute-done.2.far1_ref = bf16[16,64,256]{2,1,0:T(8,128)(2,1)} collective-permute-done((bf16[16,64,256]{2,1,0:T(8,128)(2,1)}, bf16[16,64,256]{2,1,0:T(8,128)(2,1)}, u32[]{:S(2)}, u32[]{:S(2)}) %collective-permute-start.2) | collective-permute-done | bytes 524320 | tf_op jit(solution)/shard_map/ppermute | solution.py:488
  120.1 10.2 %collective-permute-done.1.far0_ref = bf16[16,64,256]{2,1,0:T(8,128)(2,1)} collective-permute-done((bf16[16,64,256]{2,1,0:T(8,128)(2,1)}, bf16[16,64,256]{2,1,0:T(8,128)(2,1)}, u32[]{:S(2)}, u32[]{:S(2)}) %collective-permute-start.1) | collective-permute-done | bytes 524320 | tf_op jit(solution)/shard_map/ppermute | solution.py:488
  130.3 5.1 %power.1 = (f32[16,32,512]{2,1,0:T(8,128)}, bf16[16,16,512]{2,1,0:T(8,128)(2,1)}) custom-call(f32[16,64,512]{2,1,0:T(8,128)} %beams.3.own_ref, bf16[16,64,256]{2,1,0:T(8,128)(2,1)} %collective-permute-done.1.far0_ref, bf16[16,64,256]{2,1,0:T(8,128)(2,1)} %collective-permute-done.2.far1_ref, s32[1,128]{1,0:T(1,128)} %broadcast_in_dim_tile.3.pick_ref, ...), custom_call_target="tpu_custom_call" | custom-call | tf_op jit(solution)/shard_map/power/pallas_call | solution.py:426
  135.5 5.9 %all-to-all-start.2 = ((bf16[16,16,512]{2,1,0:T(8,128)(2,1)}), bf16[16,16,512]{2,1,0:T(8,128)(2,1)S(1)}, u32[]{:S(2)}, u32[]{:S(2)}) async-start(bf16[16,16,512]{2,1,0:T(8,128)(2,1)} %get-tuple-element.43), calls=%async_computation.2 | async-start | bytes 524288 | tf_op jit(solution)/shard_map/all_to_all | solution.py:492
  141.3 0.6 constant_dynamic-slice_fusion.delay_ref
  142.0 2.7 %turns.1 = (bf16[1024,512]{1,0:T(8,128)(2,1)}, bf16[1024,512]{1,0:T(8,128)(2,1)}) custom-call(s32[64,256]{1,0:T(8,128)} %constant_dynamic-slice_fusion.delay_ref), custom_call_target="tpu_custom_call" | custom-call | tf_op jit(solution)/shard_map/turns/pallas_call | solution.py:497
  144.7 6.6 %all-to-all-done.2 = bf16[16,16,512]{2,1,0:T(8,128)(2,1)S(1)} async-done(((bf16[16,16,512]{2,1,0:T(8,128)(2,1)}), bf16[16,16,512]{2,1,0:T(8,128)(2,1)S(1)}, u32[]{:S(2)}, u32[]{:S(2)}) %all-to-all-start.2) | async-done | bytes 262176 | tf_op jit(solution)/shard_map/all_to_all | solution.py:492
  151.3 0.7 copy-done.2
  152.0 5.6 %plane.1 = f32[16,32,64]{2,1,0:T(8,128)} custom-call(bf16[256,512]{1,0:T(8,128)(2,1)} %bitcast.8, bf16[1024,512]{1,0:T(8,128)(2,1)} %get-tuple-element.44.high_ref, bf16[1024,512]{1,0:T(8,128)(2,1)} %get-tuple-element.45.low_ref), custom_call_target="tpu_custom_call" | custom-call | tf_op jit(solution)/shard_map/plane/pallas_call | solution.py:500
  (15 shorter events, 0.0 us)
Async XLA Ops:
  0.6 140.7 %copy-start = (s32[1024,256]{1,0:T(8,128)S(1)}, s32[1024,256]{1,0:T(8,128)}, u32[]{:S(2)}) copy-start(s32[1024,256]{1,0:T(8,128)} %param.15) | copy-start | bytes 3145732
  10.1 31.1 %all-to-all-start.1 = ((bf16[8,16,64,128]{3,2,1,0:T(8,128)(2,1)}), bf16[8,16,64,128]{3,2,1,0:T(8,128)(2,1)}, u32[]{:S(2)}, u32[]{:S(2)}) async-start(bf16[8,16,64,128]{3,2,1,0:T(8,128)(2,1)} %get-tuple-element.38), calls=%async_computation.1 | async-start | bytes 4194304 | tf_op jit(solution)/shard_map/all_to_all | solution.py:460
  15.3 5.9 %copy-start.4 = (f32[3,2048]{1,0:T(4,128)S(1)}, f32[3,2048]{1,0:T(4,128)}, u32[]{:S(2)}) copy-start(f32[3,2048]{1,0:T(4,128)} %param.12) | copy-start | bytes 73732
  15.3 6.2 %copy-start.6 = (s32[16]{0:T(128)S(1)}, s32[16]{0:T(128)}, u32[]{:S(2)}) copy-start(s32[16]{0:T(128)} %param.16) | copy-start | bytes 196
  15.4 6.9 %copy-start.5 = (s32[2048]{0:T(1024)S(1)}, s32[2048]{0:T(1024)}, u32[]{:S(2)}) copy-start(s32[2048]{0:T(1024)} %param.14) | copy-start | bytes 24580
  22.2 3.5 %copy-start.3 = (f32[16,2,2048]{2,1,0:T(2,128)S(1)}, f32[16,2,2048]{2,1,0:T(2,128)}, u32[]{:S(2)}) copy-start(f32[16,2,2048]{2,1,0:T(2,128)} %param.11) | copy-start | bytes 786436
  41.2 52.8 %all-to-all-start = ((bf16[8,16,64,128]{3,2,1,0:T(8,128)(2,1)}), bf16[8,16,64,128]{3,2,1,0:T(8,128)(2,1)S(1)}, u32[]{:S(2)}, u32[]{:S(2)}) async-start(bf16[8,16,64,128]{3,2,1,0:T(8,128)(2,1)} %spectra.1), calls=%async_computation | async-start | bytes 4194304 | tf_op jit(solution)/shard_map/all_to_all | solution.py:460
  44.9 26.2 %collective-permute-start = (f32[16,2,1024]{2,1,0:T(2,128)S(1)}, f32[16,2,1024]{2,1,0:T(2,128)S(1)}, u32[]{:S(2)}, u32[]{:S(2)}) collective-permute-start(f32[16,2,1024]{2,1,0:T(2,128)S(1)} %get-tuple-element.46), channel_id=1, source_target_pairs={{0,8},{1,9},{2,10},{3,11},{4,12},{5,13},{6,14},{7,15},{8,0},{9,1},... | collective-permute-start | bytes 393224 | tf_op jit(solution)/shard_map/ppermute | solution.py:468
  71.1 0.6 copy-start.7
  81.2 38.9 %collective-permute-start.2 = (bf16[16,64,256]{2,1,0:T(8,128)(2,1)}, bf16[16,64,256]{2,1,0:T(8,128)(2,1)}, u32[]{:S(2)}, u32[]{:S(2)}) collective-permute-start(bf16[16,64,256]{2,1,0:T(8,128)(2,1)} %beams.5), channel_id=1, source_target_pairs={{0,8},{1,9},{2,10},{3,11},{4,12},{5,13},{6,14},{7,15},{8,0},{9,1},... | collective-permute-start | bytes 1572872 | tf_op jit(solution)/shard_map/ppermute | solution.py:488
  93.9 36.4 %collective-permute-start.1 = (bf16[16,64,256]{2,1,0:T(8,128)(2,1)}, bf16[16,64,256]{2,1,0:T(8,128)(2,1)}, u32[]{:S(2)}, u32[]{:S(2)}) collective-permute-start(bf16[16,64,256]{2,1,0:T(8,128)(2,1)} %beams.4), channel_id=1, source_target_pairs={{0,8},{1,9},{2,10},{3,11},{4,12},{5,13},{6,14},{7,15},{8,0},{9,1},... | collective-permute-start | bytes 1572872 | tf_op jit(solution)/shard_map/ppermute | solution.py:488
  94.0 1.3 copy-start.1
  135.5 15.9 %all-to-all-start.2 = ((bf16[16,16,512]{2,1,0:T(8,128)(2,1)}), bf16[16,16,512]{2,1,0:T(8,128)(2,1)S(1)}, u32[]{:S(2)}, u32[]{:S(2)}) async-start(bf16[16,16,512]{2,1,0:T(8,128)(2,1)} %get-tuple-element.43), calls=%async_computation.2 | async-start | bytes 524288 | tf_op jit(solution)/shard_map/all_to_all | solution.py:492
  151.3 0.7 copy-start.2

commit v5 on v4

--- a/solution.py
+++ b/solution.py
@@ -1,3 +1,4 @@
+import functools
 import math
 
 import jax
@@ -205,14 +206,13 @@
     def last(m, weights):
         out_ref[m] = (sum_ref[m] + accumulate(m, weights[0])).astype(out_ref.dtype)
 
-    def over_channels(body, weights):
-        unroll = min(8, chans)
+    def over_channels(body, weights, unroll=min(8, chans)):
         lax.fori_loop(0, chans, lambda m, v: (body(m, weights), v)[1], 0, unroll=unroll)
 
     @pl.when(step == 0)
     def _():
         sum_ref[...] = jnp.zeros_like(sum_ref)
-        over_channels(generate, even_ref)
+        over_channels(generate, even_ref, 1)
 
     for parity, weights in ((1, (even_ref, odd_ref)), (0, (odd_ref, even_ref))):
 
@@ -225,75 +225,108 @@
             over_channels(last, weights)
 
 
-def power_kernel(
-    own_ref, far0_ref, far1_ref, pick_ref, high_ref, low_ref, power_ref, spec_ref, chosen_ref
-):
-    step = pl.program_id(0)
-    block, _, beams = own_ref.shape
-    search = chosen_ref.shape[1] // TIME
+def pick_beams(rows, pick_ref, chans, search):
     per = 128 // search
-    far = jnp.concatenate([far0_ref[...], far1_ref[...]], axis=2)
-    total = own_ref[...] + far.astype(F32)
-    real, imag = total[:, :TIME], total[:, TIME:]
-    power = (real * real + imag * imag) * (1.0 / 2048)
-    power_ref[...] = power
-    rows = power.reshape(block * TIME, beams)
-    hit = lax.broadcasted_iota(jnp.int32, (beams, 128), 0) == pick_ref[...]
+    hit = lax.broadcasted_iota(jnp.int32, (rows.shape[1], 128), 0) == pick_ref[...]
     hot = jnp.where(hit, 1.0, 0.0).astype(BF16)
-    high, low = split_bf16(rows)
-    picked = jnp.dot(high, hot, preferred_element_type=F32)
-    picked = picked + jnp.dot(low, hot, preferred_element_type=F32)
+    if rows.dtype == BF16:
+        picked = jnp.dot(rows, hot, preferred_element_type=F32)
+    else:
+        high, low = split_bf16(rows)
+        picked = jnp.dot(high, hot, preferred_element_type=F32)
+        picked = picked + jnp.dot(low, hot, preferred_element_type=F32)
     row_id = lax.broadcasted_iota(jnp.int32, (per, 128), 0)
     lane_id = lax.broadcasted_iota(jnp.int32, (per, 128), 1) // search
-    for chan in range(block):
+    chosen = []
+    for chan in range(chans):
         pieces = []
         for j in range(TIME // per):
             start = chan * TIME + j * per
             piece = jnp.where(row_id == lane_id, picked[start : start + per], 0.0)
             pieces.append(jnp.sum(piece, axis=0, keepdims=True))
-        chosen_ref[pl.ds(step * block + chan, 1), :] = jnp.concatenate(pieces, axis=1)
+        chosen.append(jnp.concatenate(pieces, axis=1))
+    return chosen
+
+
+def far_pick_kernel(sum0_ref, sum1_ref, pick_ref, out_ref, picked_ref):
+    step = pl.program_id(0)
+    block = sum0_ref.shape[0]
+    search = out_ref.shape[1] // TIME
+    both = jnp.concatenate([sum0_ref[...], sum1_ref[...]], axis=2)
+    rows = both.reshape(block * 2 * TIME, both.shape[2])
+    half = picked_ref.shape[0] // 2
+    for k, row in enumerate(pick_beams(rows, pick_ref, 2 * block, search)):
+        place = (k % 2) * half + step * block + k // 2
+        picked_ref[pl.ds(place, 1), :] = row
 
     @pl.when(step == pl.num_programs(0) - 1)
     def _():
-        g_high, g_low = split_bf16(chosen_ref[...])
+        out_ref[...] = picked_ref[...].astype(BF16)
+
+
+def spectrum_kernel(
+    own_ref, far_ref, pick_ref, high_ref, low_ref, spec_ref, picked_ref, norm
+):
+    step = pl.program_id(0)
+    block = own_ref.shape[0]
+    copies, chans, width = spec_ref.shape
+    search = width // TIME
+    rows = own_ref[...].reshape(block * 2 * TIME, own_ref.shape[2])
+    for k, row in enumerate(pick_beams(rows, pick_ref, 2 * block, search)):
+        place = (k % 2) * chans + step * block + k // 2
+        picked_ref[pl.ds(place, 1), :] = row
+
+    @pl.when(step == pl.num_programs(0) - 1)
+    def _():
+        real = picked_ref[:chans] + far_ref[:chans].astype(F32)
+        imag = picked_ref[chans:] + far_ref[chans:].astype(F32)
+        g_high, g_low = split_bf16((real * real + imag * imag) * norm)
         spectrum = jnp.dot(g_high, high_ref[...], preferred_element_type=F32)
         spectrum = spectrum + jnp.dot(g_low, high_ref[...], preferred_element_type=F32)
         spectrum = spectrum + jnp.dot(g_high, low_ref[...], preferred_element_type=F32)
         spectrum = spectrum.astype(BF16)
-        for dest in range(spec_ref.shape[0]):
+        for dest in range(copies):
             spec_ref[dest] = spectrum
 
 
-def turn_kernel(delay_ref, high_ref, low_ref):
+def power_kernel(own_ref, far0_ref, far1_ref, power_ref, norm):
+    far = jnp.concatenate([far0_ref[...], far1_ref[...]], axis=2)
+    total = own_ref[...] + far.astype(F32)
+    real, imag = total[:, :TIME], total[:, TIME:]
+    power_ref[...] = (real * real + imag * imag) * norm
+
+
+def turn_kernel(delay_ref, turn_ref):
     trials, chans = delay_ref.shape
     dc, ds = cos_sin_turns(delay_ref[...].astype(F32) * (1.0 / TIME))
     c, s = dc, ds
     for k in range(HALF_BINS):
         rows = slice(k * trials, (k + 1) * trials)
-        for value, start in ((c, 0), (s, chans)):
-            high, low = split_bf16(value)
-            high_ref[rows, start : start + chans] = high
-            low_ref[rows, start : start + chans] = low
+        turn_ref[rows, :chans] = c.astype(BF16)
+        turn_ref[rows, chans:] = s.astype(BF16)
         c, s = c * dc - s * ds, c * ds + s * dc
 
 
-def plane_kernel(spec_ref, high_ref, low_ref, out_ref):
+def plane_kernel(spec_ref, turn_ref, out_ref, both_ref, part_ref):
     chans, width = spec_ref.shape
     _, _, trials = out_ref.shape
-    spec = spec_ref[...].astype(F32)
+    spec = spec_ref[...]
+    values = spec.astype(F32)
     lane = lax.broadcasted_iota(jnp.int32, (chans, width), 1)
-    is_real = lane % TIME < HALF_BINS
-    ahead = pltpu.roll(spec, width - HALF_BINS, 1)
-    behind = pltpu.roll(spec, HALF_BINS, 1)
-    turned = jnp.where(is_real, -ahead, behind)
-    both = jnp.concatenate([spec.astype(BF16), turned.astype(BF16)], axis=0)
+    ahead = pltpu.roll(values, width - HALF_BINS, 1)
+    behind = pltpu.roll(values, HALF_BINS, 1)
+    turned = jnp.where(lane % TIME < HALF_BINS, -ahead, behind)
+    both_ref[:chans] = spec
+    both_ref[chans:] = turned.astype(BF16)
     bin_id = lax.broadcasted_iota(jnp.int32, (trials, width), 1) % HALF_BINS
     plane = jnp.zeros((trials, width), F32)
-    for k in range(HALF_BINS):
-        rows = slice(k * trials, (k + 1) * trials)
-        part = jnp.dot(high_ref[rows], both, preferred_element_type=F32)
-        part = part + jnp.dot(low_ref[rows], both, preferred_element_type=F32)
-        plane = jnp.where(bin_id == k, part, plane)
+    group = HALF_BINS // 2
+    for first in range(0, HALF_BINS, group):
+        rows = slice(first * trials, (first + group) * trials)
+        part_ref[...] = jnp.dot(turn_ref[rows], both_ref[...], preferred_element_type=F32)
+        for k in range(group):
+            part = part_ref[k * trials : (k + 1) * trials]
+            plane = jnp.where(bin_id == first + k, part, plane)
     out_ref[...] = (plane.T * (1.0 / math.sqrt(CH))).reshape(out_ref.shape)
 
 
@@ -413,32 +446,72 @@
     )(x, gains, *state)
 
 
-def powers(own, far, pick, search, copies):
-    chans, rows, beams = own.shape
+def flat(shape):
+    return pl.BlockSpec(shape, lambda i: (0,) * len(shape))
+
+
+def cubes(block, *arrays):
+    return [pl.BlockSpec((block, *x.shape[1:]), lambda i: (i, 0, 0)) for x in arrays]
+
+
+def pick_far(sums, pick, search):
+    chans = sums[0].shape[0]
+    block = min(4, chans)
+    out = jax.ShapeDtypeStruct((2 * chans, TIME * search), BF16)
+    return pl.pallas_call(
+        far_pick_kernel,
+        out_shape=out,
+        grid=(chans // block,),
+        in_specs=cubes(block, *sums) + [flat(pick.shape)],
+        out_specs=flat(out.shape),
+        scratch_shapes=[pltpu.VMEM(out.shape, F32)],
+        compiler_params=PARAMS,
+        cost_estimate=pl.CostEstimate(
+            flops=1 << 30, bytes_accessed=2 << 20, transcendentals=0
+        ),
+        name="pick",
+    )(*sums, pick)
+
+
+def search_spectra(own, far, pick, search, copies, norm):
+    chans = own.shape[0]
     width = TIME * search
     table = time_table(search)
     high = jnp.asarray(table).astype(BF16)
     low = (jnp.asarray(table) - high.astype(F32)).astype(BF16)
     block = min(4, chans)
-    cube = pl.BlockSpec((block, rows, beams), lambda i: (i, 0, 0))
-    far_cubes = [pl.BlockSpec((block, rows, x.shape[2]), lambda i: (i, 0, 0)) for x in far]
-    flat = lambda shape: pl.BlockSpec(shape, lambda i: (0,) * len(shape))
-    return pl.pallas_call(
-        power_kernel,
-        out_shape=(
-            jax.ShapeDtypeStruct((chans, TIME, beams), F32),
-            jax.ShapeDtypeStruct((copies, chans, width), BF16),
-        ),
+    out = jax.ShapeDtypeStruct((copies, chans, width), BF16)
+    return pl.pallas_call(
+        functools.partial(spectrum_kernel, norm=norm),
+        out_shape=out,
         grid=(chans // block,),
-        in_specs=[cube, *far_cubes, flat(pick.shape), flat(high.shape), flat(low.shape)],
-        out_specs=(
-            pl.BlockSpec((block, TIME, beams), lambda i: (i, 0, 0)),
-            flat((copies, chans, width)),
-        ),
-        scratch_shapes=[pltpu.VMEM((chans, width), F32)],
-        compiler_params=PARAMS,
+        in_specs=cubes(block, own) + [flat(x.shape) for x in (far, pick, high, low)],
+        out_specs=flat(out.shape),
+        scratch_shapes=[pltpu.VMEM((2 * chans, width), F32)],
+        compiler_params=PARAMS,
+        cost_estimate=pl.CostEstimate(
+            flops=2 << 30, bytes_accessed=4 << 20, transcendentals=0
+        ),
+        name="spectrum",
+    )(own, far, pick, high, low)
+
+
+def powers(own, far, norm):
+    chans, _, beams = own.shape
+    block = min(4, chans)
+    out = jax.ShapeDtypeStruct((chans, TIME, beams), F32)
+    return pl.pallas_call(
+        functools.partial(power_kernel, norm=norm),
+        out_shape=out,
+        grid=(chans // block,),
+        in_specs=cubes(block, own, *far),
+        out_specs=cubes(block, out)[0],
+        compiler_params=PARAMS,
+        cost_estimate=pl.CostEstimate(
+            flops=1 << 28, bytes_accessed=5 << 20, transcendentals=0
+        ),
         name="power",
-    )(own, *far, pick, high, low)
+    )(own, *far)
 
 
 def on_device(voltages, gains, positions, directions, input_order, delays, search_beams):
@@ -482,27 +555,38 @@
 
     beams = directions.shape[1]
     cut = beams // 2
-    far_sums = []
-    for part in range(2):
-        sums = form_beams(far, far_gains, (dc, ds, far_c, far_s), part, cut, BF16)
-        far_sums.append(lax.ppermute(sums, "crate", partners))
+    norm = 1.0 / gains.shape[2]
+    far_state = (dc, ds, far_c, far_s)
+    sums0 = form_beams(far, far_gains, far_state, 0, cut, BF16)
+    far0 = lax.ppermute(sums0, "crate", partners)
+    sums1 = form_beams(far, far_gains, far_state, 1, cut, BF16)
+    picked = pick_far((sums0, sums1), pick, search)
+    picked = lax.ppermute(picked, "crate", partners)
+    far1 = lax.ppermute(sums1, "crate", partners)
     near_sums = form_beams(near, near_gains, (dc, ds, near_c, near_s), 0, beams, F32)
-
-    beam_power, spectrum = powers(near_sums, far_sums, pick, search, devices)
+    spectrum = search_spectra(near_sums, picked, pick, search, devices, norm)
+    near_sums, spectrum = lax.optimization_barrier((near_sums, spectrum))
     spectrum = lax.all_to_all(spectrum, "crate", split_axis=0, concat_axis=0, tiled=True)
+    beam_power = powers(near_sums, (far0, far1), norm)
     width = spectrum.shape[-1]
     trials = delays.shape[0] // devices
     own_delays = lax.dynamic_slice_in_dim(delays, position * trials, trials, 0)
-    turns = jax.ShapeDtypeStruct((HALF_BINS * trials, 2 * CH), BF16)
-    high, low = pl.pallas_call(
-        turn_kernel, out_shape=(turns, turns), compiler_params=PARAMS, name="turns"
+    turns = pl.pallas_call(
+        turn_kernel,
+        out_shape=jax.ShapeDtypeStruct((HALF_BINS * trials, 2 * CH), BF16),
+        compiler_params=PARAMS,
+        name="turns",
     )(own_delays)
     dm_plane = pl.pallas_call(
         plane_kernel,
-        out_shape=jax.ShapeDtypeStruct((search_beams.shape[0], TIME, trials), F32),
+        out_shape=jax.ShapeDtypeStruct((search, TIME, trials), F32),
+        scratch_shapes=[
+            pltpu.VMEM((2 * CH, width), BF16),
+            pltpu.VMEM((HALF_BINS // 2 * trials, width), F32),
+        ],
         compiler_params=PARAMS,
         name="plane",
-    )(spectrum.reshape(CH, width), high, low)
+    )(spectrum.reshape(CH, width), turns)
     return beam_power.transpose(0, 2, 1), dm_plane.transpose(2, 0, 1)
 
 

time: 158 us -> 157 us (level)
  waiting for transfers between devices: 50.4 us -> 42.3 us
  Pallas kernels: 75.6 us -> 78.7 us
  starting transfers between devices: 21.4 us -> 24.3 us
    ppermute x2 -> x3, waiting for transfers between devices: 18.6 us -> 13.9 us  [the longest x1 13.9 us: on_device(): picked = lax.ppermute(picked, 'crate', partners)]
    all_to_all x1, waiting for transfers between devices: 6.63 us -> 3.33 us  [on_device(): lax.all_to_all(spectrum, 'crate', split_axis=0, concat_axis=0, tiled=True)]
    pallas_call x3 -> x5, Pallas kernels: 13.5 us -> 16.7 us  [the longest x1 4.5 us: search_spectra(): pl.pallas_call(functools.partial(spectrum_kernel, norm=norm), out_shape=o...]
    ppermute x2 -> x3, starting transfers between devices: 3.4 us -> 6.32 us  [the longest x1 3.39 us: on_device(): far1 = lax.ppermute(sums1, 'crate', partners)]
    unnamed x16 -> x18, local copies, waits for them, and re-layouts: 2.7 us -> 3.3 us
  transfers between devices with their start and end apart: 6 -> 7, of which waited for: 5 -> 4; matrix products, arithmetic and copies ran while one was open for 4% -> 4% of each run, Pallas kernels for 35% -> 42%
where the time goes in v5:
time: 157 us; the launch traced here: 156 us
  Pallas kernels  78.7 us (50%)
  waiting for transfers between devices  42.3 us (27%)
  starting transfers between devices  24.3 us (15%)
  local copies, waits for them, and re-layouts  8.41 us (5%)
  other arithmetic  1.67 us (1%)
    pallas_call x3, Pallas kernels, form_beams(): pl.pallas_call(beam_kernel, out_shape=jax.ShapeDtypeStruct((chans, rows,...  35 us
    ppermute x1, waiting for transfers between devices, on_device(): far_gains = lax.ppermute(far_gains, 'crate', partners)  23.1 us
    ppermute x1, waiting for transfers between devices, on_device(): picked = lax.ppermute(picked, 'crate', partners)  13.9 us
    pallas_call x1, Pallas kernels, phasors(): pl.pallas_call(phasor_kernel, out_shape=[jax.ShapeDtypeStruct((total, bea...  11.7 us
    pallas_call x1, Pallas kernels, fold(): pl.pallas_call(fold_kernel, out_shape=(spectra, folded), grid_spec=pltpu....  9.39 us
    all_to_all x2, starting transfers between devices, exchange(): lax.all_to_all(x, 'crate', split_axis=0, concat_axis=0, axis_index_groups...  9.07 us
    all_to_all x1, starting transfers between devices, on_device(): lax.all_to_all(spectrum, 'crate', split_axis=0, concat_axis=0, tiled=True)  5.86 us
    pallas_call x1, Pallas kernels, more_spectra(): pl.pallas_call(spectra_kernel, out_shape=out, grid_spec=pltpu.PrefetchSca...  5.83 us
  transfers between devices with their start and end apart: 7, of which 4 were waited for; matrix products, arithmetic and copies ran while one was open for 4% of the time, Pallas kernels for 42%

profile of v5, /device:TPU:0, one launch (start us, length us, event | category | flops | bytes accessed | tf_op | source)
XLA Modules:
  0.0 156.2 jit_solution(16096980934532158485)
XLA Ops:
  0.7 9.4 %fold.1 = (bf16[8,16,64,128]{3,2,1,0:T(8,128)(2,1)}, bf16[4096,512]{1,0:T(8,128)(2,1)}) custom-call(s32[1]{0:T(128)S(6)} %sub.14.half_ref, bf16[128,17920]{1,0:T(8,128)(2,1)} %volt_ref.1, f32[4,512]{1,0:T(4,128)} %constant.66.clone.window_ref, bf16[512,512]{1,0:T(8,128)(2,1)} %constant.68.table_ref), custom_call_target="tpu_custom_call" | custom-call | flops 4294967296 | bytes 12582912 | tf_op jit(solution)/shard_map/fold/pallas_call | solution.py:344
  10.1 5.3 %all-to-all-start.1 = ((bf16[8,16,64,128]{3,2,1,0:T(8,128)(2,1)}), bf16[8,16,64,128]{3,2,1,0:T(8,128)(2,1)}, u32[]{:S(2)}, u32[]{:S(2)}) async-start(bf16[8,16,64,128]{3,2,1,0:T(8,128)(2,1)} %get-tuple-element.36), calls=%async_computation.1 | async-start | bytes 4194304 | tf_op jit(solution)/shard_map/all_to_all | solution.py:533
  15.4 5.8 %spectra.1 = bf16[8,16,64,128]{3,2,1,0:T(8,128)(2,1)} custom-call(s32[1]{0:T(128)} %bitcast.block_ref, bf16[4096,512]{1,0:T(8,128)(2,1)} %get-tuple-element.22.folded_ref, bf16[512,512]{1,0:T(8,128)(2,1)} %constant.68.table_ref), custom_call_target="tpu_custom_call" | custom-call | flops 2147483648 | bytes 6291456 | tf_op jit(solution)/shard_map/spectra/pallas_call | solution.py:370
  21.2 0.4 copy.12
  21.6 0.6 broadcast_in_dim_tile.3.pick_ref
  22.2 2.8 %gather_fusion = f32[1024,3]{1,0:T(8,128)S(1)} fusion(f32[2048,3]{1,0:T(8,128)S(1)} %bitcast.7, s32[1024]{0:T(1024)S(1)} %fusion), kind=kCustom, calls=%fused_computation | custom fusion | bytes 28672 | tf_op jit(solution)/shard_map/jit(_take)/gather | solution.py:544
  25.1 0.7 add_multiply_fusion.first_ref
  25.7 0.7 constant_dynamic-slice_fusion.1
  26.4 1.0 broadcast_select_fusion.place_ref
  27.4 11.7 %phasors.1 = (f32[1024,512]{1,0:T(8,128)}, f32[1024,512]{1,0:T(8,128)}, f32[1024,512]{1,0:T(8,128)}, f32[1024,512]{1,0:T(8,128)}, f32[1024,512]{1,0:T(8,128)}, /*index=5*/f32[1024,512]{1,0:T(8,128)}) custom-call(s32[2]{0:T(128)} %add_multiply_fusion.first_ref, f32[1024,3]{1,0:T(8,128)} %broadcast_select_fusion.place_ref, f32[3,512]{1,0:T(4,128)} %dir_ref.1), custom_call_target="tpu_custom_call" | custom-call | flops 4194304000 | bytes 12582912 | tf_op jit(solution)/shard_map/phasors/pallas_call | solution.py:395
  39.1 2.1 %all-to-all-done.1.x_ref = bf16[8,16,64,128]{3,2,1,0:T(8,128)(2,1)} async-done(((bf16[8,16,64,128]{3,2,1,0:T(8,128)(2,1)}), bf16[8,16,64,128]{3,2,1,0:T(8,128)(2,1)}, u32[]{:S(2)}, u32[]{:S(2)}) %all-to-all-start.1) | async-done | bytes 2097184 | tf_op jit(solution)/shard_map/all_to_all | solution.py:533
  41.2 3.8 %all-to-all-start = ((bf16[8,16,64,128]{3,2,1,0:T(8,128)(2,1)}), bf16[8,16,64,128]{3,2,1,0:T(8,128)(2,1)S(1)}, u32[]{:S(2)}, u32[]{:S(2)}) async-start(bf16[8,16,64,128]{3,2,1,0:T(8,128)(2,1)} %spectra.1), calls=%async_computation | async-start | bytes 4194304 | tf_op jit(solution)/shard_map/all_to_all | solution.py:533
  44.9 3.1 %collective-permute-start = (f32[16,2,1024]{2,1,0:T(2,128)S(1)}, f32[16,2,1024]{2,1,0:T(2,128)S(1)}, u32[]{:S(2)}, u32[]{:S(2)}) collective-permute-start(f32[16,2,1024]{2,1,0:T(2,128)S(1)} %get-tuple-element.42), channel_id=1, source_target_pairs={{0,8},{1,9},{2,10},{3,11},{4,12},{5,13},{6,14},{7,15},{8,0},{9,1},... | collective-permute-start | bytes 393224 | tf_op jit(solution)/shard_map/ppermute | solution.py:541
  48.0 23.1 %collective-permute-done.gain_ref = f32[16,2,1024]{2,1,0:T(2,128)S(1)} collective-permute-done((f32[16,2,1024]{2,1,0:T(2,128)S(1)}, f32[16,2,1024]{2,1,0:T(2,128)S(1)}, u32[]{:S(2)}, u32[]{:S(2)}) %collective-permute-start) | collective-permute-done | bytes 131104 | tf_op jit(solution)/shard_map/ppermute | solution.py:541
  71.1 0.6 copy-done.7
  71.7 9.4 %beams.5.sum1_ref = bf16[16,64,256]{2,1,0:T(8,128)(2,1)} custom-call(bf16[8,16,64,128]{3,2,1,0:T(8,128)(2,1)} %all-to-all-done.1.x_ref, f32[16,2,1024]{2,1,0:T(2,128)} %copy-done.7, f32[1024,512]{1,0:T(8,128)} %get-tuple-element.32.dc_ref, f32[1024,512]{1,0:T(8,128)} %get-tuple-element.33.ds_ref, f32[1024,512]{1,0:T(8,128)} %get-tuple-element.37.c_ref, ...), custom_call_target="tpu_custom_call" | custom-call | flops 4294967296 | bytes 12582912 | tf_op jit(solution)/shard_map/beams/pallas_call | solution.py:426
  81.1 3.4 %collective-permute-start.3 = (bf16[16,64,256]{2,1,0:T(8,128)(2,1)}, bf16[16,64,256]{2,1,0:T(8,128)(2,1)}, u32[]{:S(2)}, u32[]{:S(2)}) collective-permute-start(bf16[16,64,256]{2,1,0:T(8,128)(2,1)} %beams.5.sum1_ref), channel_id=1, source_target_pairs={{0,8},{1,9},{2,10},{3,11},{4,12},{5,13},{6,14},{7,15},{8,0},{9,1},... | collective-permute-start | bytes 1572872 | tf_op jit(solution)/shard_map/ppermute | solution.py:565
  84.5 9.3 %beams.4.sum0_ref = bf16[16,64,256]{2,1,0:T(8,128)(2,1)} custom-call(bf16[8,16,64,128]{3,2,1,0:T(8,128)(2,1)} %all-to-all-done.1.x_ref, f32[16,2,1024]{2,1,0:T(2,128)} %copy-done.7, f32[1024,512]{1,0:T(8,128)} %get-tuple-element.32.dc_ref, f32[1024,512]{1,0:T(8,128)} %get-tuple-element.33.ds_ref, f32[1024,512]{1,0:T(8,128)} %get-tuple-element.37.c_ref, ...), custom_call_target="tpu_custom_call" | custom-call | flops 4294967296 | bytes 12582912 | tf_op jit(solution)/shard_map/beams/pallas_call | solution.py:426
  93.8 3.3 %pick.1 = bf16[32,512]{1,0:T(8,128)(2,1)} custom-call(bf16[16,64,256]{2,1,0:T(8,128)(2,1)} %beams.4.sum0_ref, bf16[16,64,256]{2,1,0:T(8,128)(2,1)} %beams.5.sum1_ref, s32[1,128]{1,0:T(1,128)} %broadcast_in_dim_tile.3.pick_ref), custom_call_target="tpu_custom_call" | custom-call | flops 1073741824 | bytes 2097152 | tf_op jit(solution)/shard_map/pick/pallas_call | solution.py:461
  97.1 2.9 %collective-permute-start.1 = (bf16[32,512]{1,0:T(8,128)(2,1)}, bf16[32,512]{1,0:T(8,128)(2,1)S(1)}, u32[]{:S(2)}, u32[]{:S(2)}) collective-permute-start(bf16[32,512]{1,0:T(8,128)(2,1)} %pick.1), channel_id=1, source_target_pairs={{0,8},{1,9},{2,10},{3,11},{4,12},{5,13},{6,14},{7,15},{8,0},{9,1},... | collective-permute-start | bytes 98312 | tf_op jit(solution)/shard_map/ppermute | solution.py:564
  100.1 1.3 copy-done.1
  101.4 16.3 %beams.3.own_ref = f32[16,64,512]{2,1,0:T(8,128)} custom-call(bf16[8,16,64,128]{3,2,1,0:T(8,128)(2,1)} %copy-done.1, f32[16,2,1024]{2,1,0:T(2,128)} %get-tuple-element.31.gain_ref, f32[1024,512]{1,0:T(8,128)} %get-tuple-element.32.dc_ref, f32[1024,512]{1,0:T(8,128)} %get-tuple-element.33.ds_ref, f32[1024,512]{1,0:T(8,128)} %get-tuple-element.34.c_ref, ...), custom_call_target="tpu_custom_call" | custom-call | flops 8589934592 | bytes 12582912 | tf_op jit(solution)/shard_map/beams/pallas_call | solution.py:426
  117.7 13.9 %collective-permute-done.1.far_ref = bf16[32,512]{1,0:T(8,128)(2,1)S(1)} collective-permute-done((bf16[32,512]{1,0:T(8,128)(2,1)}, bf16[32,512]{1,0:T(8,128)(2,1)S(1)}, u32[]{:S(2)}, u32[]{:S(2)}) %collective-permute-start.1) | collective-permute-done | bytes 32800 | tf_op jit(solution)/shard_map/ppermute | solution.py:564
  131.6 0.6 copy-done.8
  132.2 4.5 %spectrum.1 = bf16[16,16,512]{2,1,0:T(8,128)(2,1)} custom-call(f32[16,64,512]{2,1,0:T(8,128)} %beams.3.own_ref, bf16[32,512]{1,0:T(8,128)(2,1)} %copy-done.8, s32[1,128]{1,0:T(1,128)} %broadcast_in_dim_tile.3.pick_ref, bf16[512,512]{1,0:T(8,128)(2,1)} %constant.69.high_ref, bf16[512,512]{1,0:T(8,128)(2,1)} %constant.72.low_ref), custom_call_target="tpu_custom_call" | custom-call | flops 2147483648 | bytes 4194304 | tf_op jit(solution)/shard_map/spectrum/pallas_call | solution.py:484
  136.7 5.9 %all-to-all-start.2 = ((bf16[16,16,512]{2,1,0:T(8,128)(2,1)}), bf16[16,16,512]{2,1,0:T(8,128)(2,1)S(1)}, u32[]{:S(2)}, u32[]{:S(2)}) async-start(bf16[16,16,512]{2,1,0:T(8,128)(2,1)} %spectrum.1), calls=%async_computation.2 | async-start | bytes 524288 | tf_op jit(solution)/shard_map/all_to_all | solution.py:569
  142.6 0.6 constant_dynamic-slice_fusion.delay_ref
  143.2 2.2 %turns.1.turn_ref = bf16[1024,512]{1,0:T(8,128)(2,1)} custom-call(s32[64,256]{1,0:T(8,128)} %constant_dynamic-slice_fusion.delay_ref), custom_call_target="tpu_custom_call" | custom-call | tf_op jit(solution)/shard_map/turns/pallas_call | solution.py:574
  145.4 3.8 %power.1 = f32[16,32,512]{2,1,0:T(8,128)} custom-call(f32[16,64,512]{2,1,0:T(8,128)} %beams.3.own_ref, bf16[16,64,256]{2,1,0:T(8,128)(2,1)} %collective-permute-done.2.far0_ref, bf16[16,64,256]{2,1,0:T(8,128)(2,1)} %collective-permute-done.3.far1_ref), custom_call_target="tpu_custom_call" | custom-call | flops 268435456 | bytes 5242880 | tf_op jit(solution)/shard_map/power/pallas_call | solution.py:503
  149.3 3.3 %all-to-all-done.2 = bf16[16,16,512]{2,1,0:T(8,128)(2,1)S(1)} async-done(((bf16[16,16,512]{2,1,0:T(8,128)(2,1)}), bf16[16,16,512]{2,1,0:T(8,128)(2,1)S(1)}, u32[]{:S(2)}, u32[]{:S(2)}) %all-to-all-start.2) | async-done | bytes 262176 | tf_op jit(solution)/shard_map/all_to_all | solution.py:569
  152.6 0.7 copy-done.2
  153.3 2.9 %plane.1 = f32[16,32,64]{2,1,0:T(8,128)} custom-call(bf16[256,512]{1,0:T(8,128)(2,1)} %bitcast.8, bf16[1024,512]{1,0:T(8,128)(2,1)} %turns.1.turn_ref), custom_call_target="tpu_custom_call" | custom-call | tf_op jit(solution)/shard_map/plane/pallas_call | solution.py:580
  (21 shorter events, 0.1 us)
Async XLA Ops:
  0.6 141.9 %copy-start = (s32[1024,256]{1,0:T(8,128)S(1)}, s32[1024,256]{1,0:T(8,128)}, u32[]{:S(2)}) copy-start(s32[1024,256]{1,0:T(8,128)} %param.15) | copy-start | bytes 3145732
  10.1 31.1 %all-to-all-start.1 = ((bf16[8,16,64,128]{3,2,1,0:T(8,128)(2,1)}), bf16[8,16,64,128]{3,2,1,0:T(8,128)(2,1)}, u32[]{:S(2)}, u32[]{:S(2)}) async-start(bf16[8,16,64,128]{3,2,1,0:T(8,128)(2,1)} %get-tuple-element.36), calls=%async_computation.1 | async-start | bytes 4194304 | tf_op jit(solution)/shard_map/all_to_all | solution.py:533
  15.3 5.9 %copy-start.4 = (f32[3,2048]{1,0:T(4,128)S(1)}, f32[3,2048]{1,0:T(4,128)}, u32[]{:S(2)}) copy-start(f32[3,2048]{1,0:T(4,128)} %param.12) | copy-start | bytes 73732
  15.3 6.2 %copy-start.6 = (s32[16]{0:T(128)S(1)}, s32[16]{0:T(128)}, u32[]{:S(2)}) copy-start(s32[16]{0:T(128)} %param.16) | copy-start | bytes 196
  15.4 6.9 %copy-start.5 = (s32[2048]{0:T(1024)S(1)}, s32[2048]{0:T(1024)}, u32[]{:S(2)}) copy-start(s32[2048]{0:T(1024)} %param.14) | copy-start | bytes 24580
  22.2 3.5 %copy-start.3 = (f32[16,2,2048]{2,1,0:T(2,128)S(1)}, f32[16,2,2048]{2,1,0:T(2,128)}, u32[]{:S(2)}) copy-start(f32[16,2,2048]{2,1,0:T(2,128)} %param.11) | copy-start | bytes 786436
  41.2 58.9 %all-to-all-start = ((bf16[8,16,64,128]{3,2,1,0:T(8,128)(2,1)}), bf16[8,16,64,128]{3,2,1,0:T(8,128)(2,1)S(1)}, u32[]{:S(2)}, u32[]{:S(2)}) async-start(bf16[8,16,64,128]{3,2,1,0:T(8,128)(2,1)} %spectra.1), calls=%async_computation | async-start | bytes 4194304 | tf_op jit(solution)/shard_map/all_to_all | solution.py:533
  44.9 26.2 %collective-permute-start = (f32[16,2,1024]{2,1,0:T(2,128)S(1)}, f32[16,2,1024]{2,1,0:T(2,128)S(1)}, u32[]{:S(2)}, u32[]{:S(2)}) collective-permute-start(f32[16,2,1024]{2,1,0:T(2,128)S(1)} %get-tuple-element.42), channel_id=1, source_target_pairs={{0,8},{1,9},{2,10},{3,11},{4,12},{5,13},{6,14},{7,15},{8,0},{9,1},... | collective-permute-start | bytes 393224 | tf_op jit(solution)/shard_map/ppermute | solution.py:541
  71.1 0.6 copy-start.7
  81.1 64.3 %collective-permute-start.3 = (bf16[16,64,256]{2,1,0:T(8,128)(2,1)}, bf16[16,64,256]{2,1,0:T(8,128)(2,1)}, u32[]{:S(2)}, u32[]{:S(2)}) collective-permute-start(bf16[16,64,256]{2,1,0:T(8,128)(2,1)} %beams.5.sum1_ref), channel_id=1, source_target_pairs={{0,8},{1,9},{2,10},{3,11},{4,12},{5,13},{6,14},{7,15},{8,0},{9,1},... | collective-permute-start | bytes 1572872 | tf_op jit(solution)/shard_map/ppermute | solution.py:565
  93.8 51.6 %collective-permute-start.2 = (bf16[16,64,256]{2,1,0:T(8,128)(2,1)}, bf16[16,64,256]{2,1,0:T(8,128)(2,1)}, u32[]{:S(2)}, u32[]{:S(2)}) collective-permute-start(bf16[16,64,256]{2,1,0:T(8,128)(2,1)} %beams.4.sum0_ref), channel_id=1, source_target_pairs={{0,8},{1,9},{2,10},{3,11},{4,12},{5,13},{6,14},{7,15},{8,0},{9,1},... | collective-permute-start | bytes 1572872 | tf_op jit(solution)/shard_map/ppermute | solution.py:561
  97.1 34.5 %collective-permute-start.1 = (bf16[32,512]{1,0:T(8,128)(2,1)}, bf16[32,512]{1,0:T(8,128)(2,1)S(1)}, u32[]{:S(2)}, u32[]{:S(2)}) collective-permute-start(bf16[32,512]{1,0:T(8,128)(2,1)} %pick.1), channel_id=1, source_target_pairs={{0,8},{1,9},{2,10},{3,11},{4,12},{5,13},{6,14},{7,15},{8,0},{9,1},... | collective-permute-start | bytes 98312 | tf_op jit(solution)/shard_map/ppermute | solution.py:564
  100.1 1.3 copy-start.1
  131.6 0.6 copy-start.8
  136.7 15.9 %all-to-all-start.2 = ((bf16[16,16,512]{2,1,0:T(8,128)(2,1)}), bf16[16,16,512]{2,1,0:T(8,128)(2,1)S(1)}, u32[]{:S(2)}, u32[]{:S(2)}) async-start(bf16[16,16,512]{2,1,0:T(8,128)(2,1)} %spectrum.1), calls=%async_computation.2 | async-start | bytes 524288 | tf_op jit(solution)/shard_map/all_to_all | solution.py:569
  152.6 0.7 copy-start.2

commit v6 on v5

--- a/solution.py
+++ b/solution.py
@@ -135,8 +135,8 @@
     transform_rows(table_ref[...], folded_ref, spread_ref, out_ref)
 
 
-def phasor_kernel(first_ref, place_ref, dir_ref, dc_ref, ds_ref, *start_refs):
-    depth, beams = dc_ref.shape
+def phasor_kernel(first_ref, place_ref, dir_ref, *out_refs):
+    depth, beams = out_refs[0].shape
     wide = 256
 
     def block(index, carry):
@@ -148,11 +148,10 @@
             geometry = place[:, 0:1] * direction[0:1, :]
             geometry = geometry + place[:, 1:2] * direction[1:2, :]
             geometry = geometry + place[:, 2:3] * direction[2:3, :]
-            dc_ref[rows, lanes], ds_ref[rows, lanes] = cos_sin_turns(geometry * (1.0 / CH))
-            for k in range(len(start_refs) // 2):
-                first = 1.0 + first_ref[k].astype(F32) * (1.0 / CH)
-                c, s = cos_sin_turns(geometry * first)
-                start_refs[2 * k][rows, lanes], start_refs[2 * k + 1][rows, lanes] = c, s
+            first = 1.0 + first_ref[0].astype(F32) * (1.0 / CH)
+            for k, scale in enumerate((first, 1.0 / CH)[: len(out_refs) // 2]):
+                c, s = cos_sin_turns(geometry * scale)
+                out_refs[2 * k][rows, lanes], out_refs[2 * k + 1][rows, lanes] = c, s
         return carry
 
     lax.fori_loop(0, depth // 16, block, 0, unroll=2)
@@ -248,12 +247,11 @@
     return chosen
 
 
-def far_pick_kernel(sum0_ref, sum1_ref, pick_ref, out_ref, picked_ref):
+def far_pick_kernel(sum_ref, pick_ref, out_ref, picked_ref):
     step = pl.program_id(0)
-    block = sum0_ref.shape[0]
+    block = sum_ref.shape[0]
     search = out_ref.shape[1] // TIME
-    both = jnp.concatenate([sum0_ref[...], sum1_ref[...]], axis=2)
-    rows = both.reshape(block * 2 * TIME, both.shape[2])
+    rows = sum_ref[...].reshape(block * 2 * TIME, sum_ref.shape[2])
     half = picked_ref.shape[0] // 2
     for k, row in enumerate(pick_beams(rows, pick_ref, 2 * block, search)):
         place = (k % 2) * half + step * block + k // 2
@@ -289,9 +287,8 @@
             spec_ref[dest] = spectrum
 
 
-def power_kernel(own_ref, far0_ref, far1_ref, power_ref, norm):
-    far = jnp.concatenate([far0_ref[...], far1_ref[...]], axis=2)
-    total = own_ref[...] + far.astype(F32)
+def power_kernel(own_ref, far_ref, power_ref, norm):
+    total = own_ref[...] + far_ref[...].astype(F32)
     real, imag = total[:, :TIME], total[:, TIME:]
     power_ref[...] = (real * real + imag * imag) * norm
 
@@ -330,7 +327,8 @@
     out_ref[...] = (plane.T * (1.0 / math.sqrt(CH))).reshape(out_ref.shape)
 
 
-PARAMS = pltpu.CompilerParams(vmem_limit_bytes=60 << 20)
+SMALL = pltpu.CompilerParams(vmem_limit_bytes=12 << 20)
+LARGE = pltpu.CompilerParams(vmem_limit_bytes=60 << 20)
 
 
 def fold(voltages, table, block_id, dests, chans):
@@ -355,7 +353,7 @@
             out_specs=(whole(spectra), whole(folded)),
             scratch_shapes=[pltpu.VMEM((rows * PITCH, inputs), F32)],
         ),
-        compiler_params=PARAMS,
+        compiler_params=LARGE,
         cost_estimate=pl.CostEstimate(
             flops=8 * rows * FFTLEN * TIME * inputs, bytes_accessed=12 << 20, transcendentals=0
         ),
@@ -380,7 +378,7 @@
             out_specs=pl.BlockSpec(out.shape, lambda i, k: (0, 0, 0, 0)),
             scratch_shapes=[pltpu.VMEM((rows * PITCH, inputs), F32)],
         ),
-        compiler_params=PARAMS,
+        compiler_params=LARGE,
         cost_estimate=pl.CostEstimate(
             flops=4 * rows * FFTLEN * TIME * inputs, bytes_accessed=6 << 20, transcendentals=0
         ),
@@ -388,10 +386,9 @@
     )(block_id, folded, table)
 
 
-def phasors(firsts, places, directions):
+def phasors(first, places, directions, count):
     total, beams = places.shape[0], directions.shape[1]
     depth = 128
-    count = 2 + 2 * firsts.shape[0]
     return pl.pallas_call(
         phasor_kernel,
         out_shape=[jax.ShapeDtypeStruct((total, beams), F32)] * count,
@@ -404,15 +401,15 @@
             ],
             out_specs=[pl.BlockSpec((depth, beams), lambda i, f: (i, 0))] * count,
         ),
-        compiler_params=PARAMS,
+        compiler_params=LARGE,
         cost_estimate=pl.CostEstimate(
             flops=8000 * total * beams, bytes_accessed=count * 4 * total * beams, transcendentals=0
         ),
         name="phasors",
-    )(firsts, places, directions)
-
-
-def form_beams(x, gains, state, start, beams, out_type):
+    )(first, places, directions)
+
+
+def form_beams(x, gains, state, beams, out_type):
     sources, chans, rows, inputs = x.shape
     total = sources * inputs
     if inputs != 128:
@@ -422,7 +419,7 @@
     blocks = depth // 128
     tiles = total // depth
     late = lambda i: jnp.maximum(i - 1, 0)
-    state_spec = pl.BlockSpec((depth, beams), lambda i: (jnp.minimum(i, tiles - 1), start))
+    state_spec = pl.BlockSpec((depth, beams), lambda i: (jnp.minimum(i, tiles - 1), 0))
     return pl.pallas_call(
         beam_kernel,
         out_shape=jax.ShapeDtypeStruct((chans, rows, beams), out_type),
@@ -438,7 +435,7 @@
             pltpu.VMEM((chans, 2 * depth, beams), BF16),
             pltpu.VMEM((chans, rows, beams), F32),
         ],
-        compiler_params=PARAMS,
+        compiler_params=LARGE,
         cost_estimate=pl.CostEstimate(
             flops=16 * chans * rows * total * beams, bytes_accessed=12 << 20, transcendentals=0
         ),
@@ -455,22 +452,22 @@
 
 
 def pick_far(sums, pick, search):
-    chans = sums[0].shape[0]
+    chans = sums.shape[0]
     block = min(4, chans)
     out = jax.ShapeDtypeStruct((2 * chans, TIME * search), BF16)
     return pl.pallas_call(
         far_pick_kernel,
         out_shape=out,
         grid=(chans // block,),
-        in_specs=cubes(block, *sums) + [flat(pick.shape)],
+        in_specs=cubes(block, sums) + [flat(pick.shape)],
         out_specs=flat(out.shape),
         scratch_shapes=[pltpu.VMEM(out.shape, F32)],
-        compiler_params=PARAMS,
+        compiler_params=LARGE,
         cost_estimate=pl.CostEstimate(
             flops=1 << 30, bytes_accessed=2 << 20, transcendentals=0
         ),
         name="pick",
-    )(*sums, pick)
+    )(sums, pick)
 
 
 def search_spectra(own, far, pick, search, copies, norm):
@@ -488,7 +485,7 @@
         in_specs=cubes(block, own) + [flat(x.shape) for x in (far, pick, high, low)],
         out_specs=flat(out.shape),
         scratch_shapes=[pltpu.VMEM((2 * chans, width), F32)],
-        compiler_params=PARAMS,
+        compiler_params=LARGE,
         cost_estimate=pl.CostEstimate(
             flops=2 << 30, bytes_accessed=4 << 20, transcendentals=0
         ),
@@ -504,14 +501,14 @@
         functools.partial(power_kernel, norm=norm),
         out_shape=out,
         grid=(chans // block,),
-        in_specs=cubes(block, own, *far),
+        in_specs=cubes(block, own, far),
         out_specs=cubes(block, out)[0],
-        compiler_params=PARAMS,
+        compiler_params=LARGE,
         cost_estimate=pl.CostEstimate(
             flops=1 << 28, bytes_accessed=5 << 20, transcendentals=0
         ),
         name="power",
-    )(own, *far)
+    )(own, far)
 
 
 def on_device(voltages, gains, positions, directions, input_order, delays, search_beams):
@@ -544,37 +541,35 @@
     places = jnp.take(positions.T, order, axis=0)
     search = search_beams.shape[0]
     pick = jnp.tile(search_beams, 128 // search)[None, :]
-    firsts = jnp.stack([(position + per_half) % devices, position]) * chans
-    dc, ds, far_c, far_s, near_c, near_s = phasors(
-        firsts.astype(jnp.int32), places, directions
-    )
-    near, near_gains, pick, dc, ds, far_c, far_s = lax.optimization_barrier(
-        (near, near_gains, pick, dc, ds, far_c, far_s)
+    own_first = (position * chans).astype(jnp.int32).reshape(1)
+    far_first = ((position + per_half) % devices * chans).astype(jnp.int32).reshape(1)
+    far_c, far_s, dc, ds = phasors(far_first, places, directions, 4)
+    near, near_gains, pick, own_first, dc, ds, far_c, far_s = lax.optimization_barrier(
+        (near, near_gains, pick, own_first, dc, ds, far_c, far_s)
     )
     near = exchange(near)
 
     beams = directions.shape[1]
-    cut = beams // 2
     norm = 1.0 / gains.shape[2]
-    far_state = (dc, ds, far_c, far_s)
-    sums0 = form_beams(far, far_gains, far_state, 0, cut, BF16)
-    far0 = lax.ppermute(sums0, "crate", partners)
-    sums1 = form_beams(far, far_gains, far_state, 1, cut, BF16)
-    picked = pick_far((sums0, sums1), pick, search)
-    picked = lax.ppermute(picked, "crate", partners)
-    far1 = lax.ppermute(sums1, "crate", partners)
-    near_sums = form_beams(near, near_gains, (dc, ds, near_c, near_s), 0, beams, F32)
-    spectrum = search_spectra(near_sums, picked, pick, search, devices, norm)
+    sums = form_beams(far, far_gains, (dc, ds, far_c, far_s), beams, BF16)
+    picked = pick_far(sums, pick, search)
+    far_picked = lax.ppermute(picked, "crate", partners)
+    far_sums = lax.ppermute(sums, "crate", partners)
+    own_first, picked = lax.optimization_barrier((own_first, picked))
+    near_c, near_s = phasors(own_first, places, directions, 2)
+    near_sums = form_beams(near, near_gains, (dc, ds, near_c, near_s), beams, F32)
+
+    spectrum = search_spectra(near_sums, far_picked, pick, search, devices, norm)
     near_sums, spectrum = lax.optimization_barrier((near_sums, spectrum))
     spectrum = lax.all_to_all(spectrum, "crate", split_axis=0, concat_axis=0, tiled=True)
-    beam_power = powers(near_sums, (far0, far1), norm)
+    beam_power = powers(near_sums, far_sums, norm)
     width = spectrum.shape[-1]
     trials = delays.shape[0] // devices
     own_delays = lax.dynamic_slice_in_dim(delays, position * trials, trials, 0)
     turns = pl.pallas_call(
         turn_kernel,
         out_shape=jax.ShapeDtypeStruct((HALF_BINS * trials, 2 * CH), BF16),
-        compiler_params=PARAMS,
+        compiler_params=LARGE,
         name="turns",
     )(own_delays)
     dm_plane = pl.pallas_call(
@@ -584,7 +579,7 @@
             pltpu.VMEM((2 * CH, width), BF16),
             pltpu.VMEM((HALF_BINS // 2 * trials, width), F32),
         ],
-        compiler_params=PARAMS,
+        compiler_params=SMALL,
         name="plane",
     )(spectrum.reshape(CH, width), turns)
     return beam_power.transpose(0, 2, 1), dm_plane.transpose(2, 0, 1)

time: 157 us -> 167 us (1.064)
  waiting for transfers between devices: 42.3 us -> 54.5 us
  starting transfers between devices: 24.3 us -> 21.2 us
    pallas_call x1 -> x2, Pallas kernels: 11.7 us -> 16.7 us  [phasors(): pl.pallas_call(phasor_kernel, out_shape=[jax.ShapeDtypeStruct((total, bea...]
    ppermute x3 -> x2, waiting for transfers between devices: 13.9 us -> 18.7 us  [the longest x1 18.7 us: on_device(): far_picked = lax.ppermute(picked, 'crate', partners)]
    all_to_all x1, waiting for transfers between devices: 3.33 us -> 7.18 us  [on_device(): lax.all_to_all(spectrum, 'crate', split_axis=0, concat_axis=0, tiled=True)]
    all_to_all x2, waiting for transfers between devices: 2.06 us -> 5.42 us  [exchange(): lax.all_to_all(x, 'crate', split_axis=0, concat_axis=0, axis_index_groups...]
    ppermute x3 -> x2, starting transfers between devices: 6.32 us -> 3.39 us  [the longest x1 3.38 us: on_device(): far_sums = lax.ppermute(sums, 'crate', partners)]
    pallas_call x3 -> x2, Pallas kernels: 35 us -> 32.3 us  [form_beams(): pl.pallas_call(beam_kernel, out_shape=jax.ShapeDtypeStruct((chans, rows,...]
  transfers between devices with their start and end apart: 7 -> 6, of which waited for: 4 -> 4; matrix products, arithmetic and copies ran while one was open for 4% -> 4% of each run, Pallas kernels for 42% -> 40%
where the time goes in v6:
time: 167 us; the launch traced here: 166 us
  Pallas kernels  79.6 us (48%)
  waiting for transfers between devices  54.5 us (33%)
  starting transfers between devices  21.2 us (13%)
  local copies, waits for them, and re-layouts  8.88 us (5%)
    pallas_call x2, Pallas kernels, form_beams(): pl.pallas_call(beam_kernel, out_shape=jax.ShapeDtypeStruct((chans, rows,...  32.3 us
    ppermute x1, waiting for transfers between devices, on_device(): far_gains = lax.ppermute(far_gains, 'crate', partners)  23.2 us
    ppermute x1, waiting for transfers between devices, on_device(): far_picked = lax.ppermute(picked, 'crate', partners)  18.7 us
    pallas_call x2, Pallas kernels, phasors(): pl.pallas_call(phasor_kernel, out_shape=[jax.ShapeDtypeStruct((total, bea...  16.7 us
    pallas_call x1, Pallas kernels, fold(): pl.pallas_call(fold_kernel, out_shape=(spectra, folded), grid_spec=pltpu....  9.41 us
    all_to_all x2, starting transfers between devices, exchange(): lax.all_to_all(x, 'crate', split_axis=0, concat_axis=0, axis_index_groups...  9.02 us
    all_to_all x1, waiting for transfers between devices, on_device(): lax.all_to_all(spectrum, 'crate', split_axis=0, concat_axis=0, tiled=True)  7.18 us
    pallas_call x1, Pallas kernels, more_spectra(): pl.pallas_call(spectra_kernel, out_shape=out, grid_spec=pltpu.PrefetchSca...  5.82 us
  transfers between devices with their start and end apart: 6, of which 4 were waited for; matrix products, arithmetic and copies ran while one was open for 4% of the time, Pallas kernels for 40%

profile of v6, /device:TPU:0, one launch (start us, length us, event | category | flops | bytes accessed | tf_op | source)
XLA Modules:
  0.0 166.0 jit_solution(11607653207299839423)
XLA Ops:
  0.6 0.0 copy-start
  0.7 9.4 %fold.1 = (bf16[8,16,64,128]{3,2,1,0:T(8,128)(2,1)}, bf16[4096,512]{1,0:T(8,128)(2,1)}) custom-call(s32[1]{0:T(128)S(6)} %sub.14.half_ref, bf16[128,17920]{1,0:T(8,128)(2,1)} %volt_ref.1, f32[4,512]{1,0:T(4,128)} %constant.65.clone.window_ref, bf16[512,512]{1,0:T(8,128)(2,1)} %constant.67.table_ref), custom_call_target="tpu_custom_call" | custom-call | flops 4294967296 | bytes 12582912 | tf_op jit(solution)/shard_map/fold/pallas_call | solution.py:342
  10.1 5.4 %all-to-all-start.1 = ((bf16[8,16,64,128]{3,2,1,0:T(8,128)(2,1)}), bf16[8,16,64,128]{3,2,1,0:T(8,128)(2,1)}, u32[]{:S(2)}, u32[]{:S(2)}) async-start(bf16[8,16,64,128]{3,2,1,0:T(8,128)(2,1)} %get-tuple-element.37), calls=%async_computation.1 | async-start | bytes 4194304 | tf_op jit(solution)/shard_map/all_to_all | solution.py:530
  15.5 0.6 broadcast_in_dim_tile.3.pick_ref
  16.1 5.8 %spectra.1 = bf16[8,16,64,128]{3,2,1,0:T(8,128)(2,1)} custom-call(s32[1]{0:T(128)} %bitcast.block_ref, bf16[4096,512]{1,0:T(8,128)(2,1)} %get-tuple-element.24.folded_ref, bf16[512,512]{1,0:T(8,128)(2,1)} %constant.67.table_ref), custom_call_target="tpu_custom_call" | custom-call | flops 2147483648 | bytes 6291456 | tf_op jit(solution)/shard_map/spectra/pallas_call | solution.py:368
  21.9 0.4 copy.12
  22.3 0.0 copy-start.3
  22.3 2.8 %gather_fusion = f32[1024,3]{1,0:T(8,128)S(1)} fusion(f32[2048,3]{1,0:T(8,128)S(1)} %bitcast.8, s32[1024]{0:T(1024)S(1)} %fusion), kind=kCustom, calls=%fused_computation | custom fusion | bytes 28672 | tf_op jit(solution)/shard_map/jit(_take)/gather | solution.py:541
  25.2 0.7 constant_dynamic-slice_fusion.1
  25.9 1.0 broadcast_select_fusion.place_ref
  26.9 9.0 %phasors.2 = (f32[1024,512]{1,0:T(8,128)}, f32[1024,512]{1,0:T(8,128)}, f32[1024,512]{1,0:T(8,128)}, f32[1024,512]{1,0:T(8,128)}) custom-call(s32[1]{0:T(128)} %bitcast.2.first_ref, f32[1024,3]{1,0:T(8,128)} %broadcast_select_fusion.place_ref, f32[3,512]{1,0:T(4,128)} %dir_ref.3), custom_call_target="tpu_custom_call" | custom-call | flops 4194304000 | bytes 8388608 | tf_op jit(solution)/shard_map/phasors/pallas_call | solution.py:392
  35.9 5.4 %all-to-all-done.1.x_ref = bf16[8,16,64,128]{3,2,1,0:T(8,128)(2,1)} async-done(((bf16[8,16,64,128]{3,2,1,0:T(8,128)(2,1)}), bf16[8,16,64,128]{3,2,1,0:T(8,128)(2,1)}, u32[]{:S(2)}, u32[]{:S(2)}) %all-to-all-start.1) | async-done | bytes 2097184 | tf_op jit(solution)/shard_map/all_to_all | solution.py:530
  41.3 3.6 %all-to-all-start = ((bf16[8,16,64,128]{3,2,1,0:T(8,128)(2,1)}), bf16[8,16,64,128]{3,2,1,0:T(8,128)(2,1)S(1)}, u32[]{:S(2)}, u32[]{:S(2)}) async-start(bf16[8,16,64,128]{3,2,1,0:T(8,128)(2,1)} %spectra.1), calls=%async_computation | async-start | bytes 4194304 | tf_op jit(solution)/shard_map/all_to_all | solution.py:530
  44.9 3.1 %collective-permute-start = (f32[16,2,1024]{2,1,0:T(2,128)S(1)}, f32[16,2,1024]{2,1,0:T(2,128)S(1)}, u32[]{:S(2)}, u32[]{:S(2)}) collective-permute-start(f32[16,2,1024]{2,1,0:T(2,128)S(1)} %get-tuple-element.46), channel_id=1, source_target_pairs={{0,8},{1,9},{2,10},{3,11},{4,12},{5,13},{6,14},{7,15},{8,0},{9,1},... | collective-permute-start | bytes 393224 | tf_op jit(solution)/shard_map/ppermute | solution.py:538
  48.0 23.2 %collective-permute-done.gain_ref = f32[16,2,1024]{2,1,0:T(2,128)S(1)} collective-permute-done((f32[16,2,1024]{2,1,0:T(2,128)S(1)}, f32[16,2,1024]{2,1,0:T(2,128)S(1)}, u32[]{:S(2)}, u32[]{:S(2)}) %collective-permute-start) | collective-permute-done | bytes 131104 | tf_op jit(solution)/shard_map/ppermute | solution.py:538
  71.3 0.7 copy-done.7
  71.9 16.0 %beams.2.sum_ref = bf16[16,64,512]{2,1,0:T(8,128)(2,1)} custom-call(bf16[8,16,64,128]{3,2,1,0:T(8,128)(2,1)} %all-to-all-done.1.x_ref, f32[16,2,1024]{2,1,0:T(2,128)} %copy-done.7, f32[1024,512]{1,0:T(8,128)} %get-tuple-element.34.dc_ref, f32[1024,512]{1,0:T(8,128)} %get-tuple-element.35.ds_ref, f32[1024,512]{1,0:T(8,128)} %get-tuple-element.38.c_ref, ...), custom_call_target="tpu_custom_call" | custom-call | flops 8589934592 | bytes 12582912 | tf_op jit(solution)/shard_map/beams/pallas_call | solution.py:423
  87.9 3.4 %collective-permute-start.2 = (bf16[16,64,512]{2,1,0:T(8,128)(2,1)}, bf16[16,64,512]{2,1,0:T(8,128)(2,1)}, u32[]{:S(2)}, u32[]{:S(2)}) collective-permute-start(bf16[16,64,512]{2,1,0:T(8,128)(2,1)} %beams.2.sum_ref), channel_id=1, source_target_pairs={{0,8},{1,9},{2,10},{3,11},{4,12},{5,13},{6,14},{7,15},{8,0},{9,1},... | collective-permute-start | bytes 3145736 | tf_op jit(solution)/shard_map/ppermute | solution.py:557
  91.2 3.3 %pick.1 = bf16[32,512]{1,0:T(8,128)(2,1)} custom-call(bf16[16,64,512]{2,1,0:T(8,128)(2,1)} %beams.2.sum_ref, s32[1,128]{1,0:T(1,128)} %broadcast_in_dim_tile.3.pick_ref), custom_call_target="tpu_custom_call" | custom-call | flops 1073741824 | bytes 2097152 | tf_op jit(solution)/shard_map/pick/pallas_call | solution.py:458
  94.5 7.6 %phasors.3 = (f32[1024,512]{1,0:T(8,128)}, f32[1024,512]{1,0:T(8,128)}) custom-call(s32[1]{0:T(128)} %bitcast.1.first_ref, f32[1024,3]{1,0:T(8,128)} %broadcast_select_fusion.place_ref, f32[3,512]{1,0:T(4,128)} %dir_ref.3), custom_call_target="tpu_custom_call" | custom-call | flops 4194304000 | bytes 4194304 | tf_op jit(solution)/shard_map/phasors/pallas_call | solution.py:392
  102.1 1.3 copy-done.2
  103.5 16.3 %beams.3.own_ref = f32[16,64,512]{2,1,0:T(8,128)} custom-call(bf16[8,16,64,128]{3,2,1,0:T(8,128)(2,1)} %copy-done.2, f32[16,2,1024]{2,1,0:T(2,128)} %get-tuple-element.33.gain_ref, f32[1024,512]{1,0:T(8,128)} %get-tuple-element.34.dc_ref, f32[1024,512]{1,0:T(8,128)} %get-tuple-element.35.ds_ref, f32[1024,512]{1,0:T(8,128)} %get-tuple-element.42.c_ref, ...), custom_call_target="tpu_custom_call" | custom-call | flops 8589934592 | bytes 12582912 | tf_op jit(solution)/shard_map/beams/pallas_call | solution.py:423
  119.8 18.7 %collective-permute-done.1.far_ref = bf16[32,512]{1,0:T(8,128)(2,1)S(1)} collective-permute-done((bf16[32,512]{1,0:T(8,128)(2,1)}, bf16[32,512]{1,0:T(8,128)(2,1)S(1)}, u32[]{:S(2)}, u32[]{:S(2)}) %collective-permute-start.1) | collective-permute-done | bytes 32800 | tf_op jit(solution)/shard_map/ppermute | solution.py:556
  138.5 0.6 copy-done.8
  139.1 4.5 %spectrum.1 = bf16[16,16,512]{2,1,0:T(8,128)(2,1)} custom-call(f32[16,64,512]{2,1,0:T(8,128)} %beams.3.own_ref, bf16[32,512]{1,0:T(8,128)(2,1)} %copy-done.8, s32[1,128]{1,0:T(1,128)} %broadcast_in_dim_tile.3.pick_ref, bf16[512,512]{1,0:T(8,128)(2,1)} %constant.68.high_ref, bf16[512,512]{1,0:T(8,128)(2,1)} %constant.71.low_ref), custom_call_target="tpu_custom_call" | custom-call | flops 2147483648 | bytes 4194304 | tf_op jit(solution)/shard_map/spectrum/pallas_call | solution.py:481
  143.6 5.7 %all-to-all-start.2 = ((bf16[16,16,512]{2,1,0:T(8,128)(2,1)}), bf16[16,16,512]{2,1,0:T(8,128)(2,1)S(1)}, u32[]{:S(2)}, u32[]{:S(2)}) async-start(bf16[16,16,512]{2,1,0:T(8,128)(2,1)} %spectrum.1), calls=%async_computation.2 | async-start | bytes 524288 | tf_op jit(solution)/shard_map/all_to_all | solution.py:564
  149.3 0.6 constant_dynamic-slice_fusion.delay_ref
  149.9 2.2 %turns.1.turn_ref = bf16[1024,512]{1,0:T(8,128)(2,1)} custom-call(s32[64,256]{1,0:T(8,128)} %constant_dynamic-slice_fusion.delay_ref), custom_call_target="tpu_custom_call" | custom-call | tf_op jit(solution)/shard_map/turns/pallas_call | solution.py:569
  152.1 7.2 %all-to-all-done.2 = bf16[16,16,512]{2,1,0:T(8,128)(2,1)S(1)} async-done(((bf16[16,16,512]{2,1,0:T(8,128)(2,1)}), bf16[16,16,512]{2,1,0:T(8,128)(2,1)S(1)}, u32[]{:S(2)}, u32[]{:S(2)}) %all-to-all-start.2) | async-done | bytes 262176 | tf_op jit(solution)/shard_map/all_to_all | solution.py:564
  159.3 1.2 copy-done.1
  160.5 1.6 plane.1
  162.2 3.8 %power.1 = f32[16,32,512]{2,1,0:T(8,128)} custom-call(f32[16,64,512]{2,1,0:T(8,128)} %beams.3.own_ref, bf16[16,64,512]{2,1,0:T(8,128)(2,1)} %collective-permute-done.2.far_ref), custom_call_target="tpu_custom_call" | custom-call | flops 268435456 | bytes 5242880 | tf_op jit(solution)/shard_map/power/pallas_call | solution.py:500
  (18 shorter events, 0.1 us)
Async XLA Ops:
  0.6 148.7 %copy-start = (s32[1024,256]{1,0:T(8,128)S(1)}, s32[1024,256]{1,0:T(8,128)}, u32[]{:S(2)}) copy-start(s32[1024,256]{1,0:T(8,128)} %param.15) | copy-start | bytes 3145732
  10.1 5.4 %copy-start.6 = (s32[16]{0:T(128)S(1)}, s32[16]{0:T(128)}, u32[]{:S(2)}) copy-start(s32[16]{0:T(128)} %param.16) | copy-start | bytes 196
  10.1 31.2 %all-to-all-start.1 = ((bf16[8,16,64,128]{3,2,1,0:T(8,128)(2,1)}), bf16[8,16,64,128]{3,2,1,0:T(8,128)(2,1)}, u32[]{:S(2)}, u32[]{:S(2)}) async-start(bf16[8,16,64,128]{3,2,1,0:T(8,128)(2,1)} %get-tuple-element.37), calls=%async_computation.1 | async-start | bytes 4194304 | tf_op jit(solution)/shard_map/all_to_all | solution.py:530
  16.1 5.8 %copy-start.4 = (f32[3,2048]{1,0:T(4,128)S(1)}, f32[3,2048]{1,0:T(4,128)}, u32[]{:S(2)}) copy-start(f32[3,2048]{1,0:T(4,128)} %param.12) | copy-start | bytes 73732
  16.1 6.2 %copy-start.5 = (s32[2048]{0:T(1024)S(1)}, s32[2048]{0:T(1024)}, u32[]{:S(2)}) copy-start(s32[2048]{0:T(1024)} %param.14) | copy-start | bytes 24580
  22.3 2.9 %copy-start.3 = (f32[16,2,2048]{2,1,0:T(2,128)S(1)}, f32[16,2,2048]{2,1,0:T(2,128)}, u32[]{:S(2)}) copy-start(f32[16,2,2048]{2,1,0:T(2,128)} %param.11) | copy-start | bytes 786436
  41.3 60.8 %all-to-all-start = ((bf16[8,16,64,128]{3,2,1,0:T(8,128)(2,1)}), bf16[8,16,64,128]{3,2,1,0:T(8,128)(2,1)S(1)}, u32[]{:S(2)}, u32[]{:S(2)}) async-start(bf16[8,16,64,128]{3,2,1,0:T(8,128)(2,1)} %spectra.1), calls=%async_computation | async-start | bytes 4194304 | tf_op jit(solution)/shard_map/all_to_all | solution.py:530
  44.9 26.3 %collective-permute-start = (f32[16,2,1024]{2,1,0:T(2,128)S(1)}, f32[16,2,1024]{2,1,0:T(2,128)S(1)}, u32[]{:S(2)}, u32[]{:S(2)}) collective-permute-start(f32[16,2,1024]{2,1,0:T(2,128)S(1)} %get-tuple-element.46), channel_id=1, source_target_pairs={{0,8},{1,9},{2,10},{3,11},{4,12},{5,13},{6,14},{7,15},{8,0},{9,1},... | collective-permute-start | bytes 393224 | tf_op jit(solution)/shard_map/ppermute | solution.py:538
  71.2 0.7 copy-start.7
  87.9 74.3 %collective-permute-start.2 = (bf16[16,64,512]{2,1,0:T(8,128)(2,1)}, bf16[16,64,512]{2,1,0:T(8,128)(2,1)}, u32[]{:S(2)}, u32[]{:S(2)}) collective-permute-start(bf16[16,64,512]{2,1,0:T(8,128)(2,1)} %beams.2.sum_ref), channel_id=1, source_target_pairs={{0,8},{1,9},{2,10},{3,11},{4,12},{5,13},{6,14},{7,15},{8,0},{9,1},... | collective-permute-start | bytes 3145736 | tf_op jit(solution)/shard_map/ppermute | solution.py:557
  94.5 44.0 %collective-permute-start.1 = (bf16[32,512]{1,0:T(8,128)(2,1)}, bf16[32,512]{1,0:T(8,128)(2,1)S(1)}, u32[]{:S(2)}, u32[]{:S(2)}) collective-permute-start(bf16[32,512]{1,0:T(8,128)(2,1)} %pick.1), channel_id=1, source_target_pairs={{0,8},{1,9},{2,10},{3,11},{4,12},{5,13},{6,14},{7,15},{8,0},{9,1},... | collective-permute-start | bytes 98312 | tf_op jit(solution)/shard_map/ppermute | solution.py:556
  102.1 1.3 copy-start.2
  138.5 0.6 copy-start.8
  143.6 15.7 %all-to-all-start.2 = ((bf16[16,16,512]{2,1,0:T(8,128)(2,1)}), bf16[16,16,512]{2,1,0:T(8,128)(2,1)S(1)}, u32[]{:S(2)}, u32[]{:S(2)}) async-start(bf16[16,16,512]{2,1,0:T(8,128)(2,1)} %spectrum.1), calls=%async_computation.2 | async-start | bytes 524288 | tf_op jit(solution)/shard_map/all_to_all | solution.py:564
  159.3 1.2 copy-start.1

commit v7 on v6

--- a/solution.py
+++ b/solution.py
@@ -164,7 +164,7 @@
     tiles = pl.num_programs(0) - 1
     chans, _, beams = out_ref.shape
     depth = dc_ref.shape[0]
-    wide = 256
+    wide = 256 if beams % 256 == 0 else 128
     chunk = depth // chans
 
     def generate(part, weight_ref):
@@ -247,11 +247,12 @@
     return chosen
 
 
-def far_pick_kernel(sum_ref, pick_ref, out_ref, picked_ref):
+def far_pick_kernel(sum0_ref, sum1_ref, pick_ref, out_ref, picked_ref):
     step = pl.program_id(0)
-    block = sum_ref.shape[0]
+    block = sum0_ref.shape[0]
     search = out_ref.shape[1] // TIME
-    rows = sum_ref[...].reshape(block * 2 * TIME, sum_ref.shape[2])
+    both = jnp.concatenate([sum0_ref[...], sum1_ref[...]], axis=2)
+    rows = both.reshape(block * 2 * TIME, both.shape[2])
     half = picked_ref.shape[0] // 2
     for k, row in enumerate(pick_beams(rows, pick_ref, 2 * block, search)):
         place = (k % 2) * half + step * block + k // 2
@@ -287,8 +288,9 @@
             spec_ref[dest] = spectrum
 
 
-def power_kernel(own_ref, far_ref, power_ref, norm):
-    total = own_ref[...] + far_ref[...].astype(F32)
+def power_kernel(own_ref, far0_ref, far1_ref, power_ref, norm):
+    far = jnp.concatenate([far0_ref[...], far1_ref[...]], axis=2)
+    total = own_ref[...] + far.astype(F32)
     real, imag = total[:, :TIME], total[:, TIME:]
     power_ref[...] = (real * real + imag * imag) * norm
 
@@ -409,7 +411,7 @@
     )(first, places, directions)
 
 
-def form_beams(x, gains, state, beams, out_type):
+def form_beams(x, gains, state, block, beams, out_type):
     sources, chans, rows, inputs = x.shape
     total = sources * inputs
     if inputs != 128:
@@ -419,7 +421,7 @@
     blocks = depth // 128
     tiles = total // depth
     late = lambda i: jnp.maximum(i - 1, 0)
-    state_spec = pl.BlockSpec((depth, beams), lambda i: (jnp.minimum(i, tiles - 1), 0))
+    state_spec = pl.BlockSpec((depth, beams), lambda i: (jnp.minimum(i, tiles - 1), block))
     return pl.pallas_call(
         beam_kernel,
         out_shape=jax.ShapeDtypeStruct((chans, rows, beams), out_type),
@@ -451,15 +453,15 @@
     return [pl.BlockSpec((block, *x.shape[1:]), lambda i: (i, 0, 0)) for x in arrays]
 
 
-def pick_far(sums, pick, search):
-    chans = sums.shape[0]
+def pick_far(sums0, sums1, pick, search):
+    chans = sums0.shape[0]
     block = min(4, chans)
     out = jax.ShapeDtypeStruct((2 * chans, TIME * search), BF16)
     return pl.pallas_call(
         far_pick_kernel,
         out_shape=out,
         grid=(chans // block,),
-        in_specs=cubes(block, sums) + [flat(pick.shape)],
+        in_specs=cubes(block, sums0, sums1) + [flat(pick.shape)],
         out_specs=flat(out.shape),
         scratch_shapes=[pltpu.VMEM(out.shape, F32)],
         compiler_params=LARGE,
@@ -467,7 +469,7 @@
             flops=1 << 30, bytes_accessed=2 << 20, transcendentals=0
         ),
         name="pick",
-    )(sums, pick)
+    )(sums0, sums1, pick)
 
 
 def search_spectra(own, far, pick, search, copies, norm):
@@ -501,14 +503,14 @@
         functools.partial(power_kernel, norm=norm),
         out_shape=out,
         grid=(chans // block,),
-        in_specs=cubes(block, own, far),
+        in_specs=cubes(block, own, *far),
         out_specs=cubes(block, out)[0],
         compiler_params=LARGE,
         cost_estimate=pl.CostEstimate(
             flops=1 << 28, bytes_accessed=5 << 20, transcendentals=0
         ),
         name="power",
-    )(own, far)
+    )(own, *far)
 
 
 def on_device(voltages, gains, positions, directions, input_order, delays, search_beams):
@@ -551,18 +553,23 @@
 
     beams = directions.shape[1]
     norm = 1.0 / gains.shape[2]
-    sums = form_beams(far, far_gains, (dc, ds, far_c, far_s), beams, BF16)
-    picked = pick_far(sums, pick, search)
+    far_state = (dc, ds, far_c, far_s)
+    few = beams // 4
+    sums1 = form_beams(far, far_gains, far_state, 3, few, BF16)
+    far1 = lax.ppermute(sums1, "crate", partners)
+    far, far1_sums = lax.optimization_barrier((far, sums1))
+    sums0 = form_beams(far, far_gains, far_state, 0, beams - few, BF16)
+    picked = pick_far(sums0, far1_sums, pick, search)
     far_picked = lax.ppermute(picked, "crate", partners)
-    far_sums = lax.ppermute(sums, "crate", partners)
+    far0 = lax.ppermute(sums0, "crate", partners)
     own_first, picked = lax.optimization_barrier((own_first, picked))
     near_c, near_s = phasors(own_first, places, directions, 2)
-    near_sums = form_beams(near, near_gains, (dc, ds, near_c, near_s), beams, F32)
+    near_sums = form_beams(near, near_gains, (dc, ds, near_c, near_s), 0, beams, F32)
 
     spectrum = search_spectra(near_sums, far_picked, pick, search, devices, norm)
     near_sums, spectrum = lax.optimization_barrier((near_sums, spectrum))
     spectrum = lax.all_to_all(spectrum, "crate", split_axis=0, concat_axis=0, tiled=True)
-    beam_power = powers(near_sums, far_sums, norm)
+    beam_power = powers(near_sums, (far0, far1), norm)
     width = spectrum.shape[-1]
     trials = delays.shape[0] // devices
     own_delays = lax.dynamic_slice_in_dim(delays, position * trials, trials, 0)

time: 167 us -> 170 us (1.018)
  waiting for transfers between devices: 54.5 us -> 48.1 us
  Pallas kernels: 79.6 us -> 84.3 us
  starting transfers between devices: 21.2 us -> 24.3 us
    ppermute x1, waiting for transfers between devices: 18.7 us -> 7.3 us  [on_device(): far_picked = lax.ppermute(picked, 'crate', partners)]
    ppermute x1 -> x2, waiting for transfers between devices: 0.01 us -> 7.44 us  [the longest x1 7.43 us: on_device(): far1 = lax.ppermute(sums1, 'crate', partners)]
    pallas_call x2 -> x3, Pallas kernels: 32.3 us -> 37 us  [form_beams(): pl.pallas_call(beam_kernel, out_shape=jax.ShapeDtypeStruct((chans, rows,...]
    ppermute x1 -> x2, starting transfers between devices: 3.38 us -> 6.27 us  [the longest x1 3.38 us: on_device(): far0 = lax.ppermute(sums0, 'crate', partners)]
    all_to_all x1, waiting for transfers between devices: 7.18 us -> 4.87 us  [on_device(): lax.all_to_all(spectrum, 'crate', split_axis=0, concat_axis=0, tiled=True)]
    unnamed x18 -> x22, local copies, waits for them, and re-layouts: 3.84 us -> 4.58 us
  transfers between devices with their start and end apart: 6 -> 7, of which waited for: 4 -> 5; matrix products, arithmetic and copies ran while one was open for 4% -> 4% of each run, Pallas kernels for 40% -> 42%
where the time goes in v7:
time: 170 us; the launch traced here: 168 us
  Pallas kernels  84.3 us (50%)
  waiting for transfers between devices  48.1 us (28%)
  starting transfers between devices  24.3 us (14%)
  local copies, waits for them, and re-layouts  9.62 us (6%)
    pallas_call x3, Pallas kernels, form_beams(): pl.pallas_call(beam_kernel, out_shape=jax.ShapeDtypeStruct((chans, rows,...  37 us
    ppermute x1, waiting for transfers between devices, on_device(): far_gains = lax.ppermute(far_gains, 'crate', partners)  23 us
    pallas_call x2, Pallas kernels, phasors(): pl.pallas_call(phasor_kernel, out_shape=[jax.ShapeDtypeStruct((total, bea...  16.7 us
    pallas_call x1, Pallas kernels, fold(): pl.pallas_call(fold_kernel, out_shape=(spectra, folded), grid_spec=pltpu....  9.39 us
    all_to_all x2, starting transfers between devices, exchange(): lax.all_to_all(x, 'crate', split_axis=0, concat_axis=0, axis_index_groups...  9.07 us
    ppermute x1, waiting for transfers between devices, on_device(): far1 = lax.ppermute(sums1, 'crate', partners)  7.43 us
    ppermute x1, waiting for transfers between devices, on_device(): far_picked = lax.ppermute(picked, 'crate', partners)  7.3 us
    all_to_all x1, starting transfers between devices, on_device(): lax.all_to_all(spectrum, 'crate', split_axis=0, concat_axis=0, tiled=True)  5.85 us
  transfers between devices with their start and end apart: 7, of which 5 were waited for; matrix products, arithmetic and copies ran while one was open for 4% of the time, Pallas kernels for 42%

profile of v7, /device:TPU:0, one launch (start us, length us, event | category | flops | bytes accessed | tf_op | source)
XLA Modules:
  0.0 168.0 jit_solution(2698502123109908575)
XLA Ops:
  0.7 9.4 %fold.1 = (bf16[8,16,64,128]{3,2,1,0:T(8,128)(2,1)}, bf16[4096,512]{1,0:T(8,128)(2,1)}) custom-call(s32[1]{0:T(128)S(6)} %sub.14.half_ref, bf16[128,17920]{1,0:T(8,128)(2,1)} %volt_ref.1, f32[4,512]{1,0:T(4,128)} %constant.65.clone.window_ref, bf16[512,512]{1,0:T(8,128)(2,1)} %constant.67.table_ref), custom_call_target="tpu_custom_call" | custom-call | flops 4294967296 | bytes 12582912 | tf_op jit(solution)/shard_map/fold/pallas_call | solution.py:344
  10.1 5.3 %all-to-all-start.1 = ((bf16[8,16,64,128]{3,2,1,0:T(8,128)(2,1)}), bf16[8,16,64,128]{3,2,1,0:T(8,128)(2,1)}, u32[]{:S(2)}, u32[]{:S(2)}) async-start(bf16[8,16,64,128]{3,2,1,0:T(8,128)(2,1)} %get-tuple-element.39), calls=%async_computation.1 | async-start | bytes 4194304 | tf_op jit(solution)/shard_map/all_to_all | solution.py:532
  15.4 5.8 %spectra.1 = bf16[8,16,64,128]{3,2,1,0:T(8,128)(2,1)} custom-call(s32[1]{0:T(128)} %bitcast.block_ref, bf16[4096,512]{1,0:T(8,128)(2,1)} %get-tuple-element.26.folded_ref, bf16[512,512]{1,0:T(8,128)(2,1)} %constant.67.table_ref), custom_call_target="tpu_custom_call" | custom-call | flops 2147483648 | bytes 6291456 | tf_op jit(solution)/shard_map/spectra/pallas_call | solution.py:370
  22.2 2.8 %gather_fusion = f32[1024,3]{1,0:T(8,128)S(1)} fusion(f32[2048,3]{1,0:T(8,128)S(1)} %bitcast.8, s32[1024]{0:T(1024)S(1)} %fusion), kind=kCustom, calls=%fused_computation | custom fusion | bytes 28672 | tf_op jit(solution)/shard_map/jit(_take)/gather | solution.py:543
  25.0 0.7 constant_dynamic-slice_fusion.1
  25.7 1.0 broadcast_select_fusion.place_ref
  26.7 9.1 %phasors.2 = (f32[1024,512]{1,0:T(8,128)}, f32[1024,512]{1,0:T(8,128)}, f32[1024,512]{1,0:T(8,128)}, f32[1024,512]{1,0:T(8,128)}) custom-call(s32[1]{0:T(128)} %bitcast.2.first_ref, f32[1024,3]{1,0:T(8,128)} %broadcast_select_fusion.place_ref, f32[3,512]{1,0:T(4,128)} %dir_ref.3), custom_call_target="tpu_custom_call" | custom-call | flops 4194304000 | bytes 8388608 | tf_op jit(solution)/shard_map/phasors/pallas_call | solution.py:394
  35.8 5.4 %all-to-all-done.1.x_ref = bf16[8,16,64,128]{3,2,1,0:T(8,128)(2,1)} async-done(((bf16[8,16,64,128]{3,2,1,0:T(8,128)(2,1)}), bf16[8,16,64,128]{3,2,1,0:T(8,128)(2,1)}, u32[]{:S(2)}, u32[]{:S(2)}) %all-to-all-start.1) | async-done | bytes 2097184 | tf_op jit(solution)/shard_map/all_to_all | solution.py:532
  41.1 3.8 %all-to-all-start = ((bf16[8,16,64,128]{3,2,1,0:T(8,128)(2,1)}), bf16[8,16,64,128]{3,2,1,0:T(8,128)(2,1)S(1)}, u32[]{:S(2)}, u32[]{:S(2)}) async-start(bf16[8,16,64,128]{3,2,1,0:T(8,128)(2,1)} %spectra.1), calls=%async_computation | async-start | bytes 4194304 | tf_op jit(solution)/shard_map/all_to_all | solution.py:532
  44.9 3.1 %collective-permute-start = (f32[16,2,1024]{2,1,0:T(2,128)S(1)}, f32[16,2,1024]{2,1,0:T(2,128)S(1)}, u32[]{:S(2)}, u32[]{:S(2)}) collective-permute-start(f32[16,2,1024]{2,1,0:T(2,128)S(1)} %get-tuple-element.50), channel_id=1, source_target_pairs={{0,8},{1,9},{2,10},{3,11},{4,12},{5,13},{6,14},{7,15},{8,0},{9,1},... | collective-permute-start | bytes 393224 | tf_op jit(solution)/shard_map/ppermute | solution.py:540
  48.0 23.0 %collective-permute-done.gain_ref = f32[16,2,1024]{2,1,0:T(2,128)S(1)} collective-permute-done((f32[16,2,1024]{2,1,0:T(2,128)S(1)}, f32[16,2,1024]{2,1,0:T(2,128)S(1)}, u32[]{:S(2)}, u32[]{:S(2)}) %collective-permute-start) | collective-permute-done | bytes 131104 | tf_op jit(solution)/shard_map/ppermute | solution.py:540
  71.1 0.7 copy-done.6
  71.7 6.5 %beams.3.sum1_ref = bf16[16,64,128]{2,1,0:T(8,128)(2,1)} custom-call(bf16[8,16,64,128]{3,2,1,0:T(8,128)(2,1)} %all-to-all-done.1.x_ref, f32[16,2,1024]{2,1,0:T(2,128)} %copy-done.6, f32[1024,512]{1,0:T(8,128)} %get-tuple-element.36.dc_ref, f32[1024,512]{1,0:T(8,128)} %get-tuple-element.37.ds_ref, f32[1024,512]{1,0:T(8,128)} %get-tuple-element.40.c_ref, ...), custom_call_target="tpu_custom_call" | custom-call | flops 2147483648 | bytes 12582912 | tf_op jit(solution)/shard_map/beams/pallas_call | solution.py:425
  78.3 14.1 %beams.4.sum0_ref = bf16[16,64,384]{2,1,0:T(8,128)(2,1)} custom-call(bf16[8,16,64,128]{3,2,1,0:T(8,128)(2,1)} %all-to-all-done.1.x_ref, f32[16,2,1024]{2,1,0:T(2,128)} %copy-done.6, f32[1024,512]{1,0:T(8,128)} %get-tuple-element.36.dc_ref, f32[1024,512]{1,0:T(8,128)} %get-tuple-element.37.ds_ref, f32[1024,512]{1,0:T(8,128)} %get-tuple-element.40.c_ref, ...), custom_call_target="tpu_custom_call" | custom-call | flops 6442450944 | bytes 12582912 | tf_op jit(solution)/shard_map/beams/pallas_call | solution.py:425
  92.4 3.4 %collective-permute-start.2 = (bf16[16,64,384]{2,1,0:T(8,128)(2,1)}, bf16[16,64,384]{2,1,0:T(8,128)(2,1)}, u32[]{:S(2)}, u32[]{:S(2)}) collective-permute-start(bf16[16,64,384]{2,1,0:T(8,128)(2,1)} %beams.4.sum0_ref), channel_id=1, source_target_pairs={{0,8},{1,9},{2,10},{3,11},{4,12},{5,13},{6,14},{7,15},{8,0},{9,1},... | collective-permute-start | bytes 2359304 | tf_op jit(solution)/shard_map/ppermute | solution.py:564
  95.8 3.2 %pick.1 = bf16[32,512]{1,0:T(8,128)(2,1)} custom-call(bf16[16,64,384]{2,1,0:T(8,128)(2,1)} %beams.4.sum0_ref, bf16[16,64,128]{2,1,0:T(8,128)(2,1)} %beams.3.sum1_ref, s32[1,128]{1,0:T(1,128)} %broadcast_in_dim_tile.3.pick_ref), custom_call_target="tpu_custom_call" | custom-call | flops 1073741824 | bytes 2097152 | tf_op jit(solution)/shard_map/pick/pallas_call | solution.py:460
  99.0 7.6 %phasors.3 = (f32[1024,512]{1,0:T(8,128)}, f32[1024,512]{1,0:T(8,128)}) custom-call(s32[1]{0:T(128)} %bitcast.1.first_ref, f32[1024,3]{1,0:T(8,128)} %broadcast_select_fusion.place_ref, f32[3,512]{1,0:T(4,128)} %dir_ref.3), custom_call_target="tpu_custom_call" | custom-call | flops 4194304000 | bytes 4194304 | tf_op jit(solution)/shard_map/phasors/pallas_call | solution.py:394
  106.7 1.4 copy-done.2
  108.0 16.3 %beams.5.own_ref = f32[16,64,512]{2,1,0:T(8,128)} custom-call(bf16[8,16,64,128]{3,2,1,0:T(8,128)(2,1)} %copy-done.2, f32[16,2,1024]{2,1,0:T(2,128)} %get-tuple-element.35.gain_ref, f32[1024,512]{1,0:T(8,128)} %get-tuple-element.36.dc_ref, f32[1024,512]{1,0:T(8,128)} %get-tuple-element.37.ds_ref, f32[1024,512]{1,0:T(8,128)} %get-tuple-element.46.c_ref, ...), custom_call_target="tpu_custom_call" | custom-call | flops 8589934592 | bytes 12582912 | tf_op jit(solution)/shard_map/beams/pallas_call | solution.py:425
  124.4 7.3 %collective-permute-done.1.far_ref = bf16[32,512]{1,0:T(8,128)(2,1)S(1)} collective-permute-done((bf16[32,512]{1,0:T(8,128)(2,1)}, bf16[32,512]{1,0:T(8,128)(2,1)S(1)}, u32[]{:S(2)}, u32[]{:S(2)}) %collective-permute-start.1) | collective-permute-done | bytes 32800 | tf_op jit(solution)/shard_map/ppermute | solution.py:563
  131.7 0.6 copy-done.10
  132.3 4.5 %spectrum.1 = bf16[16,16,512]{2,1,0:T(8,128)(2,1)} custom-call(f32[16,64,512]{2,1,0:T(8,128)} %beams.5.own_ref, bf16[32,512]{1,0:T(8,128)(2,1)} %copy-done.10, s32[1,128]{1,0:T(1,128)} %broadcast_in_dim_tile.3.pick_ref, bf16[512,512]{1,0:T(8,128)(2,1)} %constant.68.high_ref, bf16[512,512]{1,0:T(8,128)(2,1)} %constant.71.low_ref), custom_call_target="tpu_custom_call" | custom-call | flops 2147483648 | bytes 4194304 | tf_op jit(solution)/shard_map/spectrum/pallas_call | solution.py:483
  136.8 5.8 %all-to-all-start.2 = ((bf16[16,16,512]{2,1,0:T(8,128)(2,1)}), bf16[16,16,512]{2,1,0:T(8,128)(2,1)S(1)}, u32[]{:S(2)}, u32[]{:S(2)}) async-start(bf16[16,16,512]{2,1,0:T(8,128)(2,1)} %spectrum.1), calls=%async_computation.2 | async-start | bytes 524288 | tf_op jit(solution)/shard_map/all_to_all | solution.py:571
  142.6 2.9 %collective-permute-start.3 = (bf16[16,64,128]{2,1,0:T(8,128)(2,1)S(1)}, bf16[16,64,128]{2,1,0:T(8,128)(2,1)S(1)}, u32[]{:S(2)}, u32[]{:S(2)}) collective-permute-start(bf16[16,64,128]{2,1,0:T(8,128)(2,1)S(1)} %copy-done.3), channel_id=1, source_target_pairs={{0,8},{1,9},{2,10},{3,11},{4,12},{5,13},{6,14},{7,15},{8,0},{9,1},... | collective-permute-start | bytes 786440 | tf_op jit(solution)/shard_map/ppermute | solution.py:559
  145.5 0.6 constant_dynamic-slice_fusion.delay_ref
  146.2 2.2 %turns.1.turn_ref = bf16[1024,512]{1,0:T(8,128)(2,1)} custom-call(s32[64,256]{1,0:T(8,128)} %constant_dynamic-slice_fusion.delay_ref), custom_call_target="tpu_custom_call" | custom-call | tf_op jit(solution)/shard_map/turns/pallas_call | solution.py:576
  148.3 4.9 %all-to-all-done.2 = bf16[16,16,512]{2,1,0:T(8,128)(2,1)S(1)} async-done(((bf16[16,16,512]{2,1,0:T(8,128)(2,1)}), bf16[16,16,512]{2,1,0:T(8,128)(2,1)S(1)}, u32[]{:S(2)}, u32[]{:S(2)}) %all-to-all-start.2) | async-done | bytes 262176 | tf_op jit(solution)/shard_map/all_to_all | solution.py:571
  153.2 1.2 copy-done.1
  154.4 1.6 plane.1
  156.0 7.4 %collective-permute-done.3.far1_ref = bf16[16,64,128]{2,1,0:T(8,128)(2,1)S(1)} collective-permute-done((bf16[16,64,128]{2,1,0:T(8,128)(2,1)S(1)}, bf16[16,64,128]{2,1,0:T(8,128)(2,1)S(1)}, u32[]{:S(2)}, u32[]{:S(2)}) %collective-permute-start.3) | collective-permute-done | bytes 262176 | tf_op jit(solution)/shard_map/ppermute | solution.py:559
  163.5 0.7 copy-done.4
  164.2 3.9 %power.1 = f32[16,32,512]{2,1,0:T(8,128)} custom-call(f32[16,64,512]{2,1,0:T(8,128)} %beams.5.own_ref, bf16[16,64,384]{2,1,0:T(8,128)(2,1)} %collective-permute-done.2.far0_ref, bf16[16,64,128]{2,1,0:T(8,128)(2,1)} %copy-done.4), custom_call_target="tpu_custom_call" | custom-call | flops 268435456 | bytes 5242880 | tf_op jit(solution)/shard_map/power/pallas_call | solution.py:502
  (25 shorter events, 1.0 us)
Async XLA Ops:
  0.6 144.9 %copy-start = (s32[1024,256]{1,0:T(8,128)S(1)}, s32[1024,256]{1,0:T(8,128)}, u32[]{:S(2)}) copy-start(s32[1024,256]{1,0:T(8,128)} %param.15) | copy-start | bytes 3145732
  10.1 31.1 %all-to-all-start.1 = ((bf16[8,16,64,128]{3,2,1,0:T(8,128)(2,1)}), bf16[8,16,64,128]{3,2,1,0:T(8,128)(2,1)}, u32[]{:S(2)}, u32[]{:S(2)}) async-start(bf16[8,16,64,128]{3,2,1,0:T(8,128)(2,1)} %get-tuple-element.39), calls=%async_computation.1 | async-start | bytes 4194304 | tf_op jit(solution)/shard_map/all_to_all | solution.py:532
  15.3 5.8 %copy-start.7 = (f32[3,2048]{1,0:T(4,128)S(1)}, f32[3,2048]{1,0:T(4,128)}, u32[]{:S(2)}) copy-start(f32[3,2048]{1,0:T(4,128)} %param.12) | copy-start | bytes 73732
  15.3 6.2 %copy-start.9 = (s32[16]{0:T(128)S(1)}, s32[16]{0:T(128)}, u32[]{:S(2)}) copy-start(s32[16]{0:T(128)} %param.16) | copy-start | bytes 196
  15.4 6.8 %copy-start.8 = (s32[2048]{0:T(1024)S(1)}, s32[2048]{0:T(1024)}, u32[]{:S(2)}) copy-start(s32[2048]{0:T(1024)} %param.14) | copy-start | bytes 24580
  22.2 2.9 %copy-start.5 = (f32[16,2,2048]{2,1,0:T(2,128)S(1)}, f32[16,2,2048]{2,1,0:T(2,128)}, u32[]{:S(2)}) copy-start(f32[16,2,2048]{2,1,0:T(2,128)} %param.11) | copy-start | bytes 786436
  41.1 65.5 %all-to-all-start = ((bf16[8,16,64,128]{3,2,1,0:T(8,128)(2,1)}), bf16[8,16,64,128]{3,2,1,0:T(8,128)(2,1)S(1)}, u32[]{:S(2)}, u32[]{:S(2)}) async-start(bf16[8,16,64,128]{3,2,1,0:T(8,128)(2,1)} %spectra.1), calls=%async_computation | async-start | bytes 4194304 | tf_op jit(solution)/shard_map/all_to_all | solution.py:532
  44.9 26.2 %collective-permute-start = (f32[16,2,1024]{2,1,0:T(2,128)S(1)}, f32[16,2,1024]{2,1,0:T(2,128)S(1)}, u32[]{:S(2)}, u32[]{:S(2)}) collective-permute-start(f32[16,2,1024]{2,1,0:T(2,128)S(1)} %get-tuple-element.50), channel_id=1, source_target_pairs={{0,8},{1,9},{2,10},{3,11},{4,12},{5,13},{6,14},{7,15},{8,0},{9,1},... | collective-permute-start | bytes 393224 | tf_op jit(solution)/shard_map/ppermute | solution.py:540
  71.1 0.7 copy-start.6
  92.4 71.1 %collective-permute-start.2 = (bf16[16,64,384]{2,1,0:T(8,128)(2,1)}, bf16[16,64,384]{2,1,0:T(8,128)(2,1)}, u32[]{:S(2)}, u32[]{:S(2)}) collective-permute-start(bf16[16,64,384]{2,1,0:T(8,128)(2,1)} %beams.4.sum0_ref), channel_id=1, source_target_pairs={{0,8},{1,9},{2,10},{3,11},{4,12},{5,13},{6,14},{7,15},{8,0},{9,1},... | collective-permute-start | bytes 2359304 | tf_op jit(solution)/shard_map/ppermute | solution.py:564
  99.0 32.6 %collective-permute-start.1 = (bf16[32,512]{1,0:T(8,128)(2,1)}, bf16[32,512]{1,0:T(8,128)(2,1)S(1)}, u32[]{:S(2)}, u32[]{:S(2)}) collective-permute-start(bf16[32,512]{1,0:T(8,128)(2,1)} %pick.1), channel_id=1, source_target_pairs={{0,8},{1,9},{2,10},{3,11},{4,12},{5,13},{6,14},{7,15},{8,0},{9,1},... | collective-permute-start | bytes 98312 | tf_op jit(solution)/shard_map/ppermute | solution.py:563
  106.7 1.4 copy-start.2
  124.4 18.3 %copy-start.3 = (bf16[16,64,128]{2,1,0:T(8,128)(2,1)S(1)}, bf16[16,64,128]{2,1,0:T(8,128)(2,1)}, u32[]{:S(2)}) copy-start(bf16[16,64,128]{2,1,0:T(8,128)(2,1)} %beams.3.sum1_ref) | copy-start | bytes 786436
  131.7 0.6 copy-start.10
  136.8 16.4 %all-to-all-start.2 = ((bf16[16,16,512]{2,1,0:T(8,128)(2,1)}), bf16[16,16,512]{2,1,0:T(8,128)(2,1)S(1)}, u32[]{:S(2)}, u32[]{:S(2)}) async-start(bf16[16,16,512]{2,1,0:T(8,128)(2,1)} %spectrum.1), calls=%async_computation.2 | async-start | bytes 524288 | tf_op jit(solution)/shard_map/all_to_all | solution.py:571
  142.6 20.8 %collective-permute-start.3 = (bf16[16,64,128]{2,1,0:T(8,128)(2,1)S(1)}, bf16[16,64,128]{2,1,0:T(8,128)(2,1)S(1)}, u32[]{:S(2)}, u32[]{:S(2)}) collective-permute-start(bf16[16,64,128]{2,1,0:T(8,128)(2,1)S(1)} %copy-done.3), channel_id=1, source_target_pairs={{0,8},{1,9},{2,10},{3,11},{4,12},{5,13},{6,14},{7,15},{8,0},{9,1},... | collective-permute-start | bytes 786440 | tf_op jit(solution)/shard_map/ppermute | solution.py:559
  153.2 1.2 copy-start.1
  163.5 0.7 copy-start.4

commit v8 on v7

--- a/solution.py
+++ b/solution.py
@@ -13,6 +13,7 @@
 TAPS = 4
 TIME = 32
 PITCH = 40
+FRAMES = 8
 FFTLEN = 512
 HALF_BINS = TIME // 2
 TWO_PI = 2.0 * math.pi
@@ -79,21 +80,20 @@
     return high, (x - high.astype(F32)).astype(BF16)
 
 
-def transform_rows(table, folded_ref, spread_ref, out_ref):
-    dests, chans, _, inputs = out_ref.shape
+def group_size(inputs):
+    return 2 if inputs % 128 == 0 else 1
+
+
+def spread_spectra(table, frames, spread_ref, inputs, t):
     rows = table.shape[0]
-    group = 2 if inputs % 128 == 0 else 1
-
-    def step(index, carry):
-        start = pl.multiple_of(index * (group * inputs), group * inputs)
-        frames = folded_ref[pl.ds(start, group * inputs), :]
-        out = lax.dot_general(table, frames, NT, preferred_element_type=F32)
-        for part in range(group):
-            piece = out[:, part * inputs : (part + 1) * inputs]
-            spread_ref[pl.ds(index * group + part, rows, stride=PITCH), :] = piece
-        return carry
-
-    lax.fori_loop(0, TIME // group, step, 0, unroll=4)
+    out = lax.dot_general(table, frames, NT, preferred_element_type=F32)
+    for part in range(frames.shape[0] // inputs):
+        piece = out[:, part * inputs : (part + 1) * inputs]
+        spread_ref[pl.ds(t + part, rows, stride=PITCH), :] = piece
+
+
+def pack_spectra(spread_ref, out_ref):
+    dests, chans = out_ref.shape[:2]
 
     def pack(dest, carry):
         for chan in range(chans):
@@ -106,33 +106,76 @@
     lax.fori_loop(0, dests, pack, 0, unroll=2)
 
 
-def fold_kernel(half_ref, volt_ref, window_ref, table_ref, out_ref, folded_ref, spread_ref):
+def fold_kernel(block_ref, volt_ref, *refs):
+    next_refs, refs = refs[: TAPS - 1], refs[TAPS - 1 :]
+    window_ref, table_ref, out_ref, folded_ref, even_ref, odd_ref, spread_ref = refs
     step = pl.program_id(0)
-    rows = volt_ref.shape[0]
+    last = TIME // FRAMES
     inputs = out_ref.shape[-1]
     lanes = 256
-    for lane in range(0, FFTLEN, lanes):
+
+    def fold_piece(row, lane, kept_ref):
         taps = [window_ref[j : j + 1, lane : lane + lanes] for j in range(TAPS)]
-        for row in range(0, rows, 16):
-            frames = []
-            for t in range(TIME + TAPS - 1):
-                start = t * FFTLEN + lane
-                frames.append(volt_ref[row : row + 16, start : start + lanes].astype(F32))
-                if t >= TAPS - 1:
-                    first = t - TAPS + 1
-                    total = taps[0] * frames[first]
-                    for j in range(1, TAPS):
-                        total = total + taps[j] * frames[first + j]
-                    place = pl.multiple_of(first * inputs + step * rows + row, 16)
-                    folded_ref[pl.ds(place, 16), lane : lane + lanes] = total.astype(BF16)
-
-    @pl.when(step == pl.num_programs(0) - 1)
+        frames = []
+        for t in range(FRAMES + TAPS - 1):
+            ref, place = (volt_ref, t) if t < FRAMES else (next_refs[t - FRAMES], 0)
+            start = place * FFTLEN + lane
+            frames.append(ref[row : row + 16, start : start + lanes].astype(F32))
+        for t in range(FRAMES):
+            total = taps[0] * frames[t]
+            for j in range(1, TAPS):
+                total = total + taps[j] * frames[t + j]
+            total = total.astype(BF16)
+            place = t * inputs + row
+            folded_ref[place : place + 16, lane : lane + lanes] = total
+            kept_ref[place : place + 16, lane : lane + lanes] = total
+
+    pieces = [(row, lane) for lane in range(0, FFTLEN, lanes) for row in range(0, inputs, 16)]
+
+    def fold_some(kept_ref, some):
+        for row, lane in some:
+            fold_piece(row, lane, kept_ref)
+
+    def transform(kept_ref, index):
+        group = group_size(inputs)
+        start = index * group * inputs
+        frames = kept_ref[start : start + group * inputs, :]
+        t = (step - 1) * FRAMES + index * group
+        spread_spectra(table_ref[...], frames, spread_ref, inputs, t)
+
+    count = FRAMES // group_size(inputs)
+
+    @pl.when(step == 0)
     def _():
-        transform_rows(table_ref[...], folded_ref, spread_ref, out_ref)
+        fold_some(even_ref, pieces)
+
+    for parity, (old_ref, new_ref) in ((1, (even_ref, odd_ref)), (0, (odd_ref, even_ref))):
+
+        @pl.when((step > 0) & (step < last) & (lax.rem(step, 2) == parity))
+        def _(old_ref=old_ref, new_ref=new_ref):
+            for index in range(count):
+                fold_some(new_ref, pieces[index::count])
+                transform(old_ref, index)
+
+        @pl.when((step == last) & (lax.rem(step, 2) == parity))
+        def _(old_ref=old_ref):
+            for index in range(count):
+                transform(old_ref, index)
+            pack_spectra(spread_ref, out_ref)
 
 
 def spectra_kernel(block_ref, folded_ref, table_ref, out_ref, spread_ref):
-    transform_rows(table_ref[...], folded_ref, spread_ref, out_ref)
+    inputs = out_ref.shape[-1]
+    group = group_size(inputs)
+
+    def step(index, carry):
+        start = pl.multiple_of(index * (group * inputs), group * inputs)
+        frames = folded_ref[pl.ds(start, group * inputs), :]
+        spread_spectra(table_ref[...], frames, spread_ref, inputs, index * group)
+        return carry
+
+    lax.fori_loop(0, TIME // group, step, 0, unroll=4)
+    pack_spectra(spread_ref, out_ref)
 
 
 def phasor_kernel(first_ref, place_ref, dir_ref, *out_refs):
@@ -148,8 +191,10 @@
             geometry = place[:, 0:1] * direction[0:1, :]
             geometry = geometry + place[:, 1:2] * direction[1:2, :]
             geometry = geometry + place[:, 2:3] * direction[2:3, :]
-            first = 1.0 + first_ref[0].astype(F32) * (1.0 / CH)
-            for k, scale in enumerate((first, 1.0 / CH)[: len(out_refs) // 2]):
+            scales = [1.0 / CH]
+            for k in range(len(out_refs) // 2 - 1):
+                scales.append(1.0 + first_ref[k].astype(F32) * (1.0 / CH))
+            for k, scale in enumerate(scales):
                 c, s = cos_sin_turns(geometry * scale)
                 out_refs[2 * k][rows, lanes], out_refs[2 * k + 1][rows, lanes] = c, s
         return carry
@@ -334,10 +379,15 @@
 
 
 def fold(voltages, table, block_id, dests, chans):
-    inputs, samples = voltages.shape
+    inputs = voltages.shape[0]
     rows = 2 * dests * chans
     window = jnp.asarray(pfb_window())
-    block = min(32, inputs)
+    last = TIME // FRAMES
+    now = lambda i: jnp.minimum(i, last - 1)
+    following = lambda j: pl.BlockSpec(
+        (inputs, FFTLEN), lambda i, k: (0, (now(i) + 1) * FRAMES + j)
+    )
+    kept = pltpu.VMEM((FRAMES * inputs, FFTLEN), BF16)
     spectra = jax.ShapeDtypeStruct((dests, chans, 2 * TIME, inputs), BF16)
     folded = jax.ShapeDtypeStruct((TIME * inputs, FFTLEN), BF16)
     whole = lambda x: pl.BlockSpec(x.shape, lambda i, k: (0,) * len(x.shape))
@@ -346,21 +396,25 @@
         out_shape=(spectra, folded),
         grid_spec=pltpu.PrefetchScalarGridSpec(
             num_scalar_prefetch=1,
-            grid=(inputs // block,),
+            grid=(last + 1,),
             in_specs=[
-                pl.BlockSpec((block, samples), lambda i, k: (i, 0)),
+                pl.BlockSpec((inputs, FRAMES * FFTLEN), lambda i, k: (0, now(i))),
+                *[following(j) for j in range(TAPS - 1)],
                 whole(window),
                 pl.BlockSpec((rows, FFTLEN), lambda i, k: (k[0], 0)),
             ],
-            out_specs=(whole(spectra), whole(folded)),
-            scratch_shapes=[pltpu.VMEM((rows * PITCH, inputs), F32)],
+            out_specs=(
+                whole(spectra),
+                pl.BlockSpec((FRAMES * inputs, FFTLEN), lambda i, k: (now(i), 0)),
+            ),
+            scratch_shapes=[kept, kept, pltpu.VMEM((rows * PITCH, inputs), F32)],
         ),
         compiler_params=LARGE,
         cost_estimate=pl.CostEstimate(
             flops=8 * rows * FFTLEN * TIME * inputs, bytes_accessed=12 << 20, transcendentals=0
         ),
         name="fold",
-    )(block_id, voltages, window, table)
+    )(block_id, *[voltages] * TAPS, window, table)
 
 
 def more_spectra(folded, table, block_id, dests, chans):
@@ -388,7 +442,8 @@
     )(block_id, folded, table)
 
 
-def phasors(first, places, directions, count):
+def phasors(firsts, places, directions):
+    count = 2 + 2 * firsts.shape[0]
     total, beams = places.shape[0], directions.shape[1]
     depth = 128
     return pl.pallas_call(
@@ -408,7 +463,7 @@
             flops=8000 * total * beams, bytes_accessed=count * 4 * total * beams, transcendentals=0
         ),
         name="phasors",
-    )(first, places, directions)
+    )(firsts, places, directions)
 
 
 def form_beams(x, gains, state, block, beams, out_type):
@@ -543,11 +598,12 @@
     places = jnp.take(positions.T, order, axis=0)
     search = search_beams.shape[0]
     pick = jnp.tile(search_beams, 128 // search)[None, :]
-    own_first = (position * chans).astype(jnp.int32).reshape(1)
-    far_first = ((position + per_half) % devices * chans).astype(jnp.int32).reshape(1)
-    far_c, far_s, dc, ds = phasors(far_first, places, directions, 4)
-    near, near_gains, pick, own_first, dc, ds, far_c, far_s = lax.optimization_barrier(
-        (near, near_gains, pick, own_first, dc, ds, far_c, far_s)
+    firsts = jnp.stack([(position + per_half) % devices, position]) * chans
+    dc, ds, far_c, far_s, near_c, near_s = phasors(
+        firsts.astype(jnp.int32), places, directions
+    )
+    near, near_gains, pick, dc, ds, far_c, far_s = lax.optimization_barrier(
+        (near, near_gains, pick, dc, ds, far_c, far_s)
     )
     near = exchange(near)
 
@@ -562,8 +618,6 @@
     picked = pick_far(sums0, far1_sums, pick, search)
     far_picked = lax.ppermute(picked, "crate", partners)
     far0 = lax.ppermute(sums0, "crate", partners)
-    own_first, picked = lax.optimization_barrier((own_first, picked))
-    near_c, near_s = phasors(own_first, places, directions, 2)
     near_sums = form_beams(near, near_gains, (dc, ds, near_c, near_s), 0, beams, F32)
 
     spectrum = search_spectra(near_sums, far_picked, pick, search, devices, norm)

time: 170 us -> 168 us (0.988)
  Pallas kernels: 84.3 us -> 77.9 us
  waiting for transfers between devices: 48.1 us -> 52.4 us
    ppermute x1, waiting for transfers between devices: 7.3 us -> 14.9 us  [on_device(): far_picked = lax.ppermute(picked, 'crate', partners)]
    pallas_call x2 -> x1, Pallas kernels: 16.7 us -> 11.7 us  [phasors(): pl.pallas_call(phasor_kernel, out_shape=[jax.ShapeDtypeStruct((total, bea...]
    all_to_all x2, waiting for transfers between devices: 5.39 us -> 2.13 us  [exchange(): lax.all_to_all(x, 'crate', split_axis=0, concat_axis=0, axis_index_groups...]
  transfers between devices with their start and end apart: 7 -> 7, of which waited for: 5 -> 5; matrix products, arithmetic and copies ran while one was open for 4% -> 4% of each run, Pallas kernels for 42% -> 40%
where the time goes in v8:
time: 168 us; the launch traced here: 167 us
  Pallas kernels  77.9 us (46%)
  waiting for transfers between devices  52.4 us (31%)
  starting transfers between devices  24.3 us (14%)
  local copies, waits for them, and re-layouts  9.68 us (6%)
    pallas_call x3, Pallas kernels, form_beams(): pl.pallas_call(beam_kernel, out_shape=jax.ShapeDtypeStruct((chans, rows,...  37 us
    ppermute x1, waiting for transfers between devices, on_device(): far_gains = lax.ppermute(far_gains, 'crate', partners)  23 us
    ppermute x1, waiting for transfers between devices, on_device(): far_picked = lax.ppermute(picked, 'crate', partners)  14.9 us
    pallas_call x1, Pallas kernels, phasors(): pl.pallas_call(phasor_kernel, out_shape=[jax.ShapeDtypeStruct((total, bea...  11.7 us
    all_to_all x2, starting transfers between devices, exchange(): lax.all_to_all(x, 'crate', split_axis=0, concat_axis=0, axis_index_groups...  9.07 us
    pallas_call x1, Pallas kernels, fold(): pl.pallas_call(fold_kernel, out_shape=(spectra, folded), grid_spec=pltpu....  7.99 us
    ppermute x1, waiting for transfers between devices, on_device(): far1 = lax.ppermute(sums1, 'crate', partners)  7.43 us
    all_to_all x1, starting transfers between devices, on_device(): lax.all_to_all(spectrum, 'crate', split_axis=0, concat_axis=0, tiled=True)  5.86 us
  transfers between devices with their start and end apart: 7, of which 5 were waited for; matrix products, arithmetic and copies ran while one was open for 4% of the time, Pallas kernels for 40%

profile of v8, /device:TPU:0, one launch (start us, length us, event | category | flops | bytes accessed | tf_op | source)
XLA Modules:
  0.0 166.7 jit_solution(4799318560170904581)
XLA Ops:
  0.7 8.0 %fold.1 = (bf16[8,16,64,128]{3,2,1,0:T(8,128)(2,1)}, bf16[4096,512]{1,0:T(8,128)(2,1)}) custom-call(s32[1]{0:T(128)S(6)} %sub.14.block_ref, bf16[128,17920]{1,0:T(8,128)(2,1)} %refs_2_.1, bf16[128,17920]{1,0:T(8,128)(2,1)} %refs_2_.1, bf16[128,17920]{1,0:T(8,128)(2,1)} %refs_2_.1, bf16[128,17920]{1,0:T(8,128)(2,1)} %refs_2_.1, ...), custom_call_target="tpu_custom_call" | custom-call | flops 4294967296 | bytes 12582912 | tf_op jit(solution)/shard_map/fold/pallas_call | solution.py:394
  8.7 5.3 %all-to-all-start.1 = ((bf16[8,16,64,128]{3,2,1,0:T(8,128)(2,1)}), bf16[8,16,64,128]{3,2,1,0:T(8,128)(2,1)}, u32[]{:S(2)}, u32[]{:S(2)}) async-start(bf16[8,16,64,128]{3,2,1,0:T(8,128)(2,1)} %get-tuple-element.38), calls=%async_computation.1 | async-start | bytes 4194304 | tf_op jit(solution)/shard_map/all_to_all | solution.py:587
  14.0 5.8 %spectra.1 = bf16[8,16,64,128]{3,2,1,0:T(8,128)(2,1)} custom-call(s32[1]{0:T(128)} %bitcast.block_ref, bf16[4096,512]{1,0:T(8,128)(2,1)} %get-tuple-element.24.folded_ref, bf16[512,512]{1,0:T(8,128)(2,1)} %constant.68.refs_4_.table_ref), custom_call_target="tpu_custom_call" | custom-call | flops 2147483648 | bytes 6291456 | tf_op jit(solution)/shard_map/spectra/pallas_call | solution.py:424
  20.7 2.8 %gather_fusion = f32[1024,3]{1,0:T(8,128)S(1)} fusion(f32[2048,3]{1,0:T(8,128)S(1)} %bitcast.8, s32[1024]{0:T(1024)S(1)} %fusion), kind=kCustom, calls=%fused_computation | custom fusion | bytes 28672 | tf_op jit(solution)/shard_map/jit(_take)/gather | solution.py:598
  23.6 0.7 add_multiply_fusion.first_ref
  24.2 0.7 constant_dynamic-slice_fusion.1
  24.9 1.0 broadcast_select_fusion.place_ref
  25.9 11.7 %phasors.1 = (f32[1024,512]{1,0:T(8,128)}, f32[1024,512]{1,0:T(8,128)}, f32[1024,512]{1,0:T(8,128)}, f32[1024,512]{1,0:T(8,128)}, f32[1024,512]{1,0:T(8,128)}, /*index=5*/f32[1024,512]{1,0:T(8,128)}) custom-call(s32[2]{0:T(128)} %add_multiply_fusion.first_ref, f32[1024,3]{1,0:T(8,128)} %broadcast_select_fusion.place_ref, f32[3,512]{1,0:T(4,128)} %dir_ref.1), custom_call_target="tpu_custom_call" | custom-call | flops 4194304000 | bytes 12582912 | tf_op jit(solution)/shard_map/phasors/pallas_call | solution.py:449
  37.6 2.1 %all-to-all-done.1.x_ref = bf16[8,16,64,128]{3,2,1,0:T(8,128)(2,1)} async-done(((bf16[8,16,64,128]{3,2,1,0:T(8,128)(2,1)}), bf16[8,16,64,128]{3,2,1,0:T(8,128)(2,1)}, u32[]{:S(2)}, u32[]{:S(2)}) %all-to-all-start.1) | async-done | bytes 2097184 | tf_op jit(solution)/shard_map/all_to_all | solution.py:587
  39.8 3.8 %all-to-all-start = ((bf16[8,16,64,128]{3,2,1,0:T(8,128)(2,1)}), bf16[8,16,64,128]{3,2,1,0:T(8,128)(2,1)S(1)}, u32[]{:S(2)}, u32[]{:S(2)}) async-start(bf16[8,16,64,128]{3,2,1,0:T(8,128)(2,1)} %spectra.1), calls=%async_computation | async-start | bytes 4194304 | tf_op jit(solution)/shard_map/all_to_all | solution.py:587
  43.5 3.1 %collective-permute-start = (f32[16,2,1024]{2,1,0:T(2,128)S(1)}, f32[16,2,1024]{2,1,0:T(2,128)S(1)}, u32[]{:S(2)}, u32[]{:S(2)}) collective-permute-start(f32[16,2,1024]{2,1,0:T(2,128)S(1)} %get-tuple-element.46), channel_id=1, source_target_pairs={{0,8},{1,9},{2,10},{3,11},{4,12},{5,13},{6,14},{7,15},{8,0},{9,1},... | collective-permute-start | bytes 393224 | tf_op jit(solution)/shard_map/ppermute | solution.py:595
  46.6 23.0 %collective-permute-done.gain_ref = f32[16,2,1024]{2,1,0:T(2,128)S(1)} collective-permute-done((f32[16,2,1024]{2,1,0:T(2,128)S(1)}, f32[16,2,1024]{2,1,0:T(2,128)S(1)}, u32[]{:S(2)}, u32[]{:S(2)}) %collective-permute-start) | collective-permute-done | bytes 131104 | tf_op jit(solution)/shard_map/ppermute | solution.py:595
  69.7 0.7 copy-done.6
  70.3 6.5 %beams.4.sum1_ref = bf16[16,64,128]{2,1,0:T(8,128)(2,1)} custom-call(bf16[8,16,64,128]{3,2,1,0:T(8,128)(2,1)} %all-to-all-done.1.x_ref, f32[16,2,1024]{2,1,0:T(2,128)} %copy-done.6, f32[1024,512]{1,0:T(8,128)} %get-tuple-element.34.dc_ref, f32[1024,512]{1,0:T(8,128)} %get-tuple-element.35.ds_ref, f32[1024,512]{1,0:T(8,128)} %get-tuple-element.39.c_ref, ...), custom_call_target="tpu_custom_call" | custom-call | flops 2147483648 | bytes 12582912 | tf_op jit(solution)/shard_map/beams/pallas_call | solution.py:480
  76.9 14.2 %beams.5.sum0_ref = bf16[16,64,384]{2,1,0:T(8,128)(2,1)} custom-call(bf16[8,16,64,128]{3,2,1,0:T(8,128)(2,1)} %all-to-all-done.1.x_ref, f32[16,2,1024]{2,1,0:T(2,128)} %copy-done.6, f32[1024,512]{1,0:T(8,128)} %get-tuple-element.34.dc_ref, f32[1024,512]{1,0:T(8,128)} %get-tuple-element.35.ds_ref, f32[1024,512]{1,0:T(8,128)} %get-tuple-element.39.c_ref, ...), custom_call_target="tpu_custom_call" | custom-call | flops 6442450944 | bytes 12582912 | tf_op jit(solution)/shard_map/beams/pallas_call | solution.py:480
  91.0 3.4 %collective-permute-start.2 = (bf16[16,64,384]{2,1,0:T(8,128)(2,1)}, bf16[16,64,384]{2,1,0:T(8,128)(2,1)}, u32[]{:S(2)}, u32[]{:S(2)}) collective-permute-start(bf16[16,64,384]{2,1,0:T(8,128)(2,1)} %beams.5.sum0_ref), channel_id=1, source_target_pairs={{0,8},{1,9},{2,10},{3,11},{4,12},{5,13},{6,14},{7,15},{8,0},{9,1},... | collective-permute-start | bytes 2359304 | tf_op jit(solution)/shard_map/ppermute | solution.py:620
  94.4 3.3 %pick.1 = bf16[32,512]{1,0:T(8,128)(2,1)} custom-call(bf16[16,64,384]{2,1,0:T(8,128)(2,1)} %beams.5.sum0_ref, bf16[16,64,128]{2,1,0:T(8,128)(2,1)} %beams.4.sum1_ref, s32[1,128]{1,0:T(1,128)} %broadcast_in_dim_tile.3.pick_ref), custom_call_target="tpu_custom_call" | custom-call | flops 1073741824 | bytes 2097152 | tf_op jit(solution)/shard_map/pick/pallas_call | solution.py:515
  97.7 1.4 copy-done.2
  99.1 16.3 %beams.3.own_ref = f32[16,64,512]{2,1,0:T(8,128)} custom-call(bf16[8,16,64,128]{3,2,1,0:T(8,128)(2,1)} %copy-done.2, f32[16,2,1024]{2,1,0:T(2,128)} %get-tuple-element.33.gain_ref, f32[1024,512]{1,0:T(8,128)} %get-tuple-element.34.dc_ref, f32[1024,512]{1,0:T(8,128)} %get-tuple-element.35.ds_ref, f32[1024,512]{1,0:T(8,128)} %get-tuple-element.36.c_ref, ...), custom_call_target="tpu_custom_call" | custom-call | flops 8589934592 | bytes 12582912 | tf_op jit(solution)/shard_map/beams/pallas_call | solution.py:480
  115.4 14.9 %collective-permute-done.1.far_ref = bf16[32,512]{1,0:T(8,128)(2,1)S(1)} collective-permute-done((bf16[32,512]{1,0:T(8,128)(2,1)}, bf16[32,512]{1,0:T(8,128)(2,1)S(1)}, u32[]{:S(2)}, u32[]{:S(2)}) %collective-permute-start.1) | collective-permute-done | bytes 32800 | tf_op jit(solution)/shard_map/ppermute | solution.py:619
  130.3 0.6 copy-done.10
  130.9 4.5 %spectrum.1 = bf16[16,16,512]{2,1,0:T(8,128)(2,1)} custom-call(f32[16,64,512]{2,1,0:T(8,128)} %beams.3.own_ref, bf16[32,512]{1,0:T(8,128)(2,1)} %copy-done.10, s32[1,128]{1,0:T(1,128)} %broadcast_in_dim_tile.3.pick_ref, bf16[512,512]{1,0:T(8,128)(2,1)} %constant.69.high_ref, bf16[512,512]{1,0:T(8,128)(2,1)} %constant.72.low_ref), custom_call_target="tpu_custom_call" | custom-call | flops 2147483648 | bytes 4194304 | tf_op jit(solution)/shard_map/spectrum/pallas_call | solution.py:538
  135.4 5.9 %all-to-all-start.2 = ((bf16[16,16,512]{2,1,0:T(8,128)(2,1)}), bf16[16,16,512]{2,1,0:T(8,128)(2,1)S(1)}, u32[]{:S(2)}, u32[]{:S(2)}) async-start(bf16[16,16,512]{2,1,0:T(8,128)(2,1)} %spectrum.1), calls=%async_computation.2 | async-start | bytes 524288 | tf_op jit(solution)/shard_map/all_to_all | solution.py:625
  141.3 2.9 %collective-permute-start.3 = (bf16[16,64,128]{2,1,0:T(8,128)(2,1)S(1)}, bf16[16,64,128]{2,1,0:T(8,128)(2,1)S(1)}, u32[]{:S(2)}, u32[]{:S(2)}) collective-permute-start(bf16[16,64,128]{2,1,0:T(8,128)(2,1)S(1)} %copy-done.3), channel_id=1, source_target_pairs={{0,8},{1,9},{2,10},{3,11},{4,12},{5,13},{6,14},{7,15},{8,0},{9,1},... | collective-permute-start | bytes 786440 | tf_op jit(solution)/shard_map/ppermute | solution.py:615
  144.2 0.6 constant_dynamic-slice_fusion.delay_ref
  144.8 2.2 %turns.1.turn_ref = bf16[1024,512]{1,0:T(8,128)(2,1)} custom-call(s32[64,256]{1,0:T(8,128)} %constant_dynamic-slice_fusion.delay_ref), custom_call_target="tpu_custom_call" | custom-call | tf_op jit(solution)/shard_map/turns/pallas_call | solution.py:630
  147.0 4.9 %all-to-all-done.2 = bf16[16,16,512]{2,1,0:T(8,128)(2,1)S(1)} async-done(((bf16[16,16,512]{2,1,0:T(8,128)(2,1)}), bf16[16,16,512]{2,1,0:T(8,128)(2,1)S(1)}, u32[]{:S(2)}, u32[]{:S(2)}) %all-to-all-start.2) | async-done | bytes 262176 | tf_op jit(solution)/shard_map/all_to_all | solution.py:625
  151.9 1.2 copy-done.1
  153.1 1.6 plane.1
  154.7 7.4 %collective-permute-done.3.far1_ref = bf16[16,64,128]{2,1,0:T(8,128)(2,1)S(1)} collective-permute-done((bf16[16,64,128]{2,1,0:T(8,128)(2,1)S(1)}, bf16[16,64,128]{2,1,0:T(8,128)(2,1)S(1)}, u32[]{:S(2)}, u32[]{:S(2)}) %collective-permute-start.3) | collective-permute-done | bytes 262176 | tf_op jit(solution)/shard_map/ppermute | solution.py:615
  162.1 0.7 copy-done.4
  162.8 3.9 %power.1 = f32[16,32,512]{2,1,0:T(8,128)} custom-call(f32[16,64,512]{2,1,0:T(8,128)} %beams.3.own_ref, bf16[16,64,384]{2,1,0:T(8,128)(2,1)} %collective-permute-done.2.far0_ref, bf16[16,64,128]{2,1,0:T(8,128)(2,1)} %copy-done.4), custom_call_target="tpu_custom_call" | custom-call | flops 268435456 | bytes 5242880 | tf_op jit(solution)/shard_map/power/pallas_call | solution.py:557
  (25 shorter events, 1.0 us)
Async XLA Ops:
  0.6 143.5 %copy-start = (s32[1024,256]{1,0:T(8,128)S(1)}, s32[1024,256]{1,0:T(8,128)}, u32[]{:S(2)}) copy-start(s32[1024,256]{1,0:T(8,128)} %param.15) | copy-start | bytes 3145732
  8.7 31.1 %all-to-all-start.1 = ((bf16[8,16,64,128]{3,2,1,0:T(8,128)(2,1)}), bf16[8,16,64,128]{3,2,1,0:T(8,128)(2,1)}, u32[]{:S(2)}, u32[]{:S(2)}) async-start(bf16[8,16,64,128]{3,2,1,0:T(8,128)(2,1)} %get-tuple-element.38), calls=%async_computation.1 | async-start | bytes 4194304 | tf_op jit(solution)/shard_map/all_to_all | solution.py:587
  13.9 5.8 %copy-start.7 = (f32[3,2048]{1,0:T(4,128)S(1)}, f32[3,2048]{1,0:T(4,128)}, u32[]{:S(2)}) copy-start(f32[3,2048]{1,0:T(4,128)} %param.12) | copy-start | bytes 73732
  13.9 6.2 %copy-start.9 = (s32[16]{0:T(128)S(1)}, s32[16]{0:T(128)}, u32[]{:S(2)}) copy-start(s32[16]{0:T(128)} %param.16) | copy-start | bytes 196
  14.0 6.8 %copy-start.8 = (s32[2048]{0:T(1024)S(1)}, s32[2048]{0:T(1024)}, u32[]{:S(2)}) copy-start(s32[2048]{0:T(1024)} %param.14) | copy-start | bytes 24580
  20.7 3.5 %copy-start.5 = (f32[16,2,2048]{2,1,0:T(2,128)S(1)}, f32[16,2,2048]{2,1,0:T(2,128)}, u32[]{:S(2)}) copy-start(f32[16,2,2048]{2,1,0:T(2,128)} %param.11) | copy-start | bytes 786436
  39.8 57.9 %all-to-all-start = ((bf16[8,16,64,128]{3,2,1,0:T(8,128)(2,1)}), bf16[8,16,64,128]{3,2,1,0:T(8,128)(2,1)S(1)}, u32[]{:S(2)}, u32[]{:S(2)}) async-start(bf16[8,16,64,128]{3,2,1,0:T(8,128)(2,1)} %spectra.1), calls=%async_computation | async-start | bytes 4194304 | tf_op jit(solution)/shard_map/all_to_all | solution.py:587
  43.5 26.2 %collective-permute-start = (f32[16,2,1024]{2,1,0:T(2,128)S(1)}, f32[16,2,1024]{2,1,0:T(2,128)S(1)}, u32[]{:S(2)}, u32[]{:S(2)}) collective-permute-start(f32[16,2,1024]{2,1,0:T(2,128)S(1)} %get-tuple-element.46), channel_id=1, source_target_pairs={{0,8},{1,9},{2,10},{3,11},{4,12},{5,13},{6,14},{7,15},{8,0},{9,1},... | collective-permute-start | bytes 393224 | tf_op jit(solution)/shard_map/ppermute | solution.py:595
  69.7 0.7 copy-start.6
  91.0 71.1 %collective-permute-start.2 = (bf16[16,64,384]{2,1,0:T(8,128)(2,1)}, bf16[16,64,384]{2,1,0:T(8,128)(2,1)}, u32[]{:S(2)}, u32[]{:S(2)}) collective-permute-start(bf16[16,64,384]{2,1,0:T(8,128)(2,1)} %beams.5.sum0_ref), channel_id=1, source_target_pairs={{0,8},{1,9},{2,10},{3,11},{4,12},{5,13},{6,14},{7,15},{8,0},{9,1},... | collective-permute-start | bytes 2359304 | tf_op jit(solution)/shard_map/ppermute | solution.py:620
  97.7 32.6 %collective-permute-start.1 = (bf16[32,512]{1,0:T(8,128)(2,1)}, bf16[32,512]{1,0:T(8,128)(2,1)S(1)}, u32[]{:S(2)}, u32[]{:S(2)}) collective-permute-start(bf16[32,512]{1,0:T(8,128)(2,1)} %pick.1), channel_id=1, source_target_pairs={{0,8},{1,9},{2,10},{3,11},{4,12},{5,13},{6,14},{7,15},{8,0},{9,1},... | collective-permute-start | bytes 98312 | tf_op jit(solution)/shard_map/ppermute | solution.py:619
  97.7 1.4 copy-start.2
  115.4 25.9 %copy-start.3 = (bf16[16,64,128]{2,1,0:T(8,128)(2,1)S(1)}, bf16[16,64,128]{2,1,0:T(8,128)(2,1)}, u32[]{:S(2)}) copy-start(bf16[16,64,128]{2,1,0:T(8,128)(2,1)} %beams.4.sum1_ref) | copy-start | bytes 786436
  130.3 0.6 copy-start.10
  135.4 16.4 %all-to-all-start.2 = ((bf16[16,16,512]{2,1,0:T(8,128)(2,1)}), bf16[16,16,512]{2,1,0:T(8,128)(2,1)S(1)}, u32[]{:S(2)}, u32[]{:S(2)}) async-start(bf16[16,16,512]{2,1,0:T(8,128)(2,1)} %spectrum.1), calls=%async_computation.2 | async-start | bytes 524288 | tf_op jit(solution)/shard_map/all_to_all | solution.py:625
  141.3 20.8 %collective-permute-start.3 = (bf16[16,64,128]{2,1,0:T(8,128)(2,1)S(1)}, bf16[16,64,128]{2,1,0:T(8,128)(2,1)S(1)}, u32[]{:S(2)}, u32[]{:S(2)}) collective-permute-start(bf16[16,64,128]{2,1,0:T(8,128)(2,1)S(1)} %copy-done.3), channel_id=1, source_target_pairs={{0,8},{1,9},{2,10},{3,11},{4,12},{5,13},{6,14},{7,15},{8,0},{9,1},... | collective-permute-start | bytes 786440 | tf_op jit(solution)/shard_map/ppermute | solution.py:615
  151.9 1.2 copy-start.1
  162.1 0.7 copy-start.4

commit v9 on v8

--- a/solution.py
+++ b/solution.py
@@ -13,7 +13,7 @@
 TAPS = 4
 TIME = 32
 PITCH = 40
-FRAMES = 8
+FRAMES = 4
 FFTLEN = 512
 HALF_BINS = TIME // 2
 TWO_PI = 2.0 * math.pi
@@ -610,8 +610,8 @@
     beams = directions.shape[1]
     norm = 1.0 / gains.shape[2]
     far_state = (dc, ds, far_c, far_s)
-    few = beams // 4
-    sums1 = form_beams(far, far_gains, far_state, 3, few, BF16)
+    few = beams // 2
+    sums1 = form_beams(far, far_gains, far_state, 1, few, BF16)
     far1 = lax.ppermute(sums1, "crate", partners)
     far, far1_sums = lax.optimization_barrier((far, sums1))
     sums0 = form_beams(far, far_gains, far_state, 0, beams - few, BF16)

time: 168 us -> 156 us (0.929)
  waiting for transfers between devices: 52.4 us -> 42.3 us
  local copies, waits for them, and re-layouts: 9.68 us -> 7.72 us
    ppermute x1, waiting for transfers between devices: 7.43 us -> 0.01 us  [on_device(): far1 = lax.ppermute(sums1, 'crate', partners)]
    ppermute x1, starting transfers between devices: 3.38 us -> 0.02 us  [on_device(): far0 = lax.ppermute(sums0, 'crate', partners)]
    ppermute x1, starting transfers between devices: 0.02 us -> 2.91 us  [on_device(): far_picked = lax.ppermute(picked, 'crate', partners)]
    unnamed x22 -> x18, local copies, waits for them, and re-layouts: 4.6 us -> 2.61 us
    pallas_call x3, Pallas kernels: 37 us -> 35 us  [form_beams(): pl.pallas_call(beam_kernel, out_shape=jax.ShapeDtypeStruct((chans, rows,...]
    pallas_call x1, Pallas kernels: 7.99 us -> 9.93 us  [fold(): pl.pallas_call(fold_kernel, out_shape=(spectra, folded), grid_spec=pltpu....]
  transfers between devices with their start and end apart: 7 -> 7, of which waited for: 5 -> 4; matrix products, arithmetic and copies ran while one was open for 4% -> 4% of each run, Pallas kernels for 40% -> 43%
where the time goes in v9:
time: 156 us; the launch traced here: 155 us
  Pallas kernels  77.9 us (50%)
  waiting for transfers between devices  42.3 us (27%)
  starting transfers between devices  24.3 us (16%)
  local copies, waits for them, and re-layouts  7.72 us (5%)
  other arithmetic  1.67 us (1%)
    pallas_call x3, Pallas kernels, form_beams(): pl.pallas_call(beam_kernel, out_shape=jax.ShapeDtypeStruct((chans, rows,...  35 us
    ppermute x1, waiting for transfers between devices, on_device(): far_gains = lax.ppermute(far_gains, 'crate', partners)  23.1 us
    ppermute x1, waiting for transfers between devices, on_device(): far_picked = lax.ppermute(picked, 'crate', partners)  13.9 us
    pallas_call x1, Pallas kernels, phasors(): pl.pallas_call(phasor_kernel, out_shape=[jax.ShapeDtypeStruct((total, bea...  11.7 us
    pallas_call x1, Pallas kernels, fold(): pl.pallas_call(fold_kernel, out_shape=(spectra, folded), grid_spec=pltpu....  9.93 us
    all_to_all x2, starting transfers between devices, exchange(): lax.all_to_all(x, 'crate', split_axis=0, concat_axis=0, axis_index_groups...  9.07 us
    all_to_all x1, starting transfers between devices, on_device(): lax.all_to_all(spectrum, 'crate', split_axis=0, concat_axis=0, tiled=True)  5.86 us
    pallas_call x1, Pallas kernels, more_spectra(): pl.pallas_call(spectra_kernel, out_shape=out, grid_spec=pltpu.PrefetchSca...  5.77 us
  transfers between devices with their start and end apart: 7, of which 4 were waited for; matrix products, arithmetic and copies ran while one was open for 4% of the time, Pallas kernels for 43%

profile of v9, /device:TPU:0, one launch (start us, length us, event | category | flops | bytes accessed | tf_op | source)
XLA Modules:
  0.0 154.7 jit_solution(6568572568193762627)
XLA Ops:
  0.7 9.9 %fold.1 = (bf16[8,16,64,128]{3,2,1,0:T(8,128)(2,1)}, bf16[4096,512]{1,0:T(8,128)(2,1)}) custom-call(s32[1]{0:T(128)S(6)} %sub.14.block_ref, bf16[128,17920]{1,0:T(8,128)(2,1)} %refs_2_.1, bf16[128,17920]{1,0:T(8,128)(2,1)} %refs_2_.1, bf16[128,17920]{1,0:T(8,128)(2,1)} %refs_2_.1, bf16[128,17920]{1,0:T(8,128)(2,1)} %refs_2_.1, ...), custom_call_target="tpu_custom_call" | custom-call | flops 4294967296 | bytes 12582912 | tf_op jit(solution)/shard_map/fold/pallas_call | solution.py:394
  10.6 5.3 %all-to-all-start.1 = ((bf16[8,16,64,128]{3,2,1,0:T(8,128)(2,1)}), bf16[8,16,64,128]{3,2,1,0:T(8,128)(2,1)}, u32[]{:S(2)}, u32[]{:S(2)}) async-start(bf16[8,16,64,128]{3,2,1,0:T(8,128)(2,1)} %get-tuple-element.38), calls=%async_computation.1 | async-start | bytes 4194304 | tf_op jit(solution)/shard_map/all_to_all | solution.py:587
  15.9 5.8 %spectra.1 = bf16[8,16,64,128]{3,2,1,0:T(8,128)(2,1)} custom-call(s32[1]{0:T(128)} %bitcast.block_ref, bf16[4096,512]{1,0:T(8,128)(2,1)} %get-tuple-element.24.folded_ref, bf16[512,512]{1,0:T(8,128)(2,1)} %constant.68.refs_4_.table_ref), custom_call_target="tpu_custom_call" | custom-call | flops 2147483648 | bytes 6291456 | tf_op jit(solution)/shard_map/spectra/pallas_call | solution.py:424
  21.7 0.4 copy.12
  22.1 0.6 broadcast_in_dim_tile.3.pick_ref
  22.7 2.8 %gather_fusion = f32[1024,3]{1,0:T(8,128)S(1)} fusion(f32[2048,3]{1,0:T(8,128)S(1)} %bitcast.8, s32[1024]{0:T(1024)S(1)} %fusion), kind=kCustom, calls=%fused_computation | custom fusion | bytes 28672 | tf_op jit(solution)/shard_map/jit(_take)/gather | solution.py:598
  25.5 0.7 add_multiply_fusion.first_ref
  26.2 0.7 constant_dynamic-slice_fusion.1
  26.9 1.0 broadcast_select_fusion.place_ref
  27.9 11.7 %phasors.1 = (f32[1024,512]{1,0:T(8,128)}, f32[1024,512]{1,0:T(8,128)}, f32[1024,512]{1,0:T(8,128)}, f32[1024,512]{1,0:T(8,128)}, f32[1024,512]{1,0:T(8,128)}, /*index=5*/f32[1024,512]{1,0:T(8,128)}) custom-call(s32[2]{0:T(128)} %add_multiply_fusion.first_ref, f32[1024,3]{1,0:T(8,128)} %broadcast_select_fusion.place_ref, f32[3,512]{1,0:T(4,128)} %dir_ref.1), custom_call_target="tpu_custom_call" | custom-call | flops 4194304000 | bytes 12582912 | tf_op jit(solution)/shard_map/phasors/pallas_call | solution.py:449
  39.6 2.1 %all-to-all-done.1.x_ref = bf16[8,16,64,128]{3,2,1,0:T(8,128)(2,1)} async-done(((bf16[8,16,64,128]{3,2,1,0:T(8,128)(2,1)}), bf16[8,16,64,128]{3,2,1,0:T(8,128)(2,1)}, u32[]{:S(2)}, u32[]{:S(2)}) %all-to-all-start.1) | async-done | bytes 2097184 | tf_op jit(solution)/shard_map/all_to_all | solution.py:587
  41.7 3.8 %all-to-all-start = ((bf16[8,16,64,128]{3,2,1,0:T(8,128)(2,1)}), bf16[8,16,64,128]{3,2,1,0:T(8,128)(2,1)S(1)}, u32[]{:S(2)}, u32[]{:S(2)}) async-start(bf16[8,16,64,128]{3,2,1,0:T(8,128)(2,1)} %spectra.1), calls=%async_computation | async-start | bytes 4194304 | tf_op jit(solution)/shard_map/all_to_all | solution.py:587
  45.5 3.1 %collective-permute-start = (f32[16,2,1024]{2,1,0:T(2,128)S(1)}, f32[16,2,1024]{2,1,0:T(2,128)S(1)}, u32[]{:S(2)}, u32[]{:S(2)}) collective-permute-start(f32[16,2,1024]{2,1,0:T(2,128)S(1)} %get-tuple-element.46), channel_id=1, source_target_pairs={{0,8},{1,9},{2,10},{3,11},{4,12},{5,13},{6,14},{7,15},{8,0},{9,1},... | collective-permute-start | bytes 393224 | tf_op jit(solution)/shard_map/ppermute | solution.py:595
  48.6 23.1 %collective-permute-done.gain_ref = f32[16,2,1024]{2,1,0:T(2,128)S(1)} collective-permute-done((f32[16,2,1024]{2,1,0:T(2,128)S(1)}, f32[16,2,1024]{2,1,0:T(2,128)S(1)}, u32[]{:S(2)}, u32[]{:S(2)}) %collective-permute-start) | collective-permute-done | bytes 131104 | tf_op jit(solution)/shard_map/ppermute | solution.py:595
  71.6 0.6 copy-done.7
  72.3 9.4 %beams.4.sum1_ref = bf16[16,64,256]{2,1,0:T(8,128)(2,1)} custom-call(bf16[8,16,64,128]{3,2,1,0:T(8,128)(2,1)} %all-to-all-done.1.x_ref, f32[16,2,1024]{2,1,0:T(2,128)} %copy-done.7, f32[1024,512]{1,0:T(8,128)} %get-tuple-element.34.dc_ref, f32[1024,512]{1,0:T(8,128)} %get-tuple-element.35.ds_ref, f32[1024,512]{1,0:T(8,128)} %get-tuple-element.39.c_ref, ...), custom_call_target="tpu_custom_call" | custom-call | flops 4294967296 | bytes 12582912 | tf_op jit(solution)/shard_map/beams/pallas_call | solution.py:480
  81.7 3.4 %collective-permute-start.3 = (bf16[16,64,256]{2,1,0:T(8,128)(2,1)}, bf16[16,64,256]{2,1,0:T(8,128)(2,1)}, u32[]{:S(2)}, u32[]{:S(2)}) collective-permute-start(bf16[16,64,256]{2,1,0:T(8,128)(2,1)} %beams.4.sum1_ref), channel_id=1, source_target_pairs={{0,8},{1,9},{2,10},{3,11},{4,12},{5,13},{6,14},{7,15},{8,0},{9,1},... | collective-permute-start | bytes 1572872 | tf_op jit(solution)/shard_map/ppermute | solution.py:615
  85.0 9.3 %beams.5.sum0_ref = bf16[16,64,256]{2,1,0:T(8,128)(2,1)} custom-call(bf16[8,16,64,128]{3,2,1,0:T(8,128)(2,1)} %all-to-all-done.1.x_ref, f32[16,2,1024]{2,1,0:T(2,128)} %copy-done.7, f32[1024,512]{1,0:T(8,128)} %get-tuple-element.34.dc_ref, f32[1024,512]{1,0:T(8,128)} %get-tuple-element.35.ds_ref, f32[1024,512]{1,0:T(8,128)} %get-tuple-element.39.c_ref, ...), custom_call_target="tpu_custom_call" | custom-call | flops 4294967296 | bytes 12582912 | tf_op jit(solution)/shard_map/beams/pallas_call | solution.py:480
  94.4 0.0 collective-permute-start.2
  94.4 3.3 %pick.1 = bf16[32,512]{1,0:T(8,128)(2,1)} custom-call(bf16[16,64,256]{2,1,0:T(8,128)(2,1)} %beams.5.sum0_ref, bf16[16,64,256]{2,1,0:T(8,128)(2,1)} %beams.4.sum1_ref, s32[1,128]{1,0:T(1,128)} %broadcast_in_dim_tile.3.pick_ref), custom_call_target="tpu_custom_call" | custom-call | flops 1073741824 | bytes 2097152 | tf_op jit(solution)/shard_map/pick/pallas_call | solution.py:515
  97.7 2.9 %collective-permute-start.1 = (bf16[32,512]{1,0:T(8,128)(2,1)}, bf16[32,512]{1,0:T(8,128)(2,1)S(1)}, u32[]{:S(2)}, u32[]{:S(2)}) collective-permute-start(bf16[32,512]{1,0:T(8,128)(2,1)} %pick.1), channel_id=1, source_target_pairs={{0,8},{1,9},{2,10},{3,11},{4,12},{5,13},{6,14},{7,15},{8,0},{9,1},... | collective-permute-start | bytes 98312 | tf_op jit(solution)/shard_map/ppermute | solution.py:619
  100.6 1.3 copy-done.2
  101.9 16.3 %beams.3.own_ref = f32[16,64,512]{2,1,0:T(8,128)} custom-call(bf16[8,16,64,128]{3,2,1,0:T(8,128)(2,1)} %copy-done.2, f32[16,2,1024]{2,1,0:T(2,128)} %get-tuple-element.33.gain_ref, f32[1024,512]{1,0:T(8,128)} %get-tuple-element.34.dc_ref, f32[1024,512]{1,0:T(8,128)} %get-tuple-element.35.ds_ref, f32[1024,512]{1,0:T(8,128)} %get-tuple-element.36.c_ref, ...), custom_call_target="tpu_custom_call" | custom-call | flops 8589934592 | bytes 12582912 | tf_op jit(solution)/shard_map/beams/pallas_call | solution.py:480
  118.3 13.9 %collective-permute-done.1.far_ref = bf16[32,512]{1,0:T(8,128)(2,1)S(1)} collective-permute-done((bf16[32,512]{1,0:T(8,128)(2,1)}, bf16[32,512]{1,0:T(8,128)(2,1)S(1)}, u32[]{:S(2)}, u32[]{:S(2)}) %collective-permute-start.1) | collective-permute-done | bytes 32800 | tf_op jit(solution)/shard_map/ppermute | solution.py:619
  132.1 0.6 copy-done.8
  132.7 4.5 %spectrum.1 = bf16[16,16,512]{2,1,0:T(8,128)(2,1)} custom-call(f32[16,64,512]{2,1,0:T(8,128)} %beams.3.own_ref, bf16[32,512]{1,0:T(8,128)(2,1)} %copy-done.8, s32[1,128]{1,0:T(1,128)} %broadcast_in_dim_tile.3.pick_ref, bf16[512,512]{1,0:T(8,128)(2,1)} %constant.69.high_ref, bf16[512,512]{1,0:T(8,128)(2,1)} %constant.72.low_ref), custom_call_target="tpu_custom_call" | custom-call | flops 2147483648 | bytes 4194304 | tf_op jit(solution)/shard_map/spectrum/pallas_call | solution.py:538
  137.2 5.9 %all-to-all-start.2 = ((bf16[16,16,512]{2,1,0:T(8,128)(2,1)}), bf16[16,16,512]{2,1,0:T(8,128)(2,1)S(1)}, u32[]{:S(2)}, u32[]{:S(2)}) async-start(bf16[16,16,512]{2,1,0:T(8,128)(2,1)} %spectrum.1), calls=%async_computation.2 | async-start | bytes 524288 | tf_op jit(solution)/shard_map/all_to_all | solution.py:625
  143.1 0.6 constant_dynamic-slice_fusion.delay_ref
  143.8 2.2 %turns.1.turn_ref = bf16[1024,512]{1,0:T(8,128)(2,1)} custom-call(s32[64,256]{1,0:T(8,128)} %constant_dynamic-slice_fusion.delay_ref), custom_call_target="tpu_custom_call" | custom-call | tf_op jit(solution)/shard_map/turns/pallas_call | solution.py:630
  146.0 3.9 %power.1 = f32[16,32,512]{2,1,0:T(8,128)} custom-call(f32[16,64,512]{2,1,0:T(8,128)} %beams.3.own_ref, bf16[16,64,256]{2,1,0:T(8,128)(2,1)} %collective-permute-done.2.far0_ref, bf16[16,64,256]{2,1,0:T(8,128)(2,1)} %collective-permute-done.3.far1_ref), custom_call_target="tpu_custom_call" | custom-call | flops 268435456 | bytes 5242880 | tf_op jit(solution)/shard_map/power/pallas_call | solution.py:557
  149.9 3.2 %all-to-all-done.2 = bf16[16,16,512]{2,1,0:T(8,128)(2,1)S(1)} async-done(((bf16[16,16,512]{2,1,0:T(8,128)(2,1)}), bf16[16,16,512]{2,1,0:T(8,128)(2,1)S(1)}, u32[]{:S(2)}, u32[]{:S(2)}) %all-to-all-start.2) | async-done | bytes 262176 | tf_op jit(solution)/shard_map/all_to_all | solution.py:625
  153.1 1.6 %plane.1 = f32[16,32,64]{2,1,0:T(8,128)} custom-call(bf16[256,512]{1,0:T(8,128)(2,1)S(1)} %bitcast.7, bf16[1024,512]{1,0:T(8,128)(2,1)S(1)} %copy-done.1), custom_call_target="tpu_custom_call" | custom-call | tf_op jit(solution)/shard_map/plane/pallas_call | solution.py:636
  (21 shorter events, 0.1 us)
Async XLA Ops:
  0.6 142.5 %copy-start = (s32[1024,256]{1,0:T(8,128)S(1)}, s32[1024,256]{1,0:T(8,128)}, u32[]{:S(2)}) copy-start(s32[1024,256]{1,0:T(8,128)} %param.15) | copy-start | bytes 3145732
  10.6 31.1 %all-to-all-start.1 = ((bf16[8,16,64,128]{3,2,1,0:T(8,128)(2,1)}), bf16[8,16,64,128]{3,2,1,0:T(8,128)(2,1)}, u32[]{:S(2)}, u32[]{:S(2)}) async-start(bf16[8,16,64,128]{3,2,1,0:T(8,128)(2,1)} %get-tuple-element.38), calls=%async_computation.1 | async-start | bytes 4194304 | tf_op jit(solution)/shard_map/all_to_all | solution.py:587
  15.9 5.8 %copy-start.4 = (f32[3,2048]{1,0:T(4,128)S(1)}, f32[3,2048]{1,0:T(4,128)}, u32[]{:S(2)}) copy-start(f32[3,2048]{1,0:T(4,128)} %param.12) | copy-start | bytes 73732
  15.9 6.2 %copy-start.6 = (s32[16]{0:T(128)S(1)}, s32[16]{0:T(128)}, u32[]{:S(2)}) copy-start(s32[16]{0:T(128)} %param.16) | copy-start | bytes 196
  15.9 6.8 %copy-start.5 = (s32[2048]{0:T(1024)S(1)}, s32[2048]{0:T(1024)}, u32[]{:S(2)}) copy-start(s32[2048]{0:T(1024)} %param.14) | copy-start | bytes 24580
  22.7 3.5 %copy-start.3 = (f32[16,2,2048]{2,1,0:T(2,128)S(1)}, f32[16,2,2048]{2,1,0:T(2,128)}, u32[]{:S(2)}) copy-start(f32[16,2,2048]{2,1,0:T(2,128)} %param.11) | copy-start | bytes 786436
  41.7 58.9 %all-to-all-start = ((bf16[8,16,64,128]{3,2,1,0:T(8,128)(2,1)}), bf16[8,16,64,128]{3,2,1,0:T(8,128)(2,1)S(1)}, u32[]{:S(2)}, u32[]{:S(2)}) async-start(bf16[8,16,64,128]{3,2,1,0:T(8,128)(2,1)} %spectra.1), calls=%async_computation | async-start | bytes 4194304 | tf_op jit(solution)/shard_map/all_to_all | solution.py:587
  45.5 26.2 %collective-permute-start = (f32[16,2,1024]{2,1,0:T(2,128)S(1)}, f32[16,2,1024]{2,1,0:T(2,128)S(1)}, u32[]{:S(2)}, u32[]{:S(2)}) collective-permute-start(f32[16,2,1024]{2,1,0:T(2,128)S(1)} %get-tuple-element.46), channel_id=1, source_target_pairs={{0,8},{1,9},{2,10},{3,11},{4,12},{5,13},{6,14},{7,15},{8,0},{9,1},... | collective-permute-start | bytes 393224 | tf_op jit(solution)/shard_map/ppermute | solution.py:595
  71.6 0.6 copy-start.7
  81.7 64.3 %collective-permute-start.3 = (bf16[16,64,256]{2,1,0:T(8,128)(2,1)}, bf16[16,64,256]{2,1,0:T(8,128)(2,1)}, u32[]{:S(2)}, u32[]{:S(2)}) collective-permute-start(bf16[16,64,256]{2,1,0:T(8,128)(2,1)} %beams.4.sum1_ref), channel_id=1, source_target_pairs={{0,8},{1,9},{2,10},{3,11},{4,12},{5,13},{6,14},{7,15},{8,0},{9,1},... | collective-permute-start | bytes 1572872 | tf_op jit(solution)/shard_map/ppermute | solution.py:615
  94.4 51.6 %collective-permute-start.2 = (bf16[16,64,256]{2,1,0:T(8,128)(2,1)}, bf16[16,64,256]{2,1,0:T(8,128)(2,1)}, u32[]{:S(2)}, u32[]{:S(2)}) collective-permute-start(bf16[16,64,256]{2,1,0:T(8,128)(2,1)} %beams.5.sum0_ref), channel_id=1, source_target_pairs={{0,8},{1,9},{2,10},{3,11},{4,12},{5,13},{6,14},{7,15},{8,0},{9,1},... | collective-permute-start | bytes 1572872 | tf_op jit(solution)/shard_map/ppermute | solution.py:620
  97.7 34.5 %collective-permute-start.1 = (bf16[32,512]{1,0:T(8,128)(2,1)}, bf16[32,512]{1,0:T(8,128)(2,1)S(1)}, u32[]{:S(2)}, u32[]{:S(2)}) collective-permute-start(bf16[32,512]{1,0:T(8,128)(2,1)} %pick.1), channel_id=1, source_target_pairs={{0,8},{1,9},{2,10},{3,11},{4,12},{5,13},{6,14},{7,15},{8,0},{9,1},... | collective-permute-start | bytes 98312 | tf_op jit(solution)/shard_map/ppermute | solution.py:619
  100.6 1.3 copy-start.2
  132.1 0.6 copy-start.8
  137.2 15.9 %all-to-all-start.2 = ((bf16[16,16,512]{2,1,0:T(8,128)(2,1)}), bf16[16,16,512]{2,1,0:T(8,128)(2,1)S(1)}, u32[]{:S(2)}, u32[]{:S(2)}) async-start(bf16[16,16,512]{2,1,0:T(8,128)(2,1)} %spectrum.1), calls=%async_computation.2 | async-start | bytes 524288 | tf_op jit(solution)/shard_map/all_to_all | solution.py:625
  145.9 7.2 %copy-start.1 = (bf16[1024,512]{1,0:T(8,128)(2,1)S(1)}, bf16[1024,512]{1,0:T(8,128)(2,1)}, u32[]{:S(2)}) copy-start(bf16[1024,512]{1,0:T(8,128)(2,1)} %turns.1.turn_ref) | copy-start | bytes 3145732
